TPU v7x, 32 devices: a whole 2x2x4 slice. The times are simulated.
32 devices in a mesh: exp: 4 (over y, core), fsdp: 8 (over z, x).
Axes of the slice: x: 2, y: 2, z: 4, core: 2. Of those that a mesh axis runs over, the one named last changes fastest.
Arguments:
- tokens: bfloat16 [8, 2048, 768], P('fsdp', 'exp'), may hold values from -6 to 6
- gate_res: float32 [8, 2048, 8], P('fsdp', 'exp'), may hold values from -3 to 3
- routes: int32 [8, 2048, 2], P('fsdp', 'exp'), may hold values from 0 to 7, all different within a row; in each aligned block of 512 rows (0 to 511, 512 to 1023, ..., all dimensions but the last counted through in order) at most 160 rows name the same one
- piece_starts: int32 [8, 4], P('fsdp'), may hold values from 0 to 1792, as said below
- norm_attn: float32 [768], replicated, may hold values from 0.5 to 1.5
- norm_ffn: float32 [768], replicated, may hold values from 0.5 to 1.5
- w_query: bfloat16 [768, 768], P('fsdp'), may hold values from -0.21875 to 0.21875
- w_key: bfloat16 [768, 768], P('fsdp'), may hold values from -0.21875 to 0.21875
- w_value: bfloat16 [768, 768], P('fsdp'), may hold values from -0.21875 to 0.21875
- w_out: bfloat16 [768, 768], P('fsdp'), may hold values from -1.25 to 1.25
- router: float32 [768, 8], replicated, may hold values from -0.15625 to 0.15625
- mixing: float32 [8, 8], replicated, may hold values from -2 to 2
- const_proj: float32 [768, 4], replicated, may hold values from -0.21875 to 0.21875
- const_vec: float32 [2, 768], replicated, may hold values from -6 to 6
- w_gate: bfloat16 [4, 768, 2048], P('exp', 'fsdp'), may hold values from -0.21875 to 0.21875
- w_up: bfloat16 [4, 768, 2048], P('exp', 'fsdp'), may hold values from -0.21875 to 0.21875
- w_down: bfloat16 [4, 2048, 768], P('exp', 'fsdp'), may hold values from -0.1875 to 0.1875
- cotangent: bfloat16 [8, 2048, 768], P('fsdp', 'exp'), may hold values from -6 to 6
Outputs:
- layer_out: bfloat16 [8, 2048, 768], P('fsdp', 'exp')
- grad_tokens: bfloat16 [8, 2048, 768], P('fsdp', 'exp')
- grad_gate_res: float32 [8, 2048, 8], P('fsdp', 'exp')
- grad_norm_attn: float32 [768], replicated
- grad_norm_ffn: float32 [768], replicated
- grad_query: float32 [768, 768], P('fsdp')
- grad_key: float32 [768, 768], P('fsdp')
- grad_value: float32 [768, 768], P('fsdp')
- grad_out: float32 [768, 768], P('fsdp')
- grad_router: float32 [768, 8], replicated
- grad_mixing: float32 [8, 8], replicated
- grad_const_proj: float32 [768, 4], replicated
- grad_const_vec: float32 [2, 768], replicated
- grad_gate: float32 [4, 768, 2048], P('exp', 'fsdp')
- grad_up: float32 [4, 768, 2048], P('exp', 'fsdp')
- grad_down: float32 [4, 2048, 768], P('exp', 'fsdp')
Inputs may be any that keep to these rules, and one draw needn't show every extreme that they name: `routes`: each row names two different experts. Numbers below 4 are the feed-forward experts (expert e is owned by index e of exp), 4 is the zero expert, 5 the copy expert, 6 and 7 the constant experts. Within the 512 positions of one device no number is named by more than 160 rows, a bound that some block reaches. `piece_starts`: each sequence has 4 image pieces of 256 positions; piece j starts between j * 512 and (j + 1) * 512 - 256, so pieces never intersect.
All inputs are finite; a program needn't handle non-finite values.
Results may differ from a plain program's by a relative error of at most 0.02.
Values may be sent and summed in bfloat16 or wider, within the bound.
A program may use at most 192 MiB of HBM per device.

v0:
```python
import math

import jax
import jax.numpy as jnp
from jax import lax
from jax.sharding import PartitionSpec as P

H = 12
HD = 64
PIECE = 256
KBLK = 512
CAP = 160


EPS = 1e-05
HIGH = lax.Precision.HIGHEST
NEG = -1e30


def rms_scale(values, gain_vec):
    inverse = lax.rsqrt(jnp.mean(values * values, axis=-1, keepdims=True) + EPS)
    return values * inverse * gain_vec


def piece_ids(positions, starts, extent):
    inside = (positions[:, None] >= starts[None, :]) & (
        positions[:, None] < starts[None, :] + extent
    )
    labels = jnp.arange(1, starts.shape[0] + 1, dtype=jnp.int32)
    return jnp.sum(jnp.where(inside, labels[None, :], 0), axis=1)


def reach_bounds(positions, starts, extent):
    inside = (positions[:, None] >= starts[None, :]) & (
        positions[:, None] < starts[None, :] + extent
    )
    piece_last = jnp.max(jnp.where(inside, starts[None, :] + extent - 1, 0))
    piece_first = jnp.min(jnp.where(inside, starts[None, :], positions[0]))
    upper = jnp.maximum(positions[-1], piece_last)
    lower = jnp.minimum(positions[0], piece_first)
    return (upper, lower)


def allowed_mask(query_pos, query_ids, key_pos, key_ids):
    causal = key_pos[None, :] <= query_pos[:, None]
    shared = (key_ids[None, :] == query_ids[:, None]) & (query_ids[:, None] > 0)
    return causal | shared


def slot_dest(route_ids, n_ffn, capacity):
    flat_ids = route_ids.reshape(-1)
    onehot = (flat_ids[:, None] == jnp.arange(n_ffn, dtype=jnp.int32)[None, :]).astype(jnp.int32)
    earlier = jnp.cumsum(onehot, axis=0) - onehot
    slot_pos = jnp.sum(earlier * onehot, axis=1)
    return jnp.where(flat_ids < n_ffn, flat_ids * capacity + slot_pos, n_ffn * capacity)


def local_mix(
    normed, res_logits, router, mixing, const_proj, const_vec, expert_rows, route_ids, n_ffn
):
    n_all = router.shape[1]
    logits = jnp.dot(normed, router, precision=HIGH) + jnp.dot(res_logits, mixing, precision=HIGH)
    probs = jax.nn.softmax(logits, axis=-1)
    labels = jnp.arange(n_all, dtype=jnp.int32)
    chosen = jnp.sum(
        jnp.where(route_ids[:, :, None] == labels[None, None, :], probs[:, None, :], 0.0), axis=-1
    )
    gates = chosen / jnp.sum(chosen, axis=1, keepdims=True)
    pair_logits = jnp.dot(normed, const_proj, precision=HIGH)
    first_pair = jax.nn.softmax(pair_logits[:, 0:2], axis=-1)
    second_pair = jax.nn.softmax(pair_logits[:, 2:4], axis=-1)
    first_const = first_pair[:, 0:1] * normed + first_pair[:, 1:2] * const_vec[0][None, :]
    second_const = second_pair[:, 0:1] * normed + second_pair[:, 1:2] * const_vec[1][None, :]
    mixed = jnp.zeros_like(normed)
    for route_k in range(2):
        route_id = route_ids[:, route_k : route_k + 1]
        entry = jnp.where(route_id < n_ffn, expert_rows[:, route_k], 0.0)
        entry = entry + jnp.where(route_id == n_ffn + 1, normed, 0.0)
        entry = entry + jnp.where(route_id == n_ffn + 2, first_const, 0.0)
        entry = entry + jnp.where(route_id == n_ffn + 3, second_const, 0.0)
        mixed = mixed + gates[:, route_k : route_k + 1] * entry
    return mixed


def swiglu_act(gate_pre, up_pre):
    return jax.nn.silu(gate_pre) * up_pre


def body(
    tokens,
    gate_res,
    routes,
    piece_starts,
    norm_attn,
    norm_ffn,
    w_query,
    w_key,
    w_value,
    w_out,
    router,
    mixing,
    const_proj,
    const_vec,
    w_gate,
    w_up,
    w_down,
    cotangent,
):
    n_ffn = lax.axis_size("exp")
    rows_dev = tokens.shape[1]
    model_width = tokens.shape[2]
    seq_length = rows_dev * n_ffn
    score_scale = 1.0 / math.sqrt(HD)
    inputs_f = tokens[0].astype(jnp.float32)
    res_logits = gate_res[0]
    route_ids = routes[0]
    starts = piece_starts[0]
    full_query, full_key, full_value, full_out = (
        lax.all_gather(w_query, "fsdp", axis=0, tiled=True),
        lax.all_gather(w_key, "fsdp", axis=0, tiled=True),
        lax.all_gather(w_value, "fsdp", axis=0, tiled=True),
        lax.all_gather(w_out, "fsdp", axis=0, tiled=True),
    )
    attn_in = rms_scale(inputs_f, norm_attn).astype(jnp.bfloat16)
    query = jnp.dot(attn_in, full_query, preferred_element_type=jnp.float32).astype(jnp.bfloat16)
    key = jnp.dot(attn_in, full_key, preferred_element_type=jnp.float32).astype(jnp.bfloat16)
    value = jnp.dot(attn_in, full_value, preferred_element_type=jnp.float32).astype(jnp.bfloat16)
    keys_all, values_all = (
        lax.all_gather(key, "exp", axis=0, tiled=True),
        lax.all_gather(value, "exp", axis=0, tiled=True),
    )
    query_heads = query.reshape(rows_dev, H, HD)
    key_heads = keys_all.reshape(seq_length, H, HD)
    value_heads = values_all.reshape(seq_length, H, HD)
    query_pos = lax.axis_index("exp") * rows_dev + jnp.arange(rows_dev, dtype=jnp.int32)
    query_ids = piece_ids(query_pos, starts, PIECE)
    key_upper, query_lower = reach_bounds(query_pos, starts, PIECE)
    block_list = jnp.arange(seq_length // KBLK, dtype=jnp.int32)

    def score_block(block_index):
        key_first = block_index * KBLK
        key_block = lax.dynamic_slice_in_dim(key_heads, key_first, KBLK, 0)
        value_block = lax.dynamic_slice_in_dim(value_heads, key_first, KBLK, 0)
        key_pos = key_first + jnp.arange(KBLK, dtype=jnp.int32)
        key_ids = piece_ids(key_pos, starts, PIECE)
        scores = (
            jnp.einsum("qhd,khd->hqk", query_heads, key_block, preferred_element_type=jnp.float32)
            * score_scale
        )
        allowed = allowed_mask(query_pos, query_ids, key_pos, key_ids)[None]
        return (scores, allowed, key_block, value_block)

    def needed(block_index):
        return block_index * KBLK <= key_upper

    def lse_step(carry, block_index):

        def lse_active(state):
            run_max, run_sum = state
            scores, allowed, _, _ = score_block(block_index)
            scores = jnp.where(allowed, scores, NEG)
            new_max = jnp.maximum(run_max, jnp.max(scores, axis=-1))
            exp_terms = jnp.where(allowed, jnp.exp(scores - new_max[..., None]), 0.0)
            return (new_max, run_sum * jnp.exp(run_max - new_max) + jnp.sum(exp_terms, axis=-1))

        return (lax.cond(needed(block_index), lse_active, lambda state: state, carry), None)

    start_carry = (jnp.full((H, rows_dev), NEG, jnp.float32), jnp.zeros((H, rows_dev), jnp.float32))
    (run_max, run_sum), _ = lax.scan(lse_step, start_carry, block_list)
    log_norm = run_max + jnp.log(run_sum)

    def block_probs(scores, allowed):
        return jnp.where(allowed, jnp.exp(scores - log_norm[..., None]), 0.0)

    def out_step(accum, block_index):

        def out_active(total):
            scores, allowed, _, value_block = score_block(block_index)
            probs_low = block_probs(scores, allowed).astype(jnp.bfloat16)
            return total + jnp.einsum(
                "hqk,khd->qhd", probs_low, value_block, preferred_element_type=jnp.float32
            )

        return (lax.cond(needed(block_index), out_active, lambda total: total, accum), None)

    attn_sum, _ = lax.scan(out_step, jnp.zeros((rows_dev, H, HD), jnp.float32), block_list)
    attn_low = attn_sum.astype(jnp.bfloat16).reshape(rows_dev, model_width)
    hidden = inputs_f + jnp.dot(attn_low, full_out, preferred_element_type=jnp.float32)
    normed = rms_scale(hidden, norm_ffn)
    destination = slot_dest(route_ids, n_ffn, CAP)
    sources = jnp.arange(2 * rows_dev, dtype=jnp.int32) // 2
    slot_table = (
        jnp.full((n_ffn * CAP,), rows_dev, jnp.int32).at[destination].set(sources, mode="drop")
    )
    padded = jnp.concatenate(
        [normed.astype(jnp.bfloat16), jnp.zeros((1, model_width), jnp.bfloat16)], axis=0
    )
    dispatched = padded[slot_table].reshape(n_ffn, CAP, model_width)
    received = lax.all_to_all(dispatched, "exp", split_axis=0, concat_axis=0, tiled=True)
    full_gate, full_up, full_down = (
        lax.all_gather(w_gate[0], "fsdp", axis=0, tiled=True),
        lax.all_gather(w_up[0], "fsdp", axis=0, tiled=True),
        lax.all_gather(w_down[0], "fsdp", axis=0, tiled=True),
    )
    slot_rows = received.reshape(n_ffn * CAP, model_width)
    gate_pre = jnp.dot(slot_rows, full_gate, preferred_element_type=jnp.float32)
    up_pre = jnp.dot(slot_rows, full_up, preferred_element_type=jnp.float32)
    inner_act = swiglu_act(gate_pre, up_pre).astype(jnp.bfloat16)
    expert_result = jnp.dot(inner_act, full_down, preferred_element_type=jnp.float32).astype(
        jnp.bfloat16
    )
    returned = lax.all_to_all(
        expert_result.reshape(n_ffn, CAP, model_width),
        "exp",
        split_axis=0,
        concat_axis=0,
        tiled=True,
    )
    returned_pad = jnp.concatenate(
        [returned.reshape(n_ffn * CAP, model_width), jnp.zeros((1, model_width), jnp.bfloat16)],
        axis=0,
    )
    expert_rows = returned_pad[destination].astype(jnp.float32).reshape(rows_dev, 2, model_width)

    def mix_local(normed_in, logits_in, router_in, mixing_in, proj_in, vec_in, rows_in):
        return local_mix(
            normed_in, logits_in, router_in, mixing_in, proj_in, vec_in, rows_in, route_ids, n_ffn
        )

    moe_out, mix_pull = jax.vjp(
        mix_local, normed, res_logits, router, mixing, const_proj, const_vec, expert_rows
    )
    layer_out = (hidden + moe_out).astype(jnp.bfloat16)
    upstream = cotangent[0].astype(jnp.float32)
    d_normed_local, d_res_logits, d_router, d_mixing, d_const_proj, d_const_vec, d_expert_rows = (
        mix_pull(upstream)
    )
    d_rows_low = d_expert_rows.reshape(2 * rows_dev, model_width).astype(jnp.bfloat16)
    d_dispatched = (
        jnp.zeros((n_ffn * CAP, model_width), jnp.bfloat16)
        .at[destination]
        .set(d_rows_low, mode="drop")
    )
    d_received = lax.all_to_all(
        d_dispatched.reshape(n_ffn, CAP, model_width),
        "exp",
        split_axis=0,
        concat_axis=0,
        tiled=True,
    )
    d_received = d_received.reshape(n_ffn * CAP, model_width)
    d_inner = jnp.einsum("rd,fd->rf", d_received, full_down, preferred_element_type=jnp.float32)
    _, act_pull = jax.vjp(swiglu_act, gate_pre, up_pre)
    d_gate_pre, d_up_pre = act_pull(d_inner)
    d_gate_low = d_gate_pre.astype(jnp.bfloat16)
    d_up_low = d_up_pre.astype(jnp.bfloat16)
    grad_down_full = jnp.einsum(
        "rf,rd->fd", inner_act, d_received, preferred_element_type=jnp.float32
    )
    grad_gate_full = jnp.einsum(
        "rd,rf->df", slot_rows, d_gate_low, preferred_element_type=jnp.float32
    )
    grad_up_full = jnp.einsum("rd,rf->df", slot_rows, d_up_low, preferred_element_type=jnp.float32)
    d_slot_rows = (
        jnp.einsum("rf,df->rd", d_gate_low, full_gate, preferred_element_type=jnp.float32)
        + jnp.einsum("rf,df->rd", d_up_low, full_up, preferred_element_type=jnp.float32)
    ).astype(jnp.bfloat16)
    d_sent = lax.all_to_all(
        d_slot_rows.reshape(n_ffn, CAP, model_width), "exp", split_axis=0, concat_axis=0, tiled=True
    )
    d_sent_pad = jnp.concatenate(
        [d_sent.reshape(n_ffn * CAP, model_width), jnp.zeros((1, model_width), jnp.bfloat16)],
        axis=0,
    )
    d_normed_sent = jnp.sum(
        d_sent_pad[destination].astype(jnp.float32).reshape(rows_dev, 2, model_width), axis=1
    )
    _, norm_ffn_pull = jax.vjp(rms_scale, hidden, norm_ffn)
    d_hidden_part, d_norm_ffn = norm_ffn_pull(d_normed_local + d_normed_sent)
    d_hidden = upstream + d_hidden_part
    d_hidden_low = d_hidden.astype(jnp.bfloat16)
    grad_out_full = jnp.einsum(
        "td,te->de", attn_low, d_hidden_low, preferred_element_type=jnp.float32
    )
    d_attn = jnp.einsum(
        "te,de->td", d_hidden_low, full_out, preferred_element_type=jnp.float32
    ).astype(jnp.bfloat16)
    d_attn_heads = d_attn.reshape(rows_dev, H, HD)
    zero_block = jnp.zeros((KBLK, H, HD), jnp.float32)

    def delta_terms(block_index):
        scores, allowed, _, value_block = score_block(block_index)
        probs = block_probs(scores, allowed)
        d_probs = jnp.einsum(
            "qhd,khd->hqk", d_attn_heads, value_block, preferred_element_type=jnp.float32
        )
        part = jnp.sum(probs * d_probs, axis=-1)
        return (
            part,
            jnp.einsum(
                "hqk,qhd->khd",
                probs.astype(jnp.bfloat16),
                d_attn_heads,
                preferred_element_type=jnp.float32,
            ),
        )

    def query_terms(block_index, row_delta):
        scores, allowed, key_block, value_block = score_block(block_index)
        probs = block_probs(scores, allowed)
        d_probs = jnp.einsum(
            "qhd,khd->hqk", d_attn_heads, value_block, preferred_element_type=jnp.float32
        )
        d_scores = (probs * (d_probs - row_delta[..., None])).astype(jnp.bfloat16)
        part = (
            jnp.einsum("hqk,khd->qhd", d_scores, key_block, preferred_element_type=jnp.float32)
            * score_scale
        )
        return (
            part,
            jnp.einsum("hqk,qhd->khd", d_scores, query_heads, preferred_element_type=jnp.float32)
            * score_scale,
        )

    def delta_step(total, block_index):

        def delta_active(running):
            part, grad_block = delta_terms(block_index)
            return (running + part, grad_block)

        return lax.cond(
            needed(block_index), delta_active, lambda running: (running, zero_block), total
        )

    row_delta, grad_values = lax.scan(delta_step, jnp.zeros((H, rows_dev), jnp.float32), block_list)

    def query_step(total, block_index):

        def query_active(running):
            part, grad_block = query_terms(block_index, row_delta)
            return (running + part, grad_block)

        return lax.cond(
            needed(block_index), query_active, lambda running: (running, zero_block), total
        )

    d_query_sum, grad_keys = lax.scan(
        query_step, jnp.zeros((rows_dev, H, HD), jnp.float32), block_list
    )
    grad_keys = grad_keys.reshape(seq_length, model_width)
    grad_values = grad_values.reshape(seq_length, model_width)
    d_key_sum, d_value_sum = (
        lax.psum_scatter(
            grad_keys.astype(jnp.bfloat16), "exp", scatter_dimension=0, tiled=True
        ).astype(jnp.float32),
        lax.psum_scatter(
            grad_values.astype(jnp.bfloat16), "exp", scatter_dimension=0, tiled=True
        ).astype(jnp.float32),
    )
    d_query_low = d_query_sum.reshape(rows_dev, model_width).astype(jnp.bfloat16)
    d_key_low = d_key_sum.astype(jnp.bfloat16)
    d_value_low = d_value_sum.astype(jnp.bfloat16)
    d_attn_in = (
        jnp.einsum("te,de->td", d_query_low, full_query, preferred_element_type=jnp.float32)
        + jnp.einsum("te,de->td", d_key_low, full_key, preferred_element_type=jnp.float32)
        + jnp.einsum("te,de->td", d_value_low, full_value, preferred_element_type=jnp.float32)
    )
    grad_query_full = jnp.einsum(
        "td,te->de", attn_in, d_query_low, preferred_element_type=jnp.float32
    )
    grad_key_full = jnp.einsum("td,te->de", attn_in, d_key_low, preferred_element_type=jnp.float32)
    grad_value_full = jnp.einsum(
        "td,te->de", attn_in, d_value_low, preferred_element_type=jnp.float32
    )
    _, norm_attn_pull = jax.vjp(rms_scale, inputs_f, norm_attn)
    d_inputs_part, d_norm_attn = norm_attn_pull(d_attn_in)
    grad_tokens = (d_hidden + d_inputs_part).astype(jnp.bfloat16)
    attn_shards = (
        lax.psum_scatter(
            grad_query_full.astype(jnp.bfloat16), "fsdp", scatter_dimension=0, tiled=True
        ).astype(jnp.float32),
        lax.psum_scatter(
            grad_key_full.astype(jnp.bfloat16), "fsdp", scatter_dimension=0, tiled=True
        ).astype(jnp.float32),
        lax.psum_scatter(
            grad_value_full.astype(jnp.bfloat16), "fsdp", scatter_dimension=0, tiled=True
        ).astype(jnp.float32),
        lax.psum_scatter(
            grad_out_full.astype(jnp.bfloat16), "fsdp", scatter_dimension=0, tiled=True
        ).astype(jnp.float32),
    )
    attn_shards = (
        lax.psum(attn_shards[0].astype(jnp.bfloat16), "exp").astype(jnp.float32),
        lax.psum(attn_shards[1].astype(jnp.bfloat16), "exp").astype(jnp.float32),
        lax.psum(attn_shards[2].astype(jnp.bfloat16), "exp").astype(jnp.float32),
        lax.psum(attn_shards[3].astype(jnp.bfloat16), "exp").astype(jnp.float32),
    )
    expert_shards = (
        lax.psum_scatter(
            grad_gate_full.astype(jnp.bfloat16), "fsdp", scatter_dimension=0, tiled=True
        ).astype(jnp.float32),
        lax.psum_scatter(
            grad_up_full.astype(jnp.bfloat16), "fsdp", scatter_dimension=0, tiled=True
        ).astype(jnp.float32),
        lax.psum_scatter(
            grad_down_full.astype(jnp.bfloat16), "fsdp", scatter_dimension=0, tiled=True
        ).astype(jnp.float32),
    )
    small_sums = lax.psum(
        (d_norm_attn, d_norm_ffn, d_router, d_mixing, d_const_proj, d_const_vec), ("exp", "fsdp")
    )
    return (
        layer_out[None],
        grad_tokens[None],
        d_res_logits[None],
        small_sums[0],
        small_sums[1],
        attn_shards[0],
        attn_shards[1],
        attn_shards[2],
        attn_shards[3],
        small_sums[2],
        small_sums[3],
        small_sums[4],
        small_sums[5],
        expert_shards[0][None],
        expert_shards[1][None],
        expert_shards[2][None],
    )


def solution(mesh):
    placed = (
        P("fsdp", "exp", None),
        P("fsdp", "exp", None),
        P("fsdp", "exp", None),
        P("fsdp", None),
        P(),
        P(),
        P("fsdp", None),
        P("fsdp", None),
        P("fsdp", None),
        P("fsdp", None),
        P(),
        P(),
        P(),
        P(),
        P("exp", "fsdp", None),
        P("exp", "fsdp", None),
        P("exp", "fsdp", None),
        P("fsdp", "exp", None),
    )
    return jax.shard_map(
        body,
        mesh=mesh,
        in_specs=placed,
        out_specs=(
            P("fsdp", "exp", None),
            P("fsdp", "exp", None),
            P("fsdp", "exp", None),
            P(),
            P(),
            P("fsdp", None),
            P("fsdp", None),
            P("fsdp", None),
            P("fsdp", None),
            P(),
            P(),
            P(),
            P(),
            P("exp", "fsdp", None),
            P("exp", "fsdp", None),
            P("exp", "fsdp", None),
        ),
        check_vma=False,
    )
```

profile of v0, /device:TPU:30, one launch (start us, length us, event | category | flops | bytes accessed | tf_op | source)
XLA Modules:
  0.0 1310.0 jit_solution(17842984721473565674)
XLA Ops:
  10.9 39.2 %all-gather.13.cloned.1.call-done = bf16[768,768]{1,0:T(8,128)(2,1)} async-done(((bf16[96,768]{1,0:T(8,128)(2,1)}), bf16[768,768]{1,0:T(8,128)(2,1)}) %all-gather.13.cloned.1.call-update) | async-done | bytes 1179664 | tf_op jit(solution)/shard_map/all_gather | solution.py:121
  53.4 38.7 %all-gather.17.cloned.1.call-done = bf16[768,768]{1,0:T(8,128)(2,1)} async-done(((bf16[96,768]{1,0:T(8,128)(2,1)}), bf16[768,768]{1,0:T(8,128)(2,1)}) %all-gather.17.cloned.1.call-update) | async-done | bytes 1179664 | tf_op jit(solution)/shard_map/all_gather | solution.py:120
  109.0 25.2 %all-gather.21.cloned.1.call-done = bf16[768,768]{1,0:T(8,128)(2,1)} async-done(((bf16[96,768]{1,0:T(8,128)(2,1)}), bf16[768,768]{1,0:T(8,128)(2,1)}) %all-gather.21.cloned.1.call-update) | async-done | bytes 1179664 | tf_op jit(solution)/shard_map/all_gather | solution.py:119
  136.6 28.1 %all-gather.15.cloned.1.call-done = bf16[2048,768]{1,0:T(8,128)(2,1)} async-done(((bf16[512,768]{1,0:T(8,128)(2,1)}), bf16[2048,768]{1,0:T(8,128)(2,1)}) %all-gather.15.cloned.1.call-update) | async-done | bytes 3145744 | tf_op jit(solution)/shard_map/all_gather | solution.py:130
  169.5 25.8 %all-gather.19.cloned.1.call-done = bf16[2048,768]{1,0:T(8,128)(2,1)} async-done(((bf16[512,768]{1,0:T(8,128)(2,1)}), bf16[2048,768]{1,0:T(8,128)(2,1)}) %all-gather.19.cloned.1.call-update) | async-done | bytes 3145744 | tf_op jit(solution)/shard_map/all_gather | solution.py:129
  200.0 27.8 %while.59 = (s32[]{:T(128)}, f32[12,512]{1,0:T(8,128)S(1)}, f32[12,512]{1,0:T(8,128)S(1)}, s32[4]{0:T(128)S(1)}, s32[]{:T(128)}, /*index=5*/s32[1,4]{1,0:T(1,128...) while((s32[]{:T(128)}, f32[12,512]{1,0:T(8,128)S(1)}, ...), condition=%wide.region_9.10_spmd.clone, body=%wide.region_3.9_spmd.clone.sunk | while | flops 428891136 | bytes 27868588 | solution.py:169
  229.2 28.6 %while.60 = (s32[]{:T(128)}, f32[512,12,64]{0,2,1:T(8,128)}, s32[4]{0:T(128)S(1)}, s32[]{:T(128)}, bf16[2048,12,64]{0,2,1:T(8,128)(2,1)}, /*index=5*/s32[1,4]{1,...) while((s32[]{:T(128)}, f32[512,12,64]{0,2,1:T(8,128)}, ...), condition=%wide.region_14.15_spmd.clone, body=%wide.region_10.14_spmd.clone.sunk | while | flops 819342336 | bytes 6078873 | solution.py:186
  323.1 36.6 %all-gather.27.cloned.1.call-done = bf16[1,768,2048]{2,1,0:T(8,128)(2,1)} async-done(((bf16[1,96,2048]{2,1,0:T(8,128)(2,1)}), bf16[1,768,2048]{2,1,0:T(8,128)(2,1)}) %all-gather.27.cloned.1.call-update) | async-done | bytes 3145744 | tf_op jit(solution)/shard_map/all_gather | solution.py:202
  366.6 54.4 %all-gather.25.cloned.1.call-done = bf16[1,768,2048]{2,1,0:T(8,128)(2,1)} async-done(((bf16[1,96,2048]{2,1,0:T(8,128)(2,1)}), bf16[1,768,2048]{2,1,0:T(8,128)(2,1)}) %all-gather.25.cloned.1.call-update) | async-done | bytes 3145744 | tf_op jit(solution)/shard_map/all_gather | solution.py:201
  512.2 57.3 %while.61 = (s32[]{:T(128)}, f32[12,512]{1,0:T(8,128)S(1)}, bf16[4,512,12,64]{1,3,2,0:T(8,128)(2,1)}, s32[4]{0:T(128)S(1)}, s32[]{:T(128)}, /*index=5*/s32[1,4]{...) while((s32[]{:T(128)}, f32[12,512]{1,0:T(8,128)S(1)}, ...), condition=%wide.region_47.48_spmd.clone, body=%wide.region_42.47_spmd.clone.sunk | while | flops 1237330944 | bytes 95329760 | solution.py:335
  572.5 70.1 %while.62 = (s32[]{:T(128)}, f32[512,12,64]{0,2,1:T(8,128)S(1)}, bf16[4,512,12,64]{1,3,2,0:T(8,128)(2,1)}, s32[4]{0:T(128)S(1)}, s32[]{:T(128)}, /*index=5*/bf16...) while((s32[]{:T(128)}, f32[512,12,64]{0,2,1:T(8,128)S(1)}, ...), condition=%wide.region_52.53_spmd.clone, body=%wide.region_48.52_spmd.clone.sunk | while | flops 1632119808 | bytes 58007028 | solution.py:347
  573.8 20.3 %conditional.15 = (f32[512,12,64]{0,2,1:T(8,128)S(1)}, bf16[1,512,12,64]{1,3,2,0:T(8,128)(2,1)S(1)}) conditional(s32[]{:T(128)} %convert_element_type.428, f32[512,12,64]{0,2,1:T(8,128)S(1)} %get-tuple-element.1275, (s32[]{:T(128)}, bf16[2048,12,64]{0,2,1:T(8,128)(2,1)}, s32[]{:T(128)}, s32[1,4]{1,0:T(1,128)S(1)}, s32[512]{0:T(512)S(1)}, ...), branch_computations={%region_49.49_spmd, %region_50.51_spmd} | conditional | flops 1632119808 | bytes 56431820 | solution.py:343
  596.3 20.3 %conditional.15 = (f32[512,12,64]{0,2,1:T(8,128)S(1)}, bf16[1,512,12,64]{1,3,2,0:T(8,128)(2,1)S(1)}) conditional(s32[]{:T(128)} %convert_element_type.428, f32[512,12,64]{0,2,1:T(8,128)S(1)} %get-tuple-element.1275, (s32[]{:T(128)}, bf16[2048,12,64]{0,2,1:T(8,128)(2,1)}, s32[]{:T(128)}, s32[1,4]{1,0:T(1,128)S(1)}, s32[512]{0:T(512)S(1)}, ...), branch_computations={%region_49.49_spmd, %region_50.51_spmd} | conditional | flops 1632119808 | bytes 56431820 | solution.py:343
  618.9 20.3 %conditional.15 = (f32[512,12,64]{0,2,1:T(8,128)S(1)}, bf16[1,512,12,64]{1,3,2,0:T(8,128)(2,1)S(1)}) conditional(s32[]{:T(128)} %convert_element_type.428, f32[512,12,64]{0,2,1:T(8,128)S(1)} %get-tuple-element.1275, (s32[]{:T(128)}, bf16[2048,12,64]{0,2,1:T(8,128)(2,1)}, s32[]{:T(128)}, s32[1,4]{1,0:T(1,128)S(1)}, s32[512]{0:T(512)S(1)}, ...), branch_computations={%region_49.49_spmd, %region_50.51_spmd} | conditional | flops 1632119808 | bytes 56431820 | solution.py:343
  681.6 41.8 %reduce-scatter.10.cloned.1.call-done = bf16[512,768]{0,1:T(8,128)(2,1)} async-done(((bf16[2048,768]{0,1:T(8,128)(2,1)}), bf16[512,768]{0,1:T(8,128)(2,1)}) %reduce-scatter.10.cloned.1.call-update) | async-done | bytes 786448 | tf_op jit(solution)/shard_map/reduce_scatter | solution.py:353
  731.6 32.4 %reduce-scatter.12.cloned.1.call-done = bf16[512,768]{0,1:T(8,128)(2,1)} async-done(((bf16[2048,768]{0,1:T(8,128)(2,1)}), bf16[512,768]{0,1:T(8,128)(2,1)}) %reduce-scatter.12.cloned.1.call-update) | async-done | bytes 786448 | tf_op jit(solution)/shard_map/reduce_scatter | solution.py:356
  767.4 73.7 %reduce-scatter.26.cloned.1.call-done = bf16[256,768]{1,0:T(8,128)(2,1)} async-done(((bf16[2048,768]{1,0:T(8,128)(2,1)}), bf16[256,768]{1,0:T(8,128)(2,1)}) %reduce-scatter.26.cloned.1.call-update) | async-done | bytes 393232 | tf_op jit(solution)/shard_map/reduce_scatter | solution.py:405
  843.1 74.8 %reduce-scatter.22.cloned.1.call-done = bf16[96,2048]{1,0:T(8,128)(2,1)} async-done(((bf16[768,2048]{1,0:T(8,128)(2,1)}), bf16[96,2048]{1,0:T(8,128)(2,1)}) %reduce-scatter.22.cloned.1.call-update) | async-done | bytes 393232 | tf_op jit(solution)/shard_map/reduce_scatter | solution.py:399
  919.8 75.1 %reduce-scatter.24.cloned.1.call-done = bf16[96,2048]{1,0:T(8,128)(2,1)} async-done(((bf16[768,2048]{1,0:T(8,128)(2,1)}), bf16[96,2048]{1,0:T(8,128)(2,1)}) %reduce-scatter.24.cloned.1.call-update) | async-done | bytes 393232 | tf_op jit(solution)/shard_map/reduce_scatter | solution.py:402
  1001.4 41.5 %all-reduce.15 = (f32[768]{0:T(1024)}, f32[768]{0:T(1024)}, f32[768,8]{0,1:T(8,128)}, f32[8,8]{0,1:T(8,128)S(1)}, f32[768,4]{0,1:T(4,128)}, /*index=5*/f32[2,768]{1,0:T(2,128)}) all-reduce(f32[768]{0:T(1024)S(1)} %get-tuple-element.643, f32[768]{0:T(1024)S(1)} %copy-done.57, ...), channel_id=1, replica_groups=mesh['exp'=4,'fsdp'=8] {'exp','fsdp'}, use_global_device_ids=true, to_apply=%region_57.58 | all-reduce | flops 12352 | bytes 98816 | tf_op jit(solution)/shard_map/psum | solution.py:409
  1061.3 66.3 %reduce-scatter.20.cloned.1.call-done = bf16[96,768]{1,0:T(8,128)(2,1)} async-done(((bf16[768,768]{1,0:T(8,128)(2,1)}), bf16[96,768]{1,0:T(8,128)(2,1)}) %reduce-scatter.20.cloned.1.call-update) | async-done | bytes 147472 | tf_op jit(solution)/shard_map/reduce_scatter | solution.py:388
  1127.6 66.2 %reduce-scatter.16.cloned.1.call-done = bf16[96,768]{1,0:T(8,128)(2,1)} async-done(((bf16[768,768]{1,0:T(8,128)(2,1)}), bf16[96,768]{1,0:T(8,128)(2,1)}) %reduce-scatter.16.cloned.1.call-update) | async-done | bytes 147472 | tf_op jit(solution)/shard_map/reduce_scatter | solution.py:382
  1193.8 66.5 %reduce-scatter.18.cloned.1.call-done = bf16[96,768]{1,0:T(8,128)(2,1)} async-done(((bf16[768,768]{1,0:T(8,128)(2,1)}), bf16[96,768]{1,0:T(8,128)(2,1)}) %reduce-scatter.18.cloned.1.call-update) | async-done | bytes 147472 | tf_op jit(solution)/shard_map/reduce_scatter | solution.py:385
  1263.1 33.6 %all-reduce.19.cloned.1.call-done = (bf16[96,768]{1,0:T(8,128)(2,1)}, bf16[96,768]{1,0:T(8,128)(2,1)}, bf16[96,768]{1,0:T(8,128)(2,1)}, bf16[96,768]{1,0:T(8,128)(2,1)}) async-done(((bf16[96,768]{1,0:T(8,128)(2,1)}, bf16[96,768]{1,0:T(8,128)(2,1)}, bf16[96,768]{1,0:T(8,128)(2,1)}, bf16[96,768]{1,0:T(8,128)(2,1)}), (bf16[96,768]{1,0:T(8,128)(2,1)}, bf16[96,768]{1,0:T(8,128)(2,1)}, bf16[96,768]{1,0:T(8,128)(2,1)}, ...) | async-done | bytes 589840 | tf_op jit(solution)/shard_map/psum | solution.py:393
  (506 shorter events, 547.1 us)
Async XLA Ops:
  7.2 42.9 %all-gather.13.cloned.1.call-start = ((), (), s32[]{:S(2)}) async-start(), calls=%async_computation.13 | async-start | bytes 1327104 | tf_op jit(solution)/shard_map/all_gather | solution.py:121
  7.9 84.2 %all-gather.17.cloned.1.call-start = ((), (), s32[]{:S(2)}) async-start(), calls=%async_computation.15 | async-start | bytes 1327104 | tf_op jit(solution)/shard_map/all_gather | solution.py:120
  8.7 125.5 %all-gather.21.cloned.1.call-start = ((), (), s32[]{:S(2)}) async-start(), calls=%async_computation.17 | async-start | bytes 1327104 | tf_op jit(solution)/shard_map/all_gather | solution.py:119
  9.4 155.3 %all-gather.15.cloned.1.call-start = ((), (), s32[]{:S(2)}) async-start(), calls=%async_computation.14 | async-start | bytes 3932160 | tf_op jit(solution)/shard_map/all_gather | solution.py:130
  53.3 142.0 %all-gather.19.cloned.1.call-start = ((), (), s32[]{:S(2)}) async-start(), calls=%async_computation.16 | async-start | bytes 3932160 | tf_op jit(solution)/shard_map/all_gather | solution.py:129
  95.2 165.1 %all-gather.23.cloned.1.call-start = ((), (), s32[]{:S(2)}) async-start(), calls=%async_computation.18 | async-start | bytes 1327104 | tf_op jit(solution)/shard_map/all_gather | solution.py:122
  95.8 220.6 %all-gather.29.cloned.1.call-start = ((), (), s32[]{:S(2)}) async-start(), calls=%async_computation.30 | async-start | bytes 3538944 | tf_op jit(solution)/shard_map/all_gather | solution.py:203
  96.5 263.2 %all-gather.27.cloned.1.call-start = ((), (), s32[]{:S(2)}) async-start(), calls=%async_computation.29 | async-start | bytes 3538944 | tf_op jit(solution)/shard_map/all_gather | solution.py:202
  97.3 323.8 %all-gather.25.cloned.1.call-start = ((), (), s32[]{:S(2)}) async-start(), calls=%async_computation.28 | async-start | bytes 3538944 | tf_op jit(solution)/shard_map/all_gather | solution.py:201
  279.4 30.8 %all-to-all-start.2 = ((bf16[4,160,768]{2,1,0:T(8,128)(2,1)}), bf16[4,160,768]{2,1,0:T(8,128)(2,1)}, u32[]{:S(2)}, u32[]{:S(2)}) async-start(bf16[4,160,768]{2,1,0:T(8,128)(2,1)} %bitcast.59), calls=%async_computation.2 | async-start | bytes 1966080 | tf_op jit(solution)/shard_map/all_to_all | solution.py:244
  310.2 49.5 %all-to-all-start = ((bf16[4,160,768]{2,1,0:T(8,128)(2,1)}), bf16[4,160,768]{2,1,0:T(8,128)(2,1)S(1)}, u32[]{:S(2)}, u32[]{:S(2)}) async-start(bf16[4,160,768]{2,1,0:T(8,128)(2,1)} %bitcast.35), calls=%async_computation | async-start | bytes 1966080 | tf_op jit(solution)/shard_map/all_to_all | solution.py:199
  437.5 16.1 %all-to-all-start.3 = ((bf16[4,160,768]{2,1,0:T(8,128)(2,1)}), bf16[4,160,768]{2,1,0:T(8,128)(2,1)S(1)}, u32[]{:S(2)}, u32[]{:S(2)}) async-start(bf16[4,160,768]{2,1,0:T(8,128)(2,1)} %bitcast.379), calls=%async_computation.3 | async-start | bytes 1966080 | tf_op jit(solution)/shard_map/all_to_all | solution.py:268
  453.6 18.1 %all-to-all-start.1 = ((bf16[4,160,768]{2,1,0:T(8,128)(2,1)}), bf16[4,160,768]{2,1,0:T(8,128)(2,1)}, u32[]{:S(2)}, u32[]{:S(2)}) async-start(bf16[4,160,768]{2,1,0:T(8,128)(2,1)} %bitcast.378), calls=%async_computation.1 | async-start | bytes 1966080 | tf_op jit(solution)/shard_map/all_to_all | solution.py:212
  459.5 263.9 %reduce-scatter.10.cloned.1.call-start = ((), (), s32[]{:S(2)}) async-start(), calls=%async_computation.19 | async-start | bytes 3932160 | tf_op jit(solution)/shard_map/reduce_scatter | solution.py:353
  649.7 114.4 %reduce-scatter.12.cloned.1.call-start = ((), (), s32[]{:S(2)}) async-start(), calls=%async_computation.20 | async-start | bytes 3932160 | tf_op jit(solution)/shard_map/reduce_scatter | solution.py:356
  656.8 184.3 %reduce-scatter.26.cloned.1.call-start = ((), (), s32[]{:S(2)}) async-start(), calls=%async_computation.27 | async-start | bytes 3538944 | tf_op jit(solution)/shard_map/reduce_scatter | solution.py:405
  663.2 254.7 %reduce-scatter.22.cloned.1.call-start = ((), (), s32[]{:S(2)}) async-start(), calls=%async_computation.25 | async-start | bytes 3538944 | tf_op jit(solution)/shard_map/reduce_scatter | solution.py:399
  670.2 324.7 %reduce-scatter.24.cloned.1.call-start = ((), (), s32[]{:S(2)}) async-start(), calls=%async_computation.26 | async-start | bytes 3538944 | tf_op jit(solution)/shard_map/reduce_scatter | solution.py:402
  676.3 385.0 %reduce-scatter.14.cloned.1.call-start = ((), (), s32[]{:S(2)}) async-start(), calls=%async_computation.21 | async-start | bytes 1327104 | tf_op jit(solution)/shard_map/reduce_scatter | solution.py:379
  679.5 448.1 %reduce-scatter.20.cloned.1.call-start = ((), (), s32[]{:S(2)}) async-start(), calls=%async_computation.24 | async-start | bytes 1327104 | tf_op jit(solution)/shard_map/reduce_scatter | solution.py:388
  681.5 512.3 %reduce-scatter.16.cloned.1.call-start = ((), (), s32[]{:S(2)}) async-start(), calls=%async_computation.22 | async-start | bytes 1327104 | tf_op jit(solution)/shard_map/reduce_scatter | solution.py:382
  726.5 533.8 %reduce-scatter.18.cloned.1.call-start = ((), (), s32[]{:S(2)}) async-start(), calls=%async_computation.23 | async-start | bytes 1327104 | tf_op jit(solution)/shard_map/reduce_scatter | solution.py:385
  767.2 529.4 %all-reduce.19.cloned.1.call-start = ((), (), s32[]{:S(2)}) async-start(), calls=%async_computation.31 | async-start | bytes 1179648 | tf_op jit(solution)/shard_map/psum | solution.py:393
  999.1 261.2 %copy-start.7 = (f32[512,768]{1,0:T(8,128)S(1)}, f32[512,768]{1,0:T(8,128)}, u32[]{:S(2)}) copy-start(f32[512,768]{1,0:T(8,128)} %copy-done.5) | copy-start | bytes 4718596
  (74 other events, 2438.4 us)
Sparse Core Ops, SparseCore 0:
  10.2 39.8 all-gather.12
  52.2 39.8 all-gather.16
  94.3 39.8 all-gather.20
  136.2 28.5 all-gather.14
  166.7 28.5 all-gather.18
  197.3 39.8 all-gather.22
  239.4 59.0 all-gather.28
  300.6 59.0 all-gather.26
  361.9 59.0 all-gather.24
  649.8 73.5 reduce-scatter.9
  726.1 37.9 reduce-scatter.11
  767.5 73.5 reduce-scatter.25
  844.7 73.1 reduce-scatter.21
  921.3 73.5 reduce-scatter.23
  998.2 63.1 reduce-scatter.13
  1064.6 62.9 reduce-scatter.19
  1130.8 62.9 reduce-scatter.15
  1197.0 63.1 reduce-scatter.17
  1262.8 33.7 all-reduce.18
where the time goes:
time: 1320 us; the launch traced here: 1310 us
  waiting for transfers between devices  815 us (62%)
  matrix products  223 us (17%)
  local copies, waits for them, and re-layouts  107 us (8%)
  other arithmetic  52.3 us (4%)
  blocking collectives  41.5 us (3%)
  starting transfers between devices  34.8 us (3%)
  loops' own time  20.3 us (2%)
  between operations  16.7 us (1%)
    reduce_scatter x1, waiting for transfers between devices, body(): lax.psum_scatter(grad_up_full.astype(jnp.bfloat16), 'fsdp', scatter_dimen...  75.1 us
    reduce_scatter x1, waiting for transfers between devices, body(): lax.psum_scatter(grad_gate_full.astype(jnp.bfloat16), 'fsdp', scatter_dim...  74.8 us
    reduce_scatter x1, waiting for transfers between devices, body(): lax.psum_scatter(grad_down_full.astype(jnp.bfloat16), 'fsdp', scatter_dim...  73.7 us
    reduce_scatter x1, waiting for transfers between devices, body(): lax.psum_scatter(grad_value_full.astype(jnp.bfloat16), 'fsdp', scatter_di...  66.5 us
    reduce_scatter x1, waiting for transfers between devices, body(): lax.psum_scatter(grad_out_full.astype(jnp.bfloat16), 'fsdp', scatter_dime...  66.3 us
    reduce_scatter x1, waiting for transfers between devices, body(): lax.psum_scatter(grad_key_full.astype(jnp.bfloat16), 'fsdp', scatter_dime...  66.2 us
    all_gather x1, waiting for transfers between devices, body(): lax.all_gather(w_gate[0], 'fsdp', axis=0, tiled=True)  54.4 us
    reduce_scatter x1, waiting for transfers between devices, body(): lax.psum_scatter(grad_keys.astype(jnp.bfloat16), 'exp', scatter_dimension...  41.8 us
  transfers between devices with their start and end apart: 23, of which 20 were waited for; matrix products, arithmetic and copies ran while one was open for 14% of the time, Pallas kernels for 0%

commit v1 on v0

--- a/solution.py
+++ b/solution.py
@@ -1,8 +1,9 @@
-import math
-
-import jax
-import jax.numpy as jnp
+import functools, math
+import jax, jax.numpy as jnp
 from jax import lax
+from jax.experimental import pallas as pl
+from jax.experimental.pallas import tpu as pltpu
+
 from jax.sharding import PartitionSpec as P
 
 H = 12
@@ -84,6 +85,379 @@
 
 def swiglu_act(gate_pre, up_pre):
     return jax.nn.silu(gate_pre) * up_pre
+
+
+MESH = pl.DeviceIdType.MESH
+BF = jnp.bfloat16
+F32 = jnp.float32
+LOG2E = 1.4426950408889634
+QSCALE = LOG2E / math.sqrt(HD)
+
+
+class Place:
+    def __init__(self):
+        self.e = lax.axis_index("exp")
+        self.f = lax.axis_index("fsdp")
+        self.z = self.f // 2
+        self.x = self.f % 2
+        self.sib = self.e + 1 - 2 * (self.e % 2)
+        self.yp = (self.e + 2) % 4
+        self.diag = (self.sib + 2) % 4
+        self.xf = self.f + 1 - 2 * self.x
+        self.exp_peers = (self.sib, self.yp, self.diag)
+
+    def zf(self, d):
+        return ((self.z + d) % 4) * 2 + self.x
+
+    def barrier(self):
+        sem = pltpu.get_barrier_semaphore()
+        for p in self.exp_peers:
+            pl.semaphore_signal(sem, inc=1, device_id=(p, self.f), device_id_type=MESH)
+        for d in (1, 2, 3):
+            pl.semaphore_signal(sem, inc=1, device_id=(self.e, self.zf(d)), device_id_type=MESH)
+        pl.semaphore_signal(sem, inc=1, device_id=(self.e, self.xf), device_id_type=MESH)
+        pl.semaphore_wait(sem, 7)
+
+    def send(self, src, dst, ss, rs, e=None, f=None):
+        return pltpu.make_async_remote_copy(
+            src_ref=src,
+            dst_ref=dst,
+            send_sem=ss,
+            recv_sem=rs,
+            device_id=(self.e if e is None else e, self.f if f is None else f),
+            device_id_type=MESH,
+        )
+
+
+def lane_of(shape):
+    return lax.broadcasted_iota(jnp.int32, shape, len(shape) - 1)
+
+
+def ka_kernel(
+    x_ref, u_ref, wq_ref, wo_ref, wg_ref, wu_ref, wd_ref, gres_ref, routes_ref, routes_t_ref, starts_ref,
+    gain_a_ref, gain_f_ref, router_ref, proj_ref, mix_ref,
+    attn_all, q_s, k_s, v_s, o_s, lse_s, hidden_ref, logit_ref, pair_ref, place_ref, recv, wo_full, wq_full,
+    gate_full, up_full, down_full,
+    attn_recv, nb, snd, m_s, l_s, acc_s, gsel,
+    wq_ss, wq_rs, wo_ss, wo_rs, at_ss, at_rs, o_ss, o_rs, d_ss, d_rs,
+    us, ur, ds, dr, xs, xr, loc,
+):
+    me = Place()
+    e, f, z, xf = me.e, me.f, me.z, me.xf
+    T, D = x_ref.shape
+    C = D // 4
+    R = wo_ref.shape[0]
+    me.barrier()
+
+    def rows(ref, index):
+        return ref.at[pl.ds(pl.multiple_of(index * R, 32), R)]
+
+    early = ((wq_ref, wq_full, wq_ss, wq_rs, 0), (wo_ref, wo_full, wo_ss, wo_rs, 1))
+    for src, dst, ss, rs, li in early:
+        for d in (1, 3, 2):
+            me.send(src, rows(dst, f), ss.at[d], rs.at[d], f=me.zf(d)).start()
+        me.send(src, rows(dst, f), ss.at[0], rs.at[0], f=xf).start()
+        pltpu.make_async_copy(src, rows(dst, f), loc.at[li]).start()
+
+    xv = x_ref[...].astype(F32)
+    inv = lax.rsqrt(jnp.mean(xv * xv, axis=-1, keepdims=True) + EPS)
+    attn_all[e] = (xv * inv * gain_a_ref[...]).astype(BF)
+    to_sib = me.send(attn_all.at[e], attn_all.at[e], at_ss.at[0], at_rs.at[0], e=me.sib)
+    to_yp = me.send(attn_all.at[e], attn_all.at[e], at_ss.at[1], at_rs.at[1], e=me.yp)
+    to_yp.start()
+    to_sib.start()
+
+    def early_in(dst, ss, rs, d):
+        return me.send(rows(dst, f), rows(dst, ((z - d + 4) % 4) * 2 + me.x), ss.at[d], rs.at[d])
+
+    def early_fwd(dst, ss, rs, d):
+        slot = rows(dst, ((z - d + 4) % 4) * 2 + me.x)
+        return me.send(slot, slot, ss.at[3 + d], rs.at[3 + d], f=xf)
+
+    for src, dst, ss, rs, li in early:
+        for d in (1, 3, 2):
+            early_in(dst, ss, rs, d).wait_recv()
+            early_fwd(dst, ss, rs, d).start()
+
+    shards = ((wg_ref, gate_full), (wu_ref, up_full), (wd_ref, down_full))
+
+    def up_send(w, p, src, slot):
+        full = shards[w][1]
+        return me.send(src, full.at[slot], us.at[w, p], ur.at[w, p], f=f + 2)
+
+    def down_send(w, p, src, slot):
+        full = shards[w][1]
+        return me.send(src, full.at[slot], ds.at[w, p], dr.at[w, p], f=f - 2)
+
+    def x_send(w, i, src, slot):
+        full = shards[w][1]
+        return me.send(src, full.at[slot], xs.at[w, i], xr.at[w, i], f=xf)
+
+    def experts(p):
+        for w, (src, full) in enumerate(shards):
+            if p == 0:
+                x_send(w, 0, src, f).start()
+
+                @pl.when(z <= 2)
+                def _():
+                    up_send(w, 0, src, f).start()
+
+                @pl.when(z >= 1)
+                def _():
+                    down_send(w, 0, src, f).start()
+
+                pltpu.make_async_copy(src, full.at[f], loc.at[2 + w]).start()
+            else:
+
+                @pl.when(z >= p)
+                def _():
+                    slot = f - 2 * p
+                    up_send(w, p - 1, full.at[slot], slot).wait_recv()
+                    if p <= 2:
+
+                        @pl.when(z <= 2)
+                        def _():
+                            up_send(w, p, full.at[slot], slot).start()
+
+                    x_send(w, p, full.at[slot], slot).start()
+
+                @pl.when(z + p <= 3)
+                def _():
+                    slot = f + 2 * p
+                    down_send(w, p - 1, full.at[slot], slot).wait_recv()
+                    if p <= 2:
+
+                        @pl.when(z >= 1)
+                        def _():
+                            down_send(w, p, full.at[slot], slot).start()
+
+                    x_send(w, 3 + p, full.at[slot], slot).start()
+
+    experts(0)
+
+    me.send(attn_all.at[me.yp], attn_all.at[me.yp], at_ss.at[1], at_rs.at[1]).wait_recv()
+    fwd = me.send(attn_all.at[me.yp], attn_all.at[me.yp], at_ss.at[2], at_rs.at[2], e=me.sib)
+    fwd.start()
+    me.send(attn_all.at[me.sib], attn_all.at[me.sib], at_ss.at[0], at_rs.at[0]).wait_recv()
+    me.send(attn_all.at[me.diag], attn_all.at[me.diag], at_ss.at[2], at_rs.at[2]).wait_recv()
+
+    def early_wait(src, dst, ss, rs, li):
+        pltpu.make_async_copy(src, rows(dst, f), loc.at[li]).wait()
+        me.send(rows(dst, xf), rows(dst, xf), ss.at[0], rs.at[0]).wait_recv()
+        for d in (1, 2, 3):
+            slot = rows(dst, ((z - d + 4) % 4) * 2 + 1 - me.x)
+            me.send(slot, slot, ss.at[3 + d], rs.at[3 + d]).wait_recv()
+
+    early_wait(*early[0])
+
+    def qkv_step(i, _):
+        b = i // 2
+        r = pl.ds(pl.multiple_of((i % 2) * 256, 256), 256)
+        out = jnp.dot(attn_all[b, r, :], wq_full[...], preferred_element_type=F32)
+        q_s[b, r, :] = (out[:, 0:C] * QSCALE).astype(BF)
+        k_s[b, r, :] = pltpu.roll(out[:, 128:384], 192, 1)[:, 0:C].astype(BF)
+        v_s[b, r, :] = out[:, 2 * C : 3 * C].astype(BF)
+        return 0
+
+    lax.fori_loop(0, 8, qkv_step, 0)
+    experts(1)
+
+    head_of = lane_of((T, C)) // HD
+
+    def head_step(i, _):
+        qb = i // 3
+        h = i % 3
+        qh = jnp.where(head_of == h, q_s[qb], jnp.zeros((T, C), BF))
+        s = lax.dot_general(qh, k_s[qb], (((1,), (1,)), ((), ())), preferred_element_type=F32)
+        col = lane_of((T, T))
+        row = lax.broadcasted_iota(jnp.int32, (T, T), 0)
+        first = starts_ref[0, qb] - qb * T
+        inside_c = (col >= first) & (col < first + PIECE)
+        inside_r = (row >= first) & (row < first + PIECE)
+        s = jnp.where((col <= row) | (inside_c & inside_r), s, NEG)
+        m = jnp.max(s, axis=-1, keepdims=True)
+        p = jnp.exp2(s - m)
+        m_s[...] = m
+        l_s[...] = jnp.sum(p, axis=-1, keepdims=True)
+        acc_s[...] = jnp.dot(p.astype(BF), v_s[qb], preferred_element_type=F32)
+
+        def kv_step(kb, _):
+            s = lax.dot_general(qh, k_s[kb], (((1,), (1,)), ((), ())), preferred_element_type=F32)
+            m_old = m_s[...]
+            m = jnp.maximum(m_old, jnp.max(s, axis=-1, keepdims=True))
+            scale = jnp.exp2(m_old - m)
+            p = jnp.exp2(s - m)
+            m_s[...] = m
+            l_s[...] = l_s[...] * scale + jnp.sum(p, axis=-1, keepdims=True)
+            acc_s[...] = acc_s[...] * scale + jnp.dot(p.astype(BF), v_s[kb], preferred_element_type=F32)
+            return 0
+
+        lax.fori_loop(0, qb, kv_step, 0)
+        total = l_s[...]
+        o_s[qb] = jnp.where(head_of == h, (acc_s[...] / total).astype(BF), o_s[qb])
+        lse = m_s[...] + jnp.log2(total)
+        lse_s[qb] = jnp.where(lane_of((T, 8)) == h, lse, lse_s[qb])
+        return 0
+
+    lax.fori_loop(0, 12, head_step, 0)
+
+    for i, p in enumerate(me.exp_peers):
+        me.send(o_s.at[p], attn_recv.at[e], o_ss.at[i], o_rs.at[i], e=p).start()
+    attn_recv[e] = o_s[e]
+    experts(2)
+
+    r0, r1 = routes_t_ref[0:1, :], routes_t_ref[1:2, :]
+    expert = lax.broadcasted_iota(jnp.int32, (8, T), 0)
+    has = (expert == r0) | (expert == r1)
+    earlier = (lax.broadcasted_iota(jnp.int32, (T, T), 0) < lane_of((T, T))).astype(BF)
+    count = jnp.dot(has.astype(BF), earlier, preferred_element_type=F32).astype(jnp.int32)
+    count = jnp.where(has, count, -1)
+    slot_id = lax.broadcasted_iota(jnp.int32, (CAP, T), 0)
+    for k in range(4):
+        place_ref[k] = jnp.where(slot_id == count[k : k + 1, :], 1.0, 0.0).astype(BF)
+
+    early_wait(*early[1])
+    for i, p in enumerate(me.exp_peers):
+        me.send(attn_recv.at[p], attn_recv.at[p], o_ss.at[i], o_rs.at[i]).wait_recv()
+
+    def hidden_step(i, _):
+        r = pl.ds(pl.multiple_of(i * 256, 256), 256)
+        h = x_ref[r, :].astype(F32)
+        for b in range(4):
+            h = h + jnp.dot(attn_recv[b, r, :], wo_full[b * C : (b + 1) * C, :], preferred_element_type=F32)
+        hidden_ref[r, :] = h
+        n = h * lax.rsqrt(jnp.mean(h * h, axis=-1, keepdims=True) + EPS) * gain_f_ref[...]
+        nb[r, :] = n.astype(BF)
+        logits = jnp.dot(n, router_ref[...], precision=HIGH, preferred_element_type=F32)
+        logits = logits + jnp.dot(gres_ref[r, :], mix_ref[...], precision=HIGH, preferred_element_type=F32)
+        logit_ref[r, :] = logits
+        pair_ref[r, :] = jnp.dot(n, proj_ref[...], precision=HIGH, preferred_element_type=F32)
+        gsel[r, :] = gates_of(logits, routes_ref[r, :])
+        return 0
+
+    lax.fori_loop(0, 2, hidden_step, 0)
+
+    def dispatch_step(k, _):
+        place = place_ref[k]
+        snd[k, 0] = jnp.dot(place, nb[...], preferred_element_type=F32).astype(BF)
+        gate = jnp.sum(jnp.where(lane_of((T, 8)) == k, gsel[...], 0.0), axis=-1, keepdims=True)
+        gu = (gate * u_ref[...].astype(F32)).astype(BF)
+        snd[k, 1] = jnp.dot(place, gu, preferred_element_type=F32).astype(BF)
+        return 0
+
+    lax.fori_loop(0, 4, dispatch_step, 0)
+    for i, p in enumerate(me.exp_peers):
+        me.send(snd.at[p], recv.at[e], d_ss.at[i], d_rs.at[i], e=p).start()
+    recv[e] = snd[e]
+    experts(3)
+
+    for src, dst, ss, rs, li in early:
+        for j in range(4):
+            me.send(src, rows(dst, f), ss.at[j], rs.at[j]).wait_send()
+        for d in (1, 2, 3):
+            early_fwd(dst, ss, rs, d).wait_send()
+    to_sib.wait_send()
+    to_yp.wait_send()
+    fwd.wait_send()
+    for i, p in enumerate(me.exp_peers):
+        me.send(o_s.at[p], attn_recv.at[e], o_ss.at[i], o_rs.at[i]).wait_send()
+        me.send(snd.at[p], recv.at[p], d_ss.at[i], d_rs.at[i]).wait()
+    for w, (src, full) in enumerate(shards):
+        pltpu.make_async_copy(src, full.at[f], loc.at[2 + w]).wait()
+        x_send(w, 0, src, xf).wait()
+
+        @pl.when(z <= 2)
+        def _():
+            up_send(w, 0, src, f).wait_send()
+
+        @pl.when(z >= 1)
+        def _():
+            down_send(w, 0, src, f).wait_send()
+
+        for p in (1, 2, 3):
+
+            @pl.when(z >= p)
+            def _():
+                slot = f - 2 * p
+                if p <= 2:
+
+                    @pl.when(z <= 2)
+                    def _():
+                        up_send(w, p, full.at[slot], slot).wait_send()
+
+                x_send(w, p, full.at[slot], xf - 2 * p).wait()
+
+            @pl.when(z + p <= 3)
+            def _():
+                slot = f + 2 * p
+                if p <= 2:
+
+                    @pl.when(z >= 1)
+                    def _():
+                        down_send(w, p, full.at[slot], slot).wait_send()
+
+                x_send(w, 3 + p, full.at[slot], xf + 2 * p).wait()
+
+
+def gates_of(logits, routes):
+    lane = lane_of(logits.shape)
+    chosen = (lane == routes[:, 0:1]) | (lane == routes[:, 1:2])
+    top = jnp.max(jnp.where(chosen, logits, NEG), axis=-1, keepdims=True)
+    weight = jnp.where(chosen, jnp.exp(logits - top), 0.0)
+    return weight / jnp.sum(weight, axis=-1, keepdims=True)
+
+
+def sds(shape, dtype):
+    return jax.ShapeDtypeStruct(shape, dtype)
+
+
+def vmem():
+    return pl.BlockSpec(memory_space=pltpu.VMEM)
+
+
+def anyspace():
+    return pl.BlockSpec(memory_space=pl.ANY)
+
+
+def call_ka(x, u, wq, wo, wg, wu, wd, gres, routes, routes_t, starts, gain_a, gain_f, router, proj, mix):
+    T, D = x.shape
+    C = D // 4
+    FF = wg.shape[1]
+    R = wo.shape[0]
+    dma = pltpu.SemaphoreType.DMA
+    return pl.pallas_call(
+        ka_kernel,
+        name="forward",
+        out_shape=(
+            sds((4, T, D), BF),
+            sds((4, T, C), BF), sds((4, T, C), BF), sds((4, T, C), BF), sds((4, T, C), BF),
+            sds((4, T, 8), F32),
+            sds((T, D), F32),
+            sds((T, 8), F32), sds((T, 4), F32),
+            sds((4, CAP, T), BF),
+            sds((4, 2, CAP, D), BF),
+            sds((D, D), BF),
+            sds((D, 3 * C), BF),
+            sds((8, R, FF), BF), sds((8, R, FF), BF), sds((8, FF // 8, D), BF),
+        ),
+        in_specs=[vmem(), vmem(), anyspace(), anyspace(), anyspace(), anyspace(), anyspace(), vmem(), vmem(), vmem(),
+                  pl.BlockSpec(memory_space=pltpu.SMEM)] + [vmem()] * 5,
+        out_specs=tuple([vmem()] * 13 + [anyspace()] * 3),
+        scratch_shapes=[
+            pltpu.VMEM((4, T, C), BF),
+            pltpu.VMEM((T, D), BF),
+            pltpu.VMEM((4, 2, CAP, D), BF),
+            pltpu.VMEM((T, 1), F32),
+            pltpu.VMEM((T, 1), F32),
+            pltpu.VMEM((T, C), F32),
+            pltpu.VMEM((T, 8), F32),
+            dma((7,)), dma((7,)), dma((7,)), dma((7,)),
+            dma((3,)), dma((3,)), dma((3,)), dma((3,)), dma((3,)), dma((3,)),
+            dma((3, 3)), dma((3, 3)), dma((3, 3)), dma((3, 3)), dma((3, 7)), dma((3, 7)),
+            dma((5,)),
+        ],
+        compiler_params=pltpu.CompilerParams(collective_id=0, has_side_effects=True, vmem_limit_bytes=56 << 20),
+    )(x, u, wq, wo, wg, wu, wd, gres, routes, routes_t, starts, gain_a, gain_f, router, proj, mix)
 
 
 def body(
@@ -429,6 +803,326 @@
     )
 
 
+def body_fast(
+    tokens,
+    gate_res,
+    routes,
+    piece_starts,
+    norm_attn,
+    norm_ffn,
+    w_query,
+    w_key,
+    w_value,
+    w_out,
+    router,
+    mixing,
+    const_proj,
+    const_vec,
+    w_gate,
+    w_up,
+    w_down,
+    cotangent,
+):
+    n_ffn = lax.axis_size("exp")
+    rows_dev = tokens.shape[1]
+    model_width = tokens.shape[2]
+    seq_length = rows_dev * n_ffn
+    score_scale = 1.0 / math.sqrt(HD)
+    inputs_f = tokens[0].astype(jnp.float32)
+    res_logits = gate_res[0]
+    route_ids = routes[0]
+    starts = piece_starts[0]
+    full_query, full_key, full_value, full_out = (
+        lax.all_gather(w_query, "fsdp", axis=0, tiled=True),
+        lax.all_gather(w_key, "fsdp", axis=0, tiled=True),
+        lax.all_gather(w_value, "fsdp", axis=0, tiled=True),
+        lax.all_gather(w_out, "fsdp", axis=0, tiled=True),
+    )
+    attn_in = rms_scale(inputs_f, norm_attn).astype(jnp.bfloat16)
+    query = jnp.dot(attn_in, full_query, preferred_element_type=jnp.float32).astype(jnp.bfloat16)
+    key = jnp.dot(attn_in, full_key, preferred_element_type=jnp.float32).astype(jnp.bfloat16)
+    value = jnp.dot(attn_in, full_value, preferred_element_type=jnp.float32).astype(jnp.bfloat16)
+    keys_all, values_all = (
+        lax.all_gather(key, "exp", axis=0, tiled=True),
+        lax.all_gather(value, "exp", axis=0, tiled=True),
+    )
+    query_heads = query.reshape(rows_dev, H, HD)
+    key_heads = keys_all.reshape(seq_length, H, HD)
+    value_heads = values_all.reshape(seq_length, H, HD)
+    query_pos = lax.axis_index("exp") * rows_dev + jnp.arange(rows_dev, dtype=jnp.int32)
+    query_ids = piece_ids(query_pos, starts, PIECE)
+    key_upper, query_lower = reach_bounds(query_pos, starts, PIECE)
+    block_list = jnp.arange(seq_length // KBLK, dtype=jnp.int32)
+
+    def score_block(block_index):
+        key_first = block_index * KBLK
+        key_block = lax.dynamic_slice_in_dim(key_heads, key_first, KBLK, 0)
+        value_block = lax.dynamic_slice_in_dim(value_heads, key_first, KBLK, 0)
+        key_pos = key_first + jnp.arange(KBLK, dtype=jnp.int32)
+        key_ids = piece_ids(key_pos, starts, PIECE)
+        scores = (
+            jnp.einsum("qhd,khd->hqk", query_heads, key_block, preferred_element_type=jnp.float32)
+            * score_scale
+        )
+        allowed = allowed_mask(query_pos, query_ids, key_pos, key_ids)[None]
+        return (scores, allowed, key_block, value_block)
+
+    def needed(block_index):
+        return block_index * KBLK <= key_upper
+
+    def lse_step(carry, block_index):
+
+        def lse_active(state):
+            run_max, run_sum = state
+            scores, allowed, _, _ = score_block(block_index)
+            scores = jnp.where(allowed, scores, NEG)
+            new_max = jnp.maximum(run_max, jnp.max(scores, axis=-1))
+            exp_terms = jnp.where(allowed, jnp.exp(scores - new_max[..., None]), 0.0)
+            return (new_max, run_sum * jnp.exp(run_max - new_max) + jnp.sum(exp_terms, axis=-1))
+
+        return (lax.cond(needed(block_index), lse_active, lambda state: state, carry), None)
+
+    start_carry = (jnp.full((H, rows_dev), NEG, jnp.float32), jnp.zeros((H, rows_dev), jnp.float32))
+    (run_max, run_sum), _ = lax.scan(lse_step, start_carry, block_list)
+    log_norm = run_max + jnp.log(run_sum)
+
+    def block_probs(scores, allowed):
+        return jnp.where(allowed, jnp.exp(scores - log_norm[..., None]), 0.0)
+
+    exp_index = lax.axis_index("exp")
+    wqkv = jnp.concatenate(
+        [lax.dynamic_slice_in_dim(w, exp_index * 192, 192, 1) for w in (w_query, w_key, w_value)], axis=1
+    )
+    ka_out = call_ka(
+        tokens[0], cotangent[0], wqkv, w_out, w_gate[0], w_up[0], w_down[0], res_logits, route_ids, route_ids.T,
+        piece_starts, norm_attn[None], norm_ffn[None], router, const_proj, mixing,
+    )
+    def block_probs(scores, allowed):
+        return jnp.where(allowed, jnp.exp(scores - log_norm[..., None]), 0.0)
+
+    o_heads, hidden, recv = ka_out[4], ka_out[6], ka_out[10]
+    full_gate = ka_out[13].reshape(model_width, -1)
+    full_up = ka_out[14].reshape(model_width, -1)
+    full_down = ka_out[15].reshape(-1, model_width)
+    attn_low = lax.all_to_all(o_heads, "exp", split_axis=0, concat_axis=2, tiled=True).reshape(rows_dev, model_width)
+    normed = rms_scale(hidden, norm_ffn)
+    destination = slot_dest(route_ids, n_ffn, CAP)
+    sources = jnp.arange(2 * rows_dev, dtype=jnp.int32) // 2
+    received = recv[:, 0]
+    slot_rows = received.reshape(n_ffn * CAP, model_width)
+    gate_pre = jnp.dot(slot_rows, full_gate, preferred_element_type=jnp.float32)
+    up_pre = jnp.dot(slot_rows, full_up, preferred_element_type=jnp.float32)
+    inner_act = swiglu_act(gate_pre, up_pre).astype(jnp.bfloat16)
+    expert_result = jnp.dot(inner_act, full_down, preferred_element_type=jnp.float32).astype(
+        jnp.bfloat16
+    )
+    returned = lax.all_to_all(
+        expert_result.reshape(n_ffn, CAP, model_width),
+        "exp",
+        split_axis=0,
+        concat_axis=0,
+        tiled=True,
+    )
+    returned_pad = jnp.concatenate(
+        [returned.reshape(n_ffn * CAP, model_width), jnp.zeros((1, model_width), jnp.bfloat16)],
+        axis=0,
+    )
+    expert_rows = returned_pad[destination].astype(jnp.float32).reshape(rows_dev, 2, model_width)
+
+    def mix_local(normed_in, logits_in, router_in, mixing_in, proj_in, vec_in, rows_in):
+        return local_mix(
+            normed_in, logits_in, router_in, mixing_in, proj_in, vec_in, rows_in, route_ids, n_ffn
+        )
+
+    moe_out, mix_pull = jax.vjp(
+        mix_local, normed, res_logits, router, mixing, const_proj, const_vec, expert_rows
+    )
+    layer_out = (hidden + moe_out).astype(jnp.bfloat16)
+    upstream = cotangent[0].astype(jnp.float32)
+    d_normed_local, d_res_logits, d_router, d_mixing, d_const_proj, d_const_vec, d_expert_rows = (
+        mix_pull(upstream)
+    )
+    d_received = recv[:, 1].reshape(n_ffn * CAP, model_width)
+    d_inner = jnp.einsum("rd,fd->rf", d_received, full_down, preferred_element_type=jnp.float32)
+    _, act_pull = jax.vjp(swiglu_act, gate_pre, up_pre)
+    d_gate_pre, d_up_pre = act_pull(d_inner)
+    d_gate_low = d_gate_pre.astype(jnp.bfloat16)
+    d_up_low = d_up_pre.astype(jnp.bfloat16)
+    grad_down_full = jnp.einsum(
+        "rf,rd->fd", inner_act, d_received, preferred_element_type=jnp.float32
+    )
+    grad_gate_full = jnp.einsum(
+        "rd,rf->df", slot_rows, d_gate_low, preferred_element_type=jnp.float32
+    )
+    grad_up_full = jnp.einsum("rd,rf->df", slot_rows, d_up_low, preferred_element_type=jnp.float32)
+    d_slot_rows = (
+        jnp.einsum("rf,df->rd", d_gate_low, full_gate, preferred_element_type=jnp.float32)
+        + jnp.einsum("rf,df->rd", d_up_low, full_up, preferred_element_type=jnp.float32)
+    ).astype(jnp.bfloat16)
+    d_sent = lax.all_to_all(
+        d_slot_rows.reshape(n_ffn, CAP, model_width), "exp", split_axis=0, concat_axis=0, tiled=True
+    )
+    d_sent_pad = jnp.concatenate(
+        [d_sent.reshape(n_ffn * CAP, model_width), jnp.zeros((1, model_width), jnp.bfloat16)],
+        axis=0,
+    )
+    d_normed_sent = jnp.sum(
+        d_sent_pad[destination].astype(jnp.float32).reshape(rows_dev, 2, model_width), axis=1
+    )
+    _, norm_ffn_pull = jax.vjp(rms_scale, hidden, norm_ffn)
+    d_hidden_part, d_norm_ffn = norm_ffn_pull(d_normed_local + d_normed_sent)
+    d_hidden = upstream + d_hidden_part
+    d_hidden_low = d_hidden.astype(jnp.bfloat16)
+    grad_out_full = jnp.einsum(
+        "td,te->de", attn_low, d_hidden_low, preferred_element_type=jnp.float32
+    )
+    d_attn = jnp.einsum(
+        "te,de->td", d_hidden_low, full_out, preferred_element_type=jnp.float32
+    ).astype(jnp.bfloat16)
+    d_attn_heads = d_attn.reshape(rows_dev, H, HD)
+    zero_block = jnp.zeros((KBLK, H, HD), jnp.float32)
+
+    def delta_terms(block_index):
+        scores, allowed, _, value_block = score_block(block_index)
+        probs = block_probs(scores, allowed)
+        d_probs = jnp.einsum(
+            "qhd,khd->hqk", d_attn_heads, value_block, preferred_element_type=jnp.float32
+        )
+        part = jnp.sum(probs * d_probs, axis=-1)
+        return (
+            part,
+            jnp.einsum(
+                "hqk,qhd->khd",
+                probs.astype(jnp.bfloat16),
+                d_attn_heads,
+                preferred_element_type=jnp.float32,
+            ),
+        )
+
+    def query_terms(block_index, row_delta):
+        scores, allowed, key_block, value_block = score_block(block_index)
+        probs = block_probs(scores, allowed)
+        d_probs = jnp.einsum(
+            "qhd,khd->hqk", d_attn_heads, value_block, preferred_element_type=jnp.float32
+        )
+        d_scores = (probs * (d_probs - row_delta[..., None])).astype(jnp.bfloat16)
+        part = (
+            jnp.einsum("hqk,khd->qhd", d_scores, key_block, preferred_element_type=jnp.float32)
+            * score_scale
+        )
+        return (
+            part,
+            jnp.einsum("hqk,qhd->khd", d_scores, query_heads, preferred_element_type=jnp.float32)
+            * score_scale,
+        )
+
+    def delta_step(total, block_index):
+
+        def delta_active(running):
+            part, grad_block = delta_terms(block_index)
+            return (running + part, grad_block)
+
+        return lax.cond(
+            needed(block_index), delta_active, lambda running: (running, zero_block), total
+        )
+
+    row_delta, grad_values = lax.scan(delta_step, jnp.zeros((H, rows_dev), jnp.float32), block_list)
+
+    def query_step(total, block_index):
+
+        def query_active(running):
+            part, grad_block = query_terms(block_index, row_delta)
+            return (running + part, grad_block)
+
+        return lax.cond(
+            needed(block_index), query_active, lambda running: (running, zero_block), total
+        )
+
+    d_query_sum, grad_keys = lax.scan(
+        query_step, jnp.zeros((rows_dev, H, HD), jnp.float32), block_list
+    )
+    grad_keys = grad_keys.reshape(seq_length, model_width)
+    grad_values = grad_values.reshape(seq_length, model_width)
+    d_key_sum, d_value_sum = (
+        lax.psum_scatter(
+            grad_keys.astype(jnp.bfloat16), "exp", scatter_dimension=0, tiled=True
+        ).astype(jnp.float32),
+        lax.psum_scatter(
+            grad_values.astype(jnp.bfloat16), "exp", scatter_dimension=0, tiled=True
+        ).astype(jnp.float32),
+    )
+    d_query_low = d_query_sum.reshape(rows_dev, model_width).astype(jnp.bfloat16)
+    d_key_low = d_key_sum.astype(jnp.bfloat16)
+    d_value_low = d_value_sum.astype(jnp.bfloat16)
+    d_attn_in = (
+        jnp.einsum("te,de->td", d_query_low, full_query, preferred_element_type=jnp.float32)
+        + jnp.einsum("te,de->td", d_key_low, full_key, preferred_element_type=jnp.float32)
+        + jnp.einsum("te,de->td", d_value_low, full_value, preferred_element_type=jnp.float32)
+    )
+    grad_query_full = jnp.einsum(
+        "td,te->de", attn_in, d_query_low, preferred_element_type=jnp.float32
+    )
+    grad_key_full = jnp.einsum("td,te->de", attn_in, d_key_low, preferred_element_type=jnp.float32)
+    grad_value_full = jnp.einsum(
+        "td,te->de", attn_in, d_value_low, preferred_element_type=jnp.float32
+    )
+    _, norm_attn_pull = jax.vjp(rms_scale, inputs_f, norm_attn)
+    d_inputs_part, d_norm_attn = norm_attn_pull(d_attn_in)
+    grad_tokens = (d_hidden + d_inputs_part).astype(jnp.bfloat16)
+    attn_shards = (
+        lax.psum_scatter(
+            grad_query_full.astype(jnp.bfloat16), "fsdp", scatter_dimension=0, tiled=True
+        ).astype(jnp.float32),
+        lax.psum_scatter(
+            grad_key_full.astype(jnp.bfloat16), "fsdp", scatter_dimension=0, tiled=True
+        ).astype(jnp.float32),
+        lax.psum_scatter(
+            grad_value_full.astype(jnp.bfloat16), "fsdp", scatter_dimension=0, tiled=True
+        ).astype(jnp.float32),
+        lax.psum_scatter(
+            grad_out_full.astype(jnp.bfloat16), "fsdp", scatter_dimension=0, tiled=True
+        ).astype(jnp.float32),
+    )
+    attn_shards = (
+        lax.psum(attn_shards[0].astype(jnp.bfloat16), "exp").astype(jnp.float32),
+        lax.psum(attn_shards[1].astype(jnp.bfloat16), "exp").astype(jnp.float32),
+        lax.psum(attn_shards[2].astype(jnp.bfloat16), "exp").astype(jnp.float32),
+        lax.psum(attn_shards[3].astype(jnp.bfloat16), "exp").astype(jnp.float32),
+    )
+    expert_shards = (
+        lax.psum_scatter(
+            grad_gate_full.astype(jnp.bfloat16), "fsdp", scatter_dimension=0, tiled=True
+        ).astype(jnp.float32),
+        lax.psum_scatter(
+            grad_up_full.astype(jnp.bfloat16), "fsdp", scatter_dimension=0, tiled=True
+        ).astype(jnp.float32),
+        lax.psum_scatter(
+            grad_down_full.astype(jnp.bfloat16), "fsdp", scatter_dimension=0, tiled=True
+        ).astype(jnp.float32),
+    )
+    small_sums = lax.psum(
+        (d_norm_attn, d_norm_ffn, d_router, d_mixing, d_const_proj, d_const_vec), ("exp", "fsdp")
+    )
+    return (
+        layer_out[None],
+        grad_tokens[None],
+        d_res_logits[None],
+        small_sums[0],
+        small_sums[1],
+        attn_shards[0],
+        attn_shards[1],
+        attn_shards[2],
+        attn_shards[3],
+        small_sums[2],
+        small_sums[3],
+        small_sums[4],
+        small_sums[5],
+        expert_shards[0][None],
+        expert_shards[1][None],
+        expert_shards[2][None],
+    )
+
+
 def solution(mesh):
     placed = (
         P("fsdp", "exp", None),
@@ -451,7 +1145,7 @@
         P("fsdp", "exp", None),
     )
     return jax.shard_map(
-        body,
+        body_fast if (mesh.shape['exp'], mesh.shape['fsdp']) == (4, 8) else body,
         mesh=mesh,
         in_specs=placed,
         out_specs=(

time: 1320 us -> 1170 us (0.89)
  waiting for transfers between devices: 815 us -> 501 us
  Pallas kernels: 0 us -> 171 us
  blocking collectives: 41.5 us -> 99.9 us
  matrix products: 223 us -> 189 us
  starting transfers between devices: 34.8 us -> 10.4 us
    all_gather x9 -> x6, waiting for transfers between devices: 248 us -> 0.09 us  [the longest x1 0.02 us: body_fast(): lax.all_gather(w_out, 'fsdp', axis=0, tiled=True)]
    pallas_call x0 -> x1, Pallas kernels: none -> 171 us  [call_ka(): pl.pallas_call(ka_kernel, name='forward', out_shape=(sds((4, T, D), BF),...]
    all_to_all x0 -> x1, blocking collectives: none -> 58.5 us  [body_fast(): lax.all_to_all(o_heads, 'exp', split_axis=0, concat_axis=2, tiled=True)]
    reduce_scatter x9, waiting for transfers between devices: 515 us -> 464 us  [the longest x1 75 us: body_fast(): lax.psum_scatter(grad_up_full.astype(jnp.bfloat16), 'fsdp', scatter_dimen...]
    dot_general x24 -> x20, matrix products: 101 us -> 66.6 us  [the longest x1 6.11 us: body_fast(): jnp.einsum('rf,rd->fd', inner_act, d_received, preferred_element_type=jnp...]
    all_to_all x4 -> x2, starting transfers between devices: 34.1 us -> 9.28 us  [the longest x1 4.99 us: body_fast(): lax.all_to_all(d_slot_rows.reshape(n_ffn, CAP, model_width), 'exp', split...]
    all_to_all x4 -> x2, waiting for transfers between devices: 13.7 us -> 0.49 us  [the longest x1 0.48 us: body_fast(): lax.all_to_all(expert_result.reshape(n_ffn, CAP, model_width), 'exp', spl...]
    convert_element_type x8 -> x6, local copies, waits for them, and re-layouts: 26.5 us -> 20.4 us  [the longest x1 4.96 us: body_fast(): d_sent_pad[destination].astype(jnp.float32)]
  transfers between devices with their start and end apart: 23 -> 18, of which waited for: 20 -> 10; matrix products, arithmetic and copies ran while one was open for 14% -> 17% of each run, Pallas kernels for 0% -> 15%
where the time goes in v1:
time: 1170 us; the launch traced here: 1150 us
  waiting for transfers between devices  501 us (43%)
  matrix products  189 us (16%)
  Pallas kernels  171 us (15%)
  local copies, waits for them, and re-layouts  102 us (9%)
  blocking collectives  99.9 us (9%)
  other arithmetic  48 us (4%)
  between operations  16.8 us (1%)
  loops' own time  15.4 us (1%)
    pallas_call x1, Pallas kernels, call_ka(): pl.pallas_call(ka_kernel, name='forward', out_shape=(sds((4, T, D), BF),...  171 us
    reduce_scatter x1, waiting for transfers between devices, body_fast(): lax.psum_scatter(grad_up_full.astype(jnp.bfloat16), 'fsdp', scatter_dimen...  75 us
    reduce_scatter x1, waiting for transfers between devices, body_fast(): lax.psum_scatter(grad_gate_full.astype(jnp.bfloat16), 'fsdp', scatter_dim...  75 us
    reduce_scatter x1, waiting for transfers between devices, body_fast(): lax.psum_scatter(grad_down_full.astype(jnp.bfloat16), 'fsdp', scatter_dim...  73.8 us
    reduce_scatter x1, waiting for transfers between devices, body_fast(): lax.psum_scatter(grad_query_full.astype(jnp.bfloat16), 'fsdp', scatter_di...  66.6 us
    reduce_scatter x1, waiting for transfers between devices, body_fast(): lax.psum_scatter(grad_key_full.astype(jnp.bfloat16), 'fsdp', scatter_dime...  66.3 us
    reduce_scatter x1, waiting for transfers between devices, body_fast(): lax.psum_scatter(grad_value_full.astype(jnp.bfloat16), 'fsdp', scatter_di...  66.2 us
    all_to_all x1, blocking collectives, body_fast(): lax.all_to_all(o_heads, 'exp', split_axis=0, concat_axis=2, tiled=True)  58.5 us
  transfers between devices with their start and end apart: 18, of which 10 were waited for; matrix products, arithmetic and copies ran while one was open for 17% of the time, Pallas kernels for 15%

profile of v1, /device:TPU:30, one launch (start us, length us, event | category | flops | bytes accessed | tf_op | source)
XLA Modules:
  0.0 1152.9 jit_solution(14300931077951038714)
XLA Ops:
  21.3 170.5 %forward.1 = (bf16[4,512,768]{2,1,0:T(8,128)(2,1)}, bf16[4,512,192]{2,1,0:T(8,128)(2,1)}, bf16[4,512,192]{2,1,0:T(8,128)(2,1)}, bf16[4,512,192]{2,1,0:T(8,128)(2...) custom-call(bf16[512,768]{1,0:T(8,128)(2,1)} %bitcast.257, ...), custom_call_target="tpu_custom_call" | custom-call | tf_op jit(solution)/shard_map/forward/pallas_call | solution.py:428
  308.7 28.2 %while.45 = (s32[]{:T(128)}, f32[12,512]{1,0:T(8,128)S(1)}, f32[12,512]{1,0:T(8,128)S(1)}, s32[4]{0:T(128)S(1)}, s32[]{:T(128)}, /*index=5*/s32[1,4]{1,0:T(1,128...) while((s32[]{:T(128)}, f32[12,512]{1,0:T(8,128)S(1)}, ...), condition=%wide.region_34.35_spmd.clone, body=%wide.region_28.34_spmd.clone.sunk | while | flops 428891136 | bytes 27868588 | solution.py:886
  343.8 56.9 %while.46 = (s32[]{:T(128)}, f32[12,512]{1,0:T(8,128)S(1)}, bf16[4,512,12,64]{1,3,2,0:T(8,128)(2,1)}, s32[4]{0:T(128)S(1)}, s32[]{:T(128)}, /*index=5*/s32[1,4]{...) while((s32[]{:T(128)}, f32[12,512]{1,0:T(8,128)S(1)}, ...), condition=%wide.region_40.41_spmd.clone, body=%wide.region_35.40_spmd.clone.sunk | while | flops 1237330944 | bytes 95329760 | solution.py:1029
  345.0 15.9 %conditional.10 = (f32[12,512]{1,0:T(8,128)S(1)}, bf16[1,512,12,64]{1,3,2,0:T(8,128)(2,1)S(1)}) conditional(s32[]{:T(128)} %convert_element_type.337, f32[12,512]{1,0:T(8,128)S(1)} %get-tuple-element.988, (s32[]{:T(128)}, s32[]{:T(128)}, s32[1,4]{1,0:T(1,128)S(1)}, s32[512]{0:T(512)S(1)}, bf16[2048,12,64]{0,2,1:T(8,128)(2,1)}, ...), branch_computations={%region_36.36_spmd, %region_37.39_spmd} | conditional | flops 1237330944 | bytes 93754568 | solution.py:1025
  363.2 15.9 %conditional.10 = (f32[12,512]{1,0:T(8,128)S(1)}, bf16[1,512,12,64]{1,3,2,0:T(8,128)(2,1)S(1)}) conditional(s32[]{:T(128)} %convert_element_type.337, f32[12,512]{1,0:T(8,128)S(1)} %get-tuple-element.988, (s32[]{:T(128)}, s32[]{:T(128)}, s32[1,4]{1,0:T(1,128)S(1)}, s32[512]{0:T(512)S(1)}, bf16[2048,12,64]{0,2,1:T(8,128)(2,1)}, ...), branch_computations={%region_36.36_spmd, %region_37.39_spmd} | conditional | flops 1237330944 | bytes 93754568 | solution.py:1025
  381.4 15.9 %conditional.10 = (f32[12,512]{1,0:T(8,128)S(1)}, bf16[1,512,12,64]{1,3,2,0:T(8,128)(2,1)S(1)}) conditional(s32[]{:T(128)} %convert_element_type.337, f32[12,512]{1,0:T(8,128)S(1)} %get-tuple-element.988, (s32[]{:T(128)}, s32[]{:T(128)}, s32[1,4]{1,0:T(1,128)S(1)}, s32[512]{0:T(512)S(1)}, bf16[2048,12,64]{0,2,1:T(8,128)(2,1)}, ...), branch_computations={%region_36.36_spmd, %region_37.39_spmd} | conditional | flops 1237330944 | bytes 93754568 | solution.py:1025
  403.7 70.2 %while.47 = (s32[]{:T(128)}, f32[512,12,64]{0,2,1:T(8,128)S(1)}, bf16[4,512,12,64]{1,3,2,0:T(8,128)(2,1)}, s32[4]{0:T(128)S(1)}, s32[]{:T(128)}, /*index=5*/bf16...) while((s32[]{:T(128)}, f32[512,12,64]{0,2,1:T(8,128)S(1)}, ...), condition=%wide.region_45.46_spmd.clone, body=%wide.region_41.45_spmd.clone.sunk | while | flops 1632119808 | bytes 58007028 | solution.py:1041
  405.2 20.3 %conditional.11 = (f32[512,12,64]{0,2,1:T(8,128)S(1)}, bf16[1,512,12,64]{1,3,2,0:T(8,128)(2,1)S(1)}) conditional(s32[]{:T(128)} %convert_element_type.338, f32[512,12,64]{0,2,1:T(8,128)S(1)} %get-tuple-element.1034, (s32[]{:T(128)}, bf16[2048,12,64]{0,2,1:T(8,128)(2,1)}, s32[]{:T(128)}, s32[1,4]{1,0:T(1,128)S(1)}, s32[512]{0:T(512)S(1)}, ...), branch_computations={%region_42.42_spmd, %region_43.44_spmd} | conditional | flops 1632119808 | bytes 56431820 | solution.py:1037
  405.8 7.6 fusion.28
  427.7 20.3 %conditional.11 = (f32[512,12,64]{0,2,1:T(8,128)S(1)}, bf16[1,512,12,64]{1,3,2,0:T(8,128)(2,1)S(1)}) conditional(s32[]{:T(128)} %convert_element_type.338, f32[512,12,64]{0,2,1:T(8,128)S(1)} %get-tuple-element.1034, (s32[]{:T(128)}, bf16[2048,12,64]{0,2,1:T(8,128)(2,1)}, s32[]{:T(128)}, s32[1,4]{1,0:T(1,128)S(1)}, s32[512]{0:T(512)S(1)}, ...), branch_computations={%region_42.42_spmd, %region_43.44_spmd} | conditional | flops 1632119808 | bytes 56431820 | solution.py:1037
  428.4 7.6 fusion.28
  450.3 20.3 %conditional.11 = (f32[512,12,64]{0,2,1:T(8,128)S(1)}, bf16[1,512,12,64]{1,3,2,0:T(8,128)(2,1)S(1)}) conditional(s32[]{:T(128)} %convert_element_type.338, f32[512,12,64]{0,2,1:T(8,128)S(1)} %get-tuple-element.1034, (s32[]{:T(128)}, bf16[2048,12,64]{0,2,1:T(8,128)(2,1)}, s32[]{:T(128)}, s32[1,4]{1,0:T(1,128)S(1)}, s32[512]{0:T(512)S(1)}, ...), branch_computations={%region_42.42_spmd, %region_43.44_spmd} | conditional | flops 1632119808 | bytes 56431820 | solution.py:1037
  451.0 7.6 fusion.28
  510.7 58.5 %all_to_all.25 = bf16[4,512,192]{1,2,0:T(8,128)(2,1)S(1)} all-to-all(bf16[4,512,192]{1,2,0:T(8,128)(2,1)} %copy.121), channel_id=1, replica_groups=mesh['exp'=4,'fsdp'=8] {'exp'}, dimensions={0} | all-to-all | bytes 1572864 | tf_op jit(solution)/shard_map/all_to_all | solution.py:907
  581.7 24.9 %reduce-scatter.12.cloned.1.call-done = bf16[512,768]{0,1:T(8,128)(2,1)} async-done(((bf16[2048,768]{0,1:T(8,128)(2,1)}), bf16[512,768]{0,1:T(8,128)(2,1)}) %reduce-scatter.12.cloned.1.call-update) | async-done | bytes 786448 | tf_op jit(solution)/shard_map/reduce_scatter | solution.py:1050
  609.8 73.8 %reduce-scatter.26.cloned.1.call-done = bf16[256,768]{1,0:T(8,128)(2,1)} async-done(((bf16[2048,768]{1,0:T(8,128)(2,1)}), bf16[256,768]{1,0:T(8,128)(2,1)}) %reduce-scatter.26.cloned.1.call-update) | async-done | bytes 393232 | tf_op jit(solution)/shard_map/reduce_scatter | solution.py:1099
  685.5 75.0 %reduce-scatter.22.cloned.1.call-done = bf16[96,2048]{1,0:T(8,128)(2,1)} async-done(((bf16[768,2048]{1,0:T(8,128)(2,1)}), bf16[96,2048]{1,0:T(8,128)(2,1)}) %reduce-scatter.22.cloned.1.call-update) | async-done | bytes 393232 | tf_op jit(solution)/shard_map/reduce_scatter | solution.py:1093
  762.5 75.0 %reduce-scatter.24.cloned.1.call-done = bf16[96,2048]{1,0:T(8,128)(2,1)} async-done(((bf16[768,2048]{1,0:T(8,128)(2,1)}), bf16[96,2048]{1,0:T(8,128)(2,1)}) %reduce-scatter.24.cloned.1.call-update) | async-done | bytes 393232 | tf_op jit(solution)/shard_map/reduce_scatter | solution.py:1096
  845.5 41.4 %all-reduce.12 = (f32[768]{0:T(1024)}, f32[768]{0:T(1024)}, f32[768,8]{0,1:T(8,128)}, f32[8,8]{0,1:T(8,128)S(1)}, f32[768,4]{0,1:T(4,128)}, /*index=5*/f32[2,768]{1,0:T(2,128)}) all-reduce(f32[768]{0:T(1024)S(1)} %get-tuple-element.532, f32[768]{0:T(1024)S(1)} %copy-done.52, ...), channel_id=1, replica_groups=mesh['exp'=4,'fsdp'=8] {'exp','fsdp'}, use_global_device_ids=true, to_apply=%region_50.51 | all-reduce | flops 12352 | bytes 98816 | tf_op jit(solution)/shard_map/psum | solution.py:1103
  887.6 16.5 %reduce-scatter.20.cloned.1.call-done = bf16[96,768]{1,0:T(8,128)(2,1)} async-done(((bf16[768,768]{1,0:T(8,128)(2,1)}), bf16[96,768]{1,0:T(8,128)(2,1)}) %reduce-scatter.20.cloned.1.call-update) | async-done | bytes 147472 | tf_op jit(solution)/shard_map/reduce_scatter | solution.py:1082
  904.0 66.6 %reduce-scatter.14.cloned.1.call-done = bf16[96,768]{1,0:T(8,128)(2,1)} async-done(((bf16[768,768]{1,0:T(8,128)(2,1)}), bf16[96,768]{1,0:T(8,128)(2,1)}) %reduce-scatter.14.cloned.1.call-update) | async-done | bytes 147472 | tf_op jit(solution)/shard_map/reduce_scatter | solution.py:1073
  970.6 66.3 %reduce-scatter.16.cloned.1.call-done = bf16[96,768]{1,0:T(8,128)(2,1)} async-done(((bf16[768,768]{1,0:T(8,128)(2,1)}), bf16[96,768]{1,0:T(8,128)(2,1)}) %reduce-scatter.16.cloned.1.call-update) | async-done | bytes 147472 | tf_op jit(solution)/shard_map/reduce_scatter | solution.py:1076
  1036.9 66.2 %reduce-scatter.18.cloned.1.call-done = bf16[96,768]{1,0:T(8,128)(2,1)} async-done(((bf16[768,768]{1,0:T(8,128)(2,1)}), bf16[96,768]{1,0:T(8,128)(2,1)}) %reduce-scatter.18.cloned.1.call-update) | async-done | bytes 147472 | tf_op jit(solution)/shard_map/reduce_scatter | solution.py:1079
  1105.9 33.5 %all-reduce.16.cloned.1.call-done = (bf16[96,768]{1,0:T(8,128)(2,1)}, bf16[96,768]{1,0:T(8,128)(2,1)}, bf16[96,768]{1,0:T(8,128)(2,1)}, bf16[96,768]{1,0:T(8,128)(2,1)}) async-done(((bf16[96,768]{1,0:T(8,128)(2,1)}, bf16[96,768]{1,0:T(8,128)(2,1)}, bf16[96,768]{1,0:T(8,128)(2,1)}, bf16[96,768]{1,0:T(8,128)(2,1)}), (bf16[96,768]{1,0:T(8,128)(2,1)}, bf16[96,768]{1,0:T(8,128)(2,1)}, bf16[96,768]{1,0:T(8,128)(2,1)}, ...) | async-done | bytes 589840 | tf_op jit(solution)/shard_map/psum | solution.py:1087
  (452 shorter events, 352.6 us)
Async XLA Ops:
  7.2 214.8 %all-gather.7.cloned.1.call-start = ((), (), s32[]{:S(2)}) async-start(), calls=%async_computation.12 | async-start | bytes 1327104 | tf_op jit(solution)/shard_map/all_gather | solution.py:837
  7.9 260.1 %all-gather.13.cloned.1.call-start = ((), (), s32[]{:S(2)}) async-start(), calls=%async_computation.15 | async-start | bytes 1327104 | tf_op jit(solution)/shard_map/all_gather | solution.py:838
  8.7 287.8 %all-gather.11.cloned.1.call-start = ((), (), s32[]{:S(2)}) async-start(), calls=%async_computation.14 | async-start | bytes 1327104 | tf_op jit(solution)/shard_map/all_gather | solution.py:836
  210.5 29.7 %all-to-all-start.1 = ((bf16[4,160,768]{2,1,0:T(8,128)(2,1)}), bf16[4,160,768]{2,1,0:T(8,128)(2,1)S(1)}, u32[]{:S(2)}, u32[]{:S(2)}) async-start(bf16[4,160,768]{2,1,0:T(8,128)(2,1)} %bitcast.49), calls=%async_computation.1 | async-start | bytes 1966080 | tf_op jit(solution)/shard_map/all_to_all | solution.py:962
  215.5 85.6 %all-gather.17.cloned.1.call-start = ((), (), s32[]{:S(2)}) async-start(), calls=%async_computation.17 | async-start | bytes 1327104 | tf_op jit(solution)/shard_map/all_gather | solution.py:839
  216.1 87.9 %all-gather.9.cloned.1.call-start = ((), (), s32[]{:S(2)}) async-start(), calls=%async_computation.13 | async-start | bytes 3932160 | tf_op jit(solution)/shard_map/all_gather | solution.py:846
  219.8 74.5 %copy-start.31 = (f32[512]{0:T(512)}, f32[512]{0:T(512)S(1)}, u32[]{:S(2)}) copy-start(f32[512]{0:T(512)S(1)} %fusion.88) | copy-start | bytes 6148
  221.9 74.5 %copy-start.44 = (f32[512]{0:T(512)}, f32[512]{0:T(512)S(1)}, u32[]{:S(2)}) copy-start(f32[512]{0:T(512)S(1)} %fusion.89) | copy-start | bytes 6148
  240.2 16.5 %all-to-all-start = ((bf16[4,160,768]{2,1,0:T(8,128)(2,1)}), bf16[4,160,768]{2,1,0:T(8,128)(2,1)}, u32[]{:S(2)}, u32[]{:S(2)}) async-start(bf16[4,160,768]{2,1,0:T(8,128)(2,1)} %bitcast.263), calls=%async_computation | async-start | bytes 1966080 | tf_op jit(solution)/shard_map/all_to_all | solution.py:919
  244.5 92.4 %all-gather.15.cloned.1.call-start = ((), (), s32[]{:S(2)}) async-start(), calls=%async_computation.16 | async-start | bytes 3932160 | tf_op jit(solution)/shard_map/all_gather | solution.py:847
  271.3 303.2 %reduce-scatter.10.cloned.1.call-start = ((), (), s32[]{:S(2)}) async-start(), calls=%async_computation.18 | async-start | bytes 3932160 | tf_op jit(solution)/shard_map/reduce_scatter | solution.py:1047
  481.0 125.6 %reduce-scatter.12.cloned.1.call-start = ((), (), s32[]{:S(2)}) async-start(), calls=%async_computation.19 | async-start | bytes 3932160 | tf_op jit(solution)/shard_map/reduce_scatter | solution.py:1050
  488.3 195.3 %reduce-scatter.26.cloned.1.call-start = ((), (), s32[]{:S(2)}) async-start(), calls=%async_computation.26 | async-start | bytes 3538944 | tf_op jit(solution)/shard_map/reduce_scatter | solution.py:1099
  495.6 264.9 %reduce-scatter.22.cloned.1.call-start = ((), (), s32[]{:S(2)}) async-start(), calls=%async_computation.24 | async-start | bytes 3538944 | tf_op jit(solution)/shard_map/reduce_scatter | solution.py:1093
  502.5 334.9 %reduce-scatter.24.cloned.1.call-start = ((), (), s32[]{:S(2)}) async-start(), calls=%async_computation.25 | async-start | bytes 3538944 | tf_op jit(solution)/shard_map/reduce_scatter | solution.py:1096
  508.4 395.7 %reduce-scatter.20.cloned.1.call-start = ((), (), s32[]{:S(2)}) async-start(), calls=%async_computation.23 | async-start | bytes 1327104 | tf_op jit(solution)/shard_map/reduce_scatter | solution.py:1082
  508.4 60.8 %copy-start.4 = (f32[512,768]{1,0:T(8,128)S(1)}, f32[512,768]{1,0:T(8,128)}, u32[]{:S(2)}) copy-start(f32[512,768]{1,0:T(8,128)} %get-tuple-element.665) | copy-start | bytes 4718596
  571.1 399.5 %reduce-scatter.14.cloned.1.call-start = ((), (), s32[]{:S(2)}) async-start(), calls=%async_computation.20 | async-start | bytes 1327104 | tf_op jit(solution)/shard_map/reduce_scatter | solution.py:1073
  574.4 462.5 %reduce-scatter.16.cloned.1.call-start = ((), (), s32[]{:S(2)}) async-start(), calls=%async_computation.21 | async-start | bytes 1327104 | tf_op jit(solution)/shard_map/reduce_scatter | solution.py:1076
  578.2 525.0 %reduce-scatter.18.cloned.1.call-start = ((), (), s32[]{:S(2)}) async-start(), calls=%async_computation.22 | async-start | bytes 1327104 | tf_op jit(solution)/shard_map/reduce_scatter | solution.py:1079
  609.7 229.6 %copy-start.22 = (bf16[512,12,64]{0,2,1:T(8,128)(2,1)S(1)}, bf16[512,12,64]{0,2,1:T(8,128)(2,1)}, u32[]{:S(2)}) copy-start(bf16[512,12,64]{0,2,1:T(8,128)(2,1)} %copy-done.21) | copy-start | bytes 2359300
  609.8 529.6 %all-reduce.16.cloned.1.call-start = ((), (), s32[]{:S(2)}) async-start(), calls=%async_computation.27 | async-start | bytes 1179648 | tf_op jit(solution)/shard_map/psum | solution.py:1087
  843.1 44.4 %copy-start.43 = (f32[512]{0:T(512)S(1)}, f32[512]{0:T(512)}, u32[]{:S(2)}) copy-start(f32[512]{0:T(512)} %copy-done.42) | copy-start | bytes 6148
  843.1 260.0 %copy-start.5 = (f32[512,768]{1,0:T(8,128)S(1)}, f32[512,768]{1,0:T(8,128)}, u32[]{:S(2)}) copy-start(f32[512,768]{1,0:T(8,128)} %get-tuple-element.665) | copy-start | bytes 4718596
  (66 other events, 291.2 us)
Sparse Core Ops, SparseCore 0:
  10.2 49.3 all-gather.6
  61.8 49.4 all-gather.12
  113.4 47.8 all-gather.10
  218.2 39.8 all-gather.16
  260.1 28.5 all-gather.8
  290.7 28.5 all-gather.14
  481.1 82.8 reduce-scatter.9
  566.7 39.8 reduce-scatter.11
  610.2 73.3 reduce-scatter.25
  687.0 73.4 reduce-scatter.21
  764.1 73.2 reduce-scatter.23
  840.7 63.3 reduce-scatter.19
  907.4 63.1 reduce-scatter.13
  973.9 63.0 reduce-scatter.15
  1040.2 62.9 reduce-scatter.17
  1105.6 33.7 all-reduce.15

commit v2 on v0

--- a/solution.py
+++ b/solution.py
@@ -1,8 +1,9 @@
-import math
-
-import jax
-import jax.numpy as jnp
+import functools, math
+import jax, jax.numpy as jnp
 from jax import lax
+from jax.experimental import pallas as pl
+from jax.experimental.pallas import tpu as pltpu
+
 from jax.sharding import PartitionSpec as P
 
 H = 12
@@ -429,6 +430,918 @@
     )
 
 
+MESH = pl.DeviceIdType.MESH
+BF = jnp.bfloat16
+F32 = jnp.float32
+LOG2E = 1.4426950408889634
+QSCALE = LOG2E / math.sqrt(HD)
+
+
+class Place:
+    def __init__(self):
+        self.e = lax.axis_index("exp")
+        self.f = lax.axis_index("fsdp")
+        self.z = self.f // 2
+        self.x = self.f % 2
+        self.sib = self.e + 1 - 2 * (self.e % 2)
+        self.yp = (self.e + 2) % 4
+        self.diag = (self.sib + 2) % 4
+        self.xf = self.f + 1 - 2 * self.x
+        self.exp_peers = (self.sib, self.yp, self.diag)
+
+    def zf(self, d):
+        return ((self.z + d) % 4) * 2 + self.x
+
+    def barrier(self):
+        sem = pltpu.get_barrier_semaphore()
+        for p in self.exp_peers:
+            pl.semaphore_signal(sem, inc=1, device_id=(p, self.f), device_id_type=MESH)
+        for d in (1, 2, 3):
+            pl.semaphore_signal(sem, inc=1, device_id=(self.e, self.zf(d)), device_id_type=MESH)
+        pl.semaphore_signal(sem, inc=1, device_id=(self.e, self.xf), device_id_type=MESH)
+        pl.semaphore_wait(sem, 7)
+
+    def send(self, src, dst, ss, rs, e=None, f=None):
+        return pltpu.make_async_remote_copy(
+            src_ref=src,
+            dst_ref=dst,
+            send_sem=ss,
+            recv_sem=rs,
+            device_id=(self.e if e is None else e, self.f if f is None else f),
+            device_id_type=MESH,
+        )
+
+
+def lane_of(shape):
+    return lax.broadcasted_iota(jnp.int32, shape, len(shape) - 1)
+
+
+def ka_kernel(
+    x_ref, u_ref, wq_ref, wo_ref, wg_ref, wu_ref, wd_ref, gres_ref, routes_ref, routes_t_ref, starts_ref,
+    gain_a_ref, gain_f_ref, router_ref, proj_ref, mix_ref,
+    attn_all, q_s, k_s, v_s, o_s, lse_s, hidden_ref, logit_ref, pair_ref, place_ref, recv, wo_full, wq_full,
+    gate_full, up_full, down_full,
+    attn_recv, nb, snd, m_s, l_s, acc_s, gsel,
+    wq_ss, wq_rs, wo_ss, wo_rs, at_ss, at_rs, o_ss, o_rs, d_ss, d_rs,
+    us, ur, ds, dr, xs, xr, loc,
+):
+    me = Place()
+    e, f, z, xf = me.e, me.f, me.z, me.xf
+    T, D = x_ref.shape
+    C = D // 4
+    R = wo_ref.shape[0]
+    me.barrier()
+
+    def rows(ref, index):
+        return ref.at[pl.ds(pl.multiple_of(index * R, 32), R)]
+
+    early = ((wq_ref, wq_full, wq_ss, wq_rs, 0), (wo_ref, wo_full, wo_ss, wo_rs, 1))
+    for src, dst, ss, rs, li in early:
+        for d in (1, 3, 2):
+            me.send(src, rows(dst, f), ss.at[d], rs.at[d], f=me.zf(d)).start()
+        me.send(src, rows(dst, f), ss.at[0], rs.at[0], f=xf).start()
+        pltpu.make_async_copy(src, rows(dst, f), loc.at[li]).start()
+
+    xv = x_ref[...].astype(F32)
+    inv = lax.rsqrt(jnp.mean(xv * xv, axis=-1, keepdims=True) + EPS)
+    attn_all[e] = (xv * inv * gain_a_ref[...]).astype(BF)
+    to_sib = me.send(attn_all.at[e], attn_all.at[e], at_ss.at[0], at_rs.at[0], e=me.sib)
+    to_yp = me.send(attn_all.at[e], attn_all.at[e], at_ss.at[1], at_rs.at[1], e=me.yp)
+    to_yp.start()
+    to_sib.start()
+
+    def early_in(dst, ss, rs, d):
+        return me.send(rows(dst, f), rows(dst, ((z - d + 4) % 4) * 2 + me.x), ss.at[d], rs.at[d])
+
+    def early_fwd(dst, ss, rs, d):
+        slot = rows(dst, ((z - d + 4) % 4) * 2 + me.x)
+        return me.send(slot, slot, ss.at[3 + d], rs.at[3 + d], f=xf)
+
+    for src, dst, ss, rs, li in early:
+        for d in (1, 3, 2):
+            early_in(dst, ss, rs, d).wait_recv()
+            early_fwd(dst, ss, rs, d).start()
+
+    shards = ((wg_ref, gate_full), (wu_ref, up_full), (wd_ref, down_full))
+
+    def up_send(w, p, src, slot):
+        full = shards[w][1]
+        return me.send(src, full.at[slot], us.at[w, p], ur.at[w, p], f=f + 2)
+
+    def down_send(w, p, src, slot):
+        full = shards[w][1]
+        return me.send(src, full.at[slot], ds.at[w, p], dr.at[w, p], f=f - 2)
+
+    def x_send(w, i, src, slot):
+        full = shards[w][1]
+        return me.send(src, full.at[slot], xs.at[w, i], xr.at[w, i], f=xf)
+
+    def experts(p):
+        for w, (src, full) in enumerate(shards):
+            if p == 0:
+                x_send(w, 0, src, f).start()
+
+                @pl.when(z <= 2)
+                def _():
+                    up_send(w, 0, src, f).start()
+
+                @pl.when(z >= 1)
+                def _():
+                    down_send(w, 0, src, f).start()
+
+                pltpu.make_async_copy(src, full.at[f], loc.at[2 + w]).start()
+            else:
+
+                @pl.when(z >= p)
+                def _():
+                    slot = f - 2 * p
+                    up_send(w, p - 1, full.at[slot], slot).wait_recv()
+                    if p <= 2:
+
+                        @pl.when(z <= 2)
+                        def _():
+                            up_send(w, p, full.at[slot], slot).start()
+
+                    x_send(w, p, full.at[slot], slot).start()
+
+                @pl.when(z + p <= 3)
+                def _():
+                    slot = f + 2 * p
+                    down_send(w, p - 1, full.at[slot], slot).wait_recv()
+                    if p <= 2:
+
+                        @pl.when(z >= 1)
+                        def _():
+                            down_send(w, p, full.at[slot], slot).start()
+
+                    x_send(w, 3 + p, full.at[slot], slot).start()
+
+    experts(0)
+
+    me.send(attn_all.at[me.yp], attn_all.at[me.yp], at_ss.at[1], at_rs.at[1]).wait_recv()
+    fwd = me.send(attn_all.at[me.yp], attn_all.at[me.yp], at_ss.at[2], at_rs.at[2], e=me.sib)
+    fwd.start()
+    me.send(attn_all.at[me.sib], attn_all.at[me.sib], at_ss.at[0], at_rs.at[0]).wait_recv()
+    me.send(attn_all.at[me.diag], attn_all.at[me.diag], at_ss.at[2], at_rs.at[2]).wait_recv()
+
+    def early_wait(src, dst, ss, rs, li):
+        pltpu.make_async_copy(src, rows(dst, f), loc.at[li]).wait()
+        me.send(rows(dst, xf), rows(dst, xf), ss.at[0], rs.at[0]).wait_recv()
+        for d in (1, 2, 3):
+            slot = rows(dst, ((z - d + 4) % 4) * 2 + 1 - me.x)
+            me.send(slot, slot, ss.at[3 + d], rs.at[3 + d]).wait_recv()
+
+    early_wait(*early[0])
+
+    def qkv_step(i, _):
+        b = i // 2
+        r = pl.ds(pl.multiple_of((i % 2) * 256, 256), 256)
+        out = jnp.dot(attn_all[b, r, :], wq_full[...], preferred_element_type=F32)
+        q_s[b, r, :] = (out[:, 0:C] * QSCALE).astype(BF)
+        k_s[b, r, :] = pltpu.roll(out[:, 128:384], 192, 1)[:, 0:C].astype(BF)
+        v_s[b, r, :] = out[:, 2 * C : 3 * C].astype(BF)
+        return 0
+
+    lax.fori_loop(0, 8, qkv_step, 0)
+    experts(1)
+
+    lse_s[...] = jnp.zeros_like(lse_s)
+    head_of = lane_of((T, C)) // HD
+
+    def head_step(i, _):
+        qb = i // 3
+        h = i % 3
+        qh = jnp.where(head_of == h, q_s[qb], jnp.zeros((T, C), BF))
+        s = lax.dot_general(qh, k_s[qb], (((1,), (1,)), ((), ())), preferred_element_type=F32)
+        col = lane_of((T, T))
+        row = lax.broadcasted_iota(jnp.int32, (T, T), 0)
+        first = starts_ref[0, qb] - qb * T
+        inside_c = (col >= first) & (col < first + PIECE)
+        inside_r = (row >= first) & (row < first + PIECE)
+        s = jnp.where((col <= row) | (inside_c & inside_r), s, NEG)
+        m = jnp.max(s, axis=-1, keepdims=True)
+        p = jnp.exp2(s - m)
+        m_s[...] = m
+        l_s[...] = jnp.sum(p, axis=-1, keepdims=True)
+        acc_s[...] = jnp.dot(p.astype(BF), v_s[qb], preferred_element_type=F32)
+
+        def kv_step(kb, _):
+            s = lax.dot_general(qh, k_s[kb], (((1,), (1,)), ((), ())), preferred_element_type=F32)
+            m_old = m_s[...]
+            m = jnp.maximum(m_old, jnp.max(s, axis=-1, keepdims=True))
+            scale = jnp.exp2(m_old - m)
+            p = jnp.exp2(s - m)
+            m_s[...] = m
+            l_s[...] = l_s[...] * scale + jnp.sum(p, axis=-1, keepdims=True)
+            acc_s[...] = acc_s[...] * scale + jnp.dot(p.astype(BF), v_s[kb], preferred_element_type=F32)
+            return 0
+
+        lax.fori_loop(0, qb, kv_step, 0)
+        total = l_s[...]
+        o_s[qb] = jnp.where(head_of == h, (acc_s[...] / total).astype(BF), o_s[qb])
+        lse = m_s[...] + jnp.log2(total)
+        lse_s[qb] = jnp.where(lane_of((T, 8)) == h, lse, lse_s[qb])
+        return 0
+
+    lax.fori_loop(0, 12, head_step, 0)
+
+    for i, p in enumerate(me.exp_peers):
+        me.send(o_s.at[p], attn_recv.at[e], o_ss.at[i], o_rs.at[i], e=p).start()
+    attn_recv[e] = o_s[e]
+    experts(2)
+
+    r0, r1 = routes_t_ref[0:1, :], routes_t_ref[1:2, :]
+    expert = lax.broadcasted_iota(jnp.int32, (8, T), 0)
+    has = (expert == r0) | (expert == r1)
+    earlier = (lax.broadcasted_iota(jnp.int32, (T, T), 0) < lane_of((T, T))).astype(BF)
+    count = jnp.dot(has.astype(BF), earlier, preferred_element_type=F32).astype(jnp.int32)
+    count = jnp.where(has, count, -1)
+    slot_id = lax.broadcasted_iota(jnp.int32, (CAP, T), 0)
+    for k in range(4):
+        place_ref[k] = jnp.where(slot_id == count[k : k + 1, :], 1.0, 0.0).astype(BF)
+
+    early_wait(*early[1])
+    for i, p in enumerate(me.exp_peers):
+        me.send(attn_recv.at[p], attn_recv.at[p], o_ss.at[i], o_rs.at[i]).wait_recv()
+
+    def hidden_step(i, _):
+        r = pl.ds(pl.multiple_of(i * 256, 256), 256)
+        h = x_ref[r, :].astype(F32)
+        for b in range(4):
+            h = h + jnp.dot(attn_recv[b, r, :], wo_full[b * C : (b + 1) * C, :], preferred_element_type=F32)
+        hidden_ref[r, :] = h
+        n = h * lax.rsqrt(jnp.mean(h * h, axis=-1, keepdims=True) + EPS) * gain_f_ref[...]
+        nb[r, :] = n.astype(BF)
+        logits = jnp.dot(n, router_ref[...], precision=HIGH, preferred_element_type=F32)
+        logits = logits + jnp.dot(gres_ref[r, :], mix_ref[...], precision=HIGH, preferred_element_type=F32)
+        logit_ref[r, :] = logits
+        pair_ref[r, :] = jnp.dot(n, proj_ref[...], precision=HIGH, preferred_element_type=F32)
+        gsel[r, :] = gates_of(logits, routes_ref[r, :])
+        return 0
+
+    lax.fori_loop(0, 2, hidden_step, 0)
+
+    def dispatch_step(k, _):
+        place = place_ref[k]
+        snd[k, 0] = jnp.dot(place, nb[...], preferred_element_type=F32).astype(BF)
+        gate = jnp.sum(jnp.where(lane_of((T, 8)) == k, gsel[...], 0.0), axis=-1, keepdims=True)
+        gu = (gate * u_ref[...].astype(F32)).astype(BF)
+        snd[k, 1] = jnp.dot(place, gu, preferred_element_type=F32).astype(BF)
+        return 0
+
+    lax.fori_loop(0, 4, dispatch_step, 0)
+    for i, p in enumerate(me.exp_peers):
+        me.send(snd.at[p], recv.at[e], d_ss.at[i], d_rs.at[i], e=p).start()
+    recv[e] = snd[e]
+    experts(3)
+
+    for src, dst, ss, rs, li in early:
+        for j in range(4):
+            me.send(src, rows(dst, f), ss.at[j], rs.at[j]).wait_send()
+        for d in (1, 2, 3):
+            early_fwd(dst, ss, rs, d).wait_send()
+    to_sib.wait_send()
+    to_yp.wait_send()
+    fwd.wait_send()
+    for i, p in enumerate(me.exp_peers):
+        me.send(o_s.at[p], attn_recv.at[e], o_ss.at[i], o_rs.at[i]).wait_send()
+        me.send(snd.at[p], recv.at[p], d_ss.at[i], d_rs.at[i]).wait()
+    for w, (src, full) in enumerate(shards):
+        pltpu.make_async_copy(src, full.at[f], loc.at[2 + w]).wait()
+        x_send(w, 0, src, xf).wait()
+
+        @pl.when(z <= 2)
+        def _():
+            up_send(w, 0, src, f).wait_send()
+
+        @pl.when(z >= 1)
+        def _():
+            down_send(w, 0, src, f).wait_send()
+
+        for p in (1, 2, 3):
+
+            @pl.when(z >= p)
+            def _():
+                slot = f - 2 * p
+                if p <= 2:
+
+                    @pl.when(z <= 2)
+                    def _():
+                        up_send(w, p, full.at[slot], slot).wait_send()
+
+                x_send(w, p, full.at[slot], xf - 2 * p).wait()
+
+            @pl.when(z + p <= 3)
+            def _():
+                slot = f + 2 * p
+                if p <= 2:
+
+                    @pl.when(z >= 1)
+                    def _():
+                        down_send(w, p, full.at[slot], slot).wait_send()
+
+                x_send(w, 3 + p, full.at[slot], xf + 2 * p).wait()
+
+
+def gates_of(logits, routes):
+    lane = lane_of(logits.shape)
+    chosen = (lane == routes[:, 0:1]) | (lane == routes[:, 1:2])
+    top = jnp.max(jnp.where(chosen, logits, NEG), axis=-1, keepdims=True)
+    weight = jnp.where(chosen, jnp.exp(logits - top), 0.0)
+    return weight / jnp.sum(weight, axis=-1, keepdims=True)
+
+
+def sds(shape, dtype):
+    return jax.ShapeDtypeStruct(shape, dtype)
+
+
+def vmem():
+    return pl.BlockSpec(memory_space=pltpu.VMEM)
+
+
+def anyspace():
+    return pl.BlockSpec(memory_space=pl.ANY)
+
+
+def call_ka(x, u, wq, wo, wg, wu, wd, gres, routes, routes_t, starts, gain_a, gain_f, router, proj, mix):
+    T, D = x.shape
+    C = D // 4
+    FF = wg.shape[1]
+    R = wo.shape[0]
+    dma = pltpu.SemaphoreType.DMA
+    return pl.pallas_call(
+        ka_kernel,
+        name="forward",
+        out_shape=(
+            sds((4, T, D), BF),
+            sds((4, T, C), BF), sds((4, T, C), BF), sds((4, T, C), BF), sds((4, T, C), BF),
+            sds((4, T, 8), F32),
+            sds((T, D), F32),
+            sds((T, 8), F32), sds((T, 4), F32),
+            sds((4, CAP, T), BF),
+            sds((4, 2, CAP, D), BF),
+            sds((D, D), BF),
+            sds((D, 3 * C), BF),
+            sds((8, R, FF), BF), sds((8, R, FF), BF), sds((8, FF // 8, D), BF),
+        ),
+        in_specs=[vmem(), vmem(), anyspace(), anyspace(), anyspace(), anyspace(), anyspace(), vmem(), vmem(), vmem(),
+                  pl.BlockSpec(memory_space=pltpu.SMEM)] + [vmem()] * 5,
+        out_specs=tuple([vmem()] * 13 + [anyspace()] * 3),
+        scratch_shapes=[
+            pltpu.VMEM((4, T, C), BF),
+            pltpu.VMEM((T, D), BF),
+            pltpu.VMEM((4, 2, CAP, D), BF),
+            pltpu.VMEM((T, 1), F32),
+            pltpu.VMEM((T, 1), F32),
+            pltpu.VMEM((T, C), F32),
+            pltpu.VMEM((T, 8), F32),
+            dma((7,)), dma((7,)), dma((7,)), dma((7,)),
+            dma((3,)), dma((3,)), dma((3,)), dma((3,)), dma((3,)), dma((3,)),
+            dma((3, 3)), dma((3, 3)), dma((3, 3)), dma((3, 3)), dma((3, 7)), dma((3, 7)),
+            dma((5,)),
+        ],
+        compiler_params=pltpu.CompilerParams(collective_id=0, has_side_effects=True, vmem_limit_bytes=56 << 20),
+    )(x, u, wq, wo, wg, wu, wd, gres, routes, routes_t, starts, gain_a, gain_f, router, proj, mix)
+
+
+def dot(a, b, ca=1, cb=0):
+    return lax.dot_general(a, b, (((ca,), (cb,)), ((), ())), preferred_element_type=F32)
+
+
+def kf_kernel(
+    recv, gate_hbm, up_hbm, down_hbm,
+    ret, grad_gate, grad_up, grad_down,
+    gate, up, down, gate_pre, up_pre, inner, d_gate, d_up, rows, d_rows_in, acc, out, d_out,
+    e_ss, e_rs, r_ss, r_rs, loc,
+):
+    me = Place()
+    e, f = me.e, me.f
+    n, _, cap, D = recv.shape
+    S = n * cap
+    chunks = down.shape[0]
+    W = down.shape[1]
+    loads = []
+    for i, (src, dst) in enumerate(((gate_hbm, gate), (up_hbm, up), (down_hbm, down))):
+        loads.append(pltpu.make_async_copy(src, dst, loc.at[i]))
+        loads[-1].start()
+    sem = pltpu.get_barrier_semaphore()
+    for p in me.exp_peers:
+        pl.semaphore_signal(sem, inc=1, device_id=(p, f), device_id_type=MESH)
+    pl.semaphore_wait(sem, 3)
+    for k in range(n):
+        rows[k * cap : (k + 1) * cap, :] = recv[k, 0]
+        d_rows_in[k * cap : (k + 1) * cap, :] = recv[k, 1]
+    acc[...] = jnp.zeros_like(acc)
+    for load in loads:
+        load.wait()
+
+    def cols(ref, c):
+        return ref[:, :, pl.ds(pl.multiple_of(c * W, 256), W)].reshape(D, W)
+
+    def forward_step(c, _):
+        g = dot(rows[...], cols(gate, c))
+        u = dot(rows[...], cols(up, c))
+        gate_pre[c] = g
+        up_pre[c] = u
+        v = (g / (1.0 + jnp.exp(-g)) * u).astype(BF)
+        inner[c] = v
+        acc[...] += dot(v, down[c])
+        return 0
+
+    lax.fori_loop(0, chunks, forward_step, 0)
+    for k in range(n):
+        out[k] = acc[k * cap : (k + 1) * cap, :].astype(BF)
+    for i, p in enumerate(me.exp_peers):
+        me.send(out.at[p], ret.at[e, 0], e_ss.at[i], e_rs.at[i], e=p).start()
+    ret[e, 0] = out[e]
+    acc[...] = jnp.zeros_like(acc)
+
+    def backward_step(c, _):
+        d_inner = dot(d_rows_in[...], down[c], 1, 1)
+        g = gate_pre[c]
+        sig = 1.0 / (1.0 + jnp.exp(-g))
+        silu = g * sig
+        du = (d_inner * silu).astype(BF)
+        dg = (d_inner * up_pre[c] * (sig + silu * (1.0 - sig))).astype(BF)
+        d_up[c] = du
+        d_gate[c] = dg
+        acc[...] += dot(dg, cols(gate, c), 1, 1) + dot(du, cols(up, c), 1, 1)
+        return 0
+
+    lax.fori_loop(0, chunks, backward_step, 0)
+    for k in range(n):
+        d_out[k] = acc[k * cap : (k + 1) * cap, :].astype(BF)
+    for i, p in enumerate(me.exp_peers):
+        me.send(d_out.at[p], ret.at[e, 1], r_ss.at[i], r_rs.at[i], e=p).start()
+    ret[e, 1] = d_out[e]
+
+    def grad_step(c, _):
+        grad_down[c] = dot(inner[c], d_rows_in[...], 0, 0).astype(BF)
+        w = pl.ds(pl.multiple_of(c * W, 256), W)
+        grad_gate[:, :, w] = dot(rows[...], d_gate[c], 0, 0).astype(BF).reshape(chunks, D // chunks, W)
+        grad_up[:, :, w] = dot(rows[...], d_up[c], 0, 0).astype(BF).reshape(chunks, D // chunks, W)
+        return 0
+
+    lax.fori_loop(0, chunks, grad_step, 0)
+    for i, p in enumerate(me.exp_peers):
+        me.send(out.at[p], ret.at[p, 0], e_ss.at[i], e_rs.at[i]).wait()
+        me.send(d_out.at[p], ret.at[p, 1], r_ss.at[i], r_rs.at[i]).wait()
+
+
+def call_kf(recv, gate, up, down):
+    n, _, cap, D = recv.shape
+    S = n * cap
+    chunks, W, _ = down.shape
+    dma = pltpu.SemaphoreType.DMA
+    return pl.pallas_call(
+        kf_kernel,
+        name="experts",
+        out_shape=(sds(recv.shape, BF), sds(gate.shape, BF), sds(up.shape, BF), sds(down.shape, BF)),
+        in_specs=[vmem(), anyspace(), anyspace(), anyspace()],
+        out_specs=(vmem(), vmem(), vmem(), vmem()),
+        scratch_shapes=[
+            pltpu.VMEM(gate.shape, BF), pltpu.VMEM(up.shape, BF), pltpu.VMEM(down.shape, BF),
+            pltpu.VMEM((chunks, S, W), F32), pltpu.VMEM((chunks, S, W), F32),
+            pltpu.VMEM((chunks, S, W), BF), pltpu.VMEM((chunks, S, W), BF), pltpu.VMEM((chunks, S, W), BF),
+            pltpu.VMEM((S, D), BF), pltpu.VMEM((S, D), BF), pltpu.VMEM((S, D), F32),
+            pltpu.VMEM((n, cap, D), BF), pltpu.VMEM((n, cap, D), BF),
+            dma((3,)), dma((3,)), dma((3,)), dma((3,)), dma((3,)),
+        ],
+        compiler_params=pltpu.CompilerParams(collective_id=1, has_side_effects=True, vmem_limit_bytes=57 << 20),
+    )(recv, gate, up, down)
+
+
+LN2 = math.log(2.0)
+
+
+def kb_kernel(
+    ret, hidden, u_ref, x_ref, logit_ref, pair_ref, routes_ref, place_ref, gres_ref,
+    attn_all, q_s, k_s, v_s, o_s, lse_s, wo, wqkv, gain_a_ref, gain_f_ref, router_ref, proj_ref, mix_ref, cvec_ref, starts_ref,
+    g_gate, g_up, g_down,
+    layer_out, grad_tokens, d_res, small_out, ag_out, go_out, eg_out, eu_out, ed_out,
+    xin_g, xin_u, xin_d, own_g, own_u, own_d, zin_g, zin_u, zin_d,
+    dh_all, da, dq, dk, dv, dq_acc, pin, py_in, d_hidden, wk_s, lse_r, del_r, gt, ag_s, ag_in, ag_fin, go_s, go_in, go_b,
+    small, sm1, sm2,
+    xs, xr, zs, zr, own_sem, dh_ss, dh_rs, go_ss, go_rs, gb_ss, gb_rs, pd_ss, pd_rs, ag_ss, ag_rs, ab_ss, ab_rs, s1_ss, s1_rs, s2_ss, s2_rs,
+):
+    me = Place()
+    e, f, z, x, xf = me.e, me.f, me.z, me.x, me.xf
+    T, D = x_ref.shape
+    C = D // 4
+    R = D // 8
+
+    def fp(r):
+        return (f + r) % 8
+
+    sem = pltpu.get_barrier_semaphore()
+    for p in me.exp_peers:
+        pl.semaphore_signal(sem, inc=1, device_id=(p, f), device_id_type=MESH)
+    for r in range(1, 8):
+        pl.semaphore_signal(sem, inc=1, device_id=(e, fp(r)), device_id_type=MESH)
+    pl.semaphore_wait(sem, 10)
+
+    parts = ((g_gate, xin_g, own_g, zin_g), (g_up, xin_u, own_u, zin_u), (g_down, xin_d, own_d, zin_d))
+
+    def row_of(d):
+        return (z + d) % 4
+
+    def x_copy(w, d):
+        g, xin = parts[w][0], parts[w][1]
+        zz = row_of(d)
+        return me.send(g.at[2 * zz + 1 - x], xin.at[zz], xs.at[w, d], xr.at[w, d], f=xf)
+
+    def own_copy(w, d):
+        g, own = parts[w][0], parts[w][2]
+        return pltpu.make_async_copy(g.at[2 * row_of(d) + x], own, own_sem.at[w])
+
+    def z_copy(w, d):
+        xin, zin = parts[w][1], parts[w][3]
+        return me.send(xin.at[row_of(d)], zin.at[d - 1], zs.at[w, d - 1], zr.at[w, d - 1], f=me.zf(d))
+
+    def rs_send(d):
+        for w in range(3):
+            x_copy(w, d).start()
+
+    after = {2: 1, 1: 3, 3: 0}
+
+    def rs_mid(d, w):
+        xin, own = parts[w][1], parts[w][2]
+        x_copy(w, d).wait_recv()
+        own_copy(w, d).wait()
+        zz = row_of(d)
+        if d:
+            xin[zz] = (xin[zz].astype(F32) + own[...].astype(F32)).astype(BF)
+            z_copy(w, d).start()
+            own_copy(w, after[d]).start()
+
+    def rs_mid_all(d):
+        for w in range(3):
+            rs_mid(d, w)
+
+    for w in range(3):
+        own_copy(w, 2).start()
+    rs_send(2)
+    rs_send(1)
+
+    small[...] = jnp.zeros_like(small)
+    cv0, cv1 = cvec_ref[0:1, :], cvec_ref[1:2, :]
+    lane8 = lane_of((128, 8))
+
+    def pick(values, k):
+        return jnp.sum(jnp.where(lane_of(values.shape) == k, values, 0.0), axis=-1, keepdims=True)
+
+    def mix_step(i, _):
+        r = pl.ds(pl.multiple_of(i * 128, 128), 128)
+        h = hidden[r, :]
+        u = u_ref[r, :].astype(F32)
+        inv = lax.rsqrt(jnp.mean(h * h, axis=-1, keepdims=True) + EPS)
+        hn = h * inv
+        n = hn * gain_f_ref[...]
+        gates = gates_of(logit_ref[r, :], routes_ref[r, :])
+        pairs = pair_ref[r, :]
+        p0, p1, p2, p3 = pairs[:, 0:1], pairs[:, 1:2], pairs[:, 2:3], pairs[:, 3:4]
+        a0 = 1.0 / (1.0 + jnp.exp(p1 - p0))
+        b0 = 1.0 / (1.0 + jnp.exp(p0 - p1))
+        a1 = 1.0 / (1.0 + jnp.exp(p3 - p2))
+        b1 = 1.0 / (1.0 + jnp.exp(p2 - p3))
+        g5, g6, g7 = pick(gates, 5), pick(gates, 6), pick(gates, 7)
+        c_n = g5 + g6 * a0 + g7 * a1
+        c0 = g6 * b0
+        c1 = g7 * b1
+        mixed = h + c_n * n + c0 * cv0 + c1 * cv1
+        dg = jnp.zeros((128, 8), F32)
+        dn = c_n * u
+        for k in range(4):
+            place = place_ref[k, :, r]
+            rk = dot(place, ret[k, 0], 0, 0)
+            mixed = mixed + pick(gates, k) * rk
+            dg = jnp.where(lane8 == k, jnp.sum(u * rk, axis=-1, keepdims=True), dg)
+            dn = dn + dot(place, ret[k, 1], 0, 0)
+        layer_out[r, :] = mixed.astype(BF)
+        un = jnp.sum(u * n, axis=-1, keepdims=True)
+        uv0 = jnp.sum(u * cv0, axis=-1, keepdims=True)
+        uv1 = jnp.sum(u * cv1, axis=-1, keepdims=True)
+        dg = jnp.where(lane8 == 5, un, dg)
+        dg = jnp.where(lane8 == 6, a0 * un + b0 * uv0, dg)
+        dg = jnp.where(lane8 == 7, a1 * un + b1 * uv1, dg)
+        dlog = gates * (dg - jnp.sum(gates * dg, axis=-1, keepdims=True))
+        e0 = g6 * a0 * b0 * (un - uv0)
+        e1 = g7 * a1 * b1 * (un - uv1)
+        lane4 = lane_of((128, 4))
+        dpair = jnp.where(lane4 == 0, e0, jnp.where(lane4 == 1, -e0, jnp.where(lane4 == 2, e1, -e1)))
+        d_res[r, :] = lax.dot_general(dlog, mix_ref[...], (((1,), (1,)), ((), ())), precision=HIGH, preferred_element_type=F32)
+        dn = dn + lax.dot_general(dlog, router_ref[...], (((1,), (1,)), ((), ())), precision=HIGH, preferred_element_type=F32)
+        dn = dn + lax.dot_general(dpair, proj_ref[...], (((1,), (1,)), ((), ())), precision=HIGH, preferred_element_type=F32)
+        small[0:8, :] += lax.dot_general(dlog, n, (((0,), (0,)), ((), ())), precision=HIGH, preferred_element_type=F32)
+        small[8:12, :] += lax.dot_general(dpair, n, (((0,), (0,)), ((), ())), precision=HIGH, preferred_element_type=F32)
+        small[12:13, :] += jnp.sum(c0 * u, axis=0, keepdims=True)
+        small[13:14, :] += jnp.sum(c1 * u, axis=0, keepdims=True)
+        small[14:15, :] += jnp.sum(dn * hn, axis=0, keepdims=True)
+        small[16:24, 0:8] += lax.dot_general(gres_ref[r, :], dlog, (((0,), (0,)), ((), ())), precision=HIGH, preferred_element_type=F32)
+        gd = dn * gain_f_ref[...]
+        dh = u + inv * (gd - hn * jnp.mean(gd * hn, axis=-1, keepdims=True))
+        d_hidden[r, :] = dh
+        dh_all[e, r, :] = dh.astype(BF)
+        return 0
+
+    lax.fori_loop(0, T // 128, mix_step, 0)
+
+    mine = dh_all.at[e]
+    me.send(mine, mine, dh_ss.at[1], dh_rs.at[1], e=me.yp).start()
+    me.send(mine, mine, dh_ss.at[0], dh_rs.at[0], e=me.sib).start()
+    rs_mid_all(2)
+    rs_send(3)
+    wide = pltpu.roll(wqkv[:, 128:384].astype(F32), 192, 1)
+    wk_s[...] = wide[:, 0:C].astype(BF)
+    head_of = lane_of((T, C)) // HD
+    eye = (lax.broadcasted_iota(jnp.int32, (8, 8), 0) == lane_of((8, 8))).astype(F32)
+    heads = (lax.broadcasted_iota(jnp.int32, (8, C), 0) == lane_of((8, C)) // HD).astype(F32)
+    dk[...] = jnp.zeros_like(dk)
+    dv[...] = jnp.zeros_like(dv)
+    for b in range(4):
+        lse_r[b] = lax.dot_general(eye, lse_s[b], (((1,), (1,)), ((), ())), precision=HIGH, preferred_element_type=F32)
+    slot = dh_all.at[me.yp]
+    me.send(slot, slot, dh_ss.at[1], dh_rs.at[1]).wait_recv()
+    fwd = me.send(slot, slot, dh_ss.at[2], dh_rs.at[2], e=me.sib)
+    fwd.start()
+    slot = dh_all.at[me.sib]
+    me.send(slot, slot, dh_ss.at[0], dh_rs.at[0]).wait_recv()
+    slot = dh_all.at[me.diag]
+    me.send(slot, slot, dh_ss.at[2], dh_rs.at[2]).wait_recv()
+
+    gt[0] = jnp.zeros((C, D), F32)
+
+    def da_step(b, _):
+        dhb = dh_all[b]
+        d = dot(dhb, wo[pl.ds(pl.multiple_of(e * C, 64), C), :], 1, 1)
+        low = d.astype(BF)
+        da[b] = low
+        ob = o_s[b]
+        del_r[b] = lax.dot_general(
+            heads, low.astype(F32) * ob.astype(F32), (((1,), (1,)), ((), ())), precision=HIGH, preferred_element_type=F32
+        )
+        gt[0] += dot(ob, dhb, 0, 0)
+        return 0
+
+    lax.fori_loop(0, 4, da_step, 0)
+    go_s[0] = gt[0, 0:R, :].astype(BF)
+    go_s[1] = gt[0, R : 2 * R, :].astype(BF)
+    for j in range(2):
+
+        @pl.when(f != 2 * e + j)
+        def _():
+            me.send(go_s.at[j], go_in.at[f], go_ss.at[j], go_rs.at[f], f=2 * e + j).start()
+
+    rs_mid_all(1)
+    rs_send(0)
+
+    def head_step(i, _):
+        qb = i // 3
+        h = i % 3
+        zero = jnp.zeros((T, C), BF)
+        qh = jnp.where(head_of == h, q_s[qb], zero)
+        dah = jnp.where(head_of == h, da[qb], zero)
+        lse = lse_r[qb, pl.ds(h, 1), :]
+        delta = del_r[qb, pl.ds(h, 1), :]
+
+        def pair(kb, p):
+            dp = dot(v_s[kb], dah, 1, 1)
+            ds = (p * (dp - delta)).astype(BF)
+            dv[kb] += dot(p.astype(BF), dah)
+            dk[kb] += dot(ds, qh)
+            return dot(ds, k_s[kb], 0, 0)
+
+        row = lane_of((T, T))
+        col = lax.broadcasted_iota(jnp.int32, (T, T), 0)
+        first = starts_ref[0, qb] - qb * T
+        inside_c = (col >= first) & (col < first + PIECE)
+        inside_r = (row >= first) & (row < first + PIECE)
+        s = dot(k_s[qb], qh, 1, 1)
+        p = jnp.where((col <= row) | (inside_c & inside_r), jnp.exp2(s - lse), 0.0)
+        dq_acc[...] = pair(qb, p)
+
+        def kv_step(kb, _):
+            s = dot(k_s[kb], qh, 1, 1)
+            dq_acc[...] += pair(kb, jnp.exp2(s - lse))
+            return 0
+
+        lax.fori_loop(0, qb, kv_step, 0)
+        dq[qb] = jnp.where(head_of == h, dq_acc[...], dq[qb])
+        return 0
+
+    lax.fori_loop(0, 6, head_step, 0)
+    rs_mid_all(3)
+    lax.fori_loop(6, 12, head_step, 0)
+
+    @pl.when(z == e)
+    def _():
+        total = go_s[x].astype(F32)
+        for r in range(1, 8):
+            s = go_in.at[fp(r)]
+            me.send(s, s, go_ss.at[0], go_rs.at[fp(r)]).wait_recv()
+            total = total + go_in[fp(r)].astype(F32)
+        go_b[...] = total.astype(BF)
+        for i, p in enumerate(me.exp_peers):
+            me.send(go_b, go_b, gb_ss.at[i], gb_rs.at[0], e=p).start()
+
+    for i in range(3):
+        gt[i] = jnp.zeros((C, D), F32)
+
+    def low(b):
+        return (
+            (dq[b] * (1.0 / math.sqrt(HD))).astype(BF),
+            (dk[b] * LN2).astype(BF),
+            dv[b].astype(BF),
+        )
+
+    def partial_in(b):
+        low_q, low_k, low_v = low(b)
+        out = dot(low_q, wqkv[:, 0:C], 1, 1)
+        out = out + dot(low_k, wk_s[...], 1, 1)
+        out = out + dot(low_v, wqkv[:, 2 * C : 3 * C], 1, 1)
+        small[15:16, :] += jnp.sum(out * attn_all[b].astype(F32), axis=0, keepdims=True)
+        return out
+
+    for i in range(3):
+        me.send(dh_all.at[e], dh_all.at[e], dh_ss.at[i], dh_rs.at[i]).wait_send()
+
+    def far_step(i, _):
+        b = (me.sib + 2 * i) % 4
+        dh_all[b] = partial_in(b).astype(BF)
+        return 0
+
+    lax.fori_loop(0, 2, far_step, 0)
+    me.send(dh_all.at[me.sib], pin.at[0], pd_ss.at[0], pd_rs.at[0], e=me.sib).start()
+    me.send(dh_all.at[me.diag], pin.at[1], pd_ss.at[1], pd_rs.at[1], e=me.sib).start()
+
+    def near_step(i, _):
+        b = (e + 2 * (1 - i)) % 4
+        dh_all[b] = partial_in(b).astype(BF)
+        return 0
+
+    lax.fori_loop(0, 2, near_step, 0)
+    me.send(dh_all.at[me.sib], pin.at[0], pd_ss.at[0], pd_rs.at[0]).wait_recv()
+    me.send(dh_all.at[me.sib], pin.at[1], pd_ss.at[1], pd_rs.at[1]).wait_recv()
+    dh_all[me.yp] = (dh_all[me.yp].astype(F32) + pin[1].astype(F32)).astype(BF)
+    me.send(dh_all.at[me.yp], py_in, pd_ss.at[2], pd_rs.at[2], e=me.yp).start()
+
+    small[15:16, :] = small[15:16, :] / gain_a_ref[...]
+    sm1[e] = small[...]
+    for i, p in enumerate(me.exp_peers):
+        me.send(small, sm1.at[e], s1_ss.at[i], s1_rs.at[i], e=p).start()
+
+    def grad_step(b, _):
+        a = attn_all[b]
+        for i, part in enumerate(low(b)):
+            gt[i] += dot(part, a, 0, 0)
+        return 0
+
+    lax.fori_loop(0, 4, grad_step, 0)
+    for i in range(3):
+        ag_s[:, i] = gt[i].T.astype(BF).reshape(8, R, C)
+    for r in range(1, 8):
+        me.send(ag_s.at[fp(r)], ag_in.at[f], ag_ss.at[r - 1], ag_rs.at[f], f=fp(r)).start()
+    ag_in[f] = ag_s[f]
+
+    for i, p in enumerate(me.exp_peers):
+        me.send(small, sm1.at[p], s1_ss.at[i], s1_rs.at[i]).wait()
+    sm2[f] = sm1[0] + sm1[1] + sm1[2] + sm1[3]
+    for r in range(1, 8):
+        me.send(sm2.at[f], sm2.at[f], s2_ss.at[r - 1], s2_rs.at[f], f=fp(r)).start()
+
+    rs_mid_all(0)
+
+    for r in range(1, 8):
+        s = ag_in.at[fp(r)]
+        me.send(s, s, ag_ss.at[r - 1], ag_rs.at[fp(r)]).wait_recv()
+    for i in range(3):
+        total = ag_in[0, i].astype(F32)
+        for r in range(1, 8):
+            total = total + ag_in[r, i].astype(F32)
+        ag_fin[i] = total.astype(BF)
+    for i, p in enumerate(me.exp_peers):
+        me.send(ag_fin, ag_out.at[e], ab_ss.at[i], ab_rs.at[i], e=p).start()
+    ag_out[e] = ag_fin[...]
+
+    for r in range(1, 8):
+        s = sm2.at[fp(r)]
+        me.send(s, s, s2_ss.at[r - 1], s2_rs.at[fp(r)]).wait_recv()
+    total = sm2[0]
+    for r in range(1, 8):
+        total = total + sm2[r]
+    small_out[...] = total
+
+    me.send(py_in, py_in, pd_ss.at[2], pd_rs.at[2]).wait_recv()
+
+    def token_step(i, _):
+        r = pl.ds(pl.multiple_of(i * 256, 256), 256)
+        d = dh_all[e, r, :].astype(F32) + pin[0, r, :].astype(F32) + py_in[r, :].astype(F32)
+        xv = x_ref[r, :].astype(F32)
+        inv = lax.rsqrt(jnp.mean(xv * xv, axis=-1, keepdims=True) + EPS)
+        xn = xv * inv
+        gd = d * gain_a_ref[...]
+        grad_tokens[r, :] = (d_hidden[r, :] + inv * (gd - xn * jnp.mean(gd * xn, axis=-1, keepdims=True))).astype(BF)
+        return 0
+
+    lax.fori_loop(0, 2, token_step, 0)
+
+    @pl.when(z != e)
+    def _():
+        me.send(go_b, go_b, gb_ss.at[0], gb_rs.at[0]).wait_recv()
+
+    go_out[...] = go_b[...].astype(F32)
+
+    outs = (eg_out, eu_out, ed_out)
+    for w in range(3):
+        g, xin, own, zin = parts[w]
+        for d in (1, 2, 3):
+            z_copy(w, d).wait_recv()
+        total = xin[z].astype(F32) + own[...].astype(F32)
+        for d in range(3):
+            total = total + zin[d].astype(F32)
+        outs[w][...] = total
+
+    for w in range(3):
+        for d in range(4):
+            x_copy(w, d).wait_send()
+            if d:
+                z_copy(w, d).wait_send()
+    for j in range(2):
+
+        @pl.when(f != 2 * e + j)
+        def _():
+            me.send(go_s.at[j], go_in.at[f], go_ss.at[j], go_rs.at[f]).wait_send()
+
+    @pl.when(z == e)
+    def _():
+        for i in range(3):
+            me.send(go_b, go_b, gb_ss.at[i], gb_rs.at[0]).wait_send()
+
+    for i in range(3):
+        me.send(py_in, py_in, pd_ss.at[i], pd_rs.at[i]).wait_send()
+        me.send(ag_fin, ag_out.at[me.exp_peers[i]], ab_ss.at[i], ab_rs.at[i]).wait()
+    for r in range(1, 8):
+        me.send(ag_s.at[0], ag_in.at[f], ag_ss.at[r - 1], ag_rs.at[f]).wait_send()
+        me.send(sm2.at[f], sm2.at[f], s2_ss.at[r - 1], s2_rs.at[f]).wait_send()
+
+
+def call_kb(ret, hidden, u, x, logits, pair, routes, place, gres, attn_all, q, k, v, o, lse, wo, wqkv,
+            gain_a, gain_f, router, proj, mix, cvec, starts, gg, gu, gd):
+    T, D = x.shape
+    C, R = D // 4, D // 8
+    dma = pltpu.SemaphoreType.DMA
+    VM = pltpu.VMEM
+    shapes = (gg.shape[1:], gu.shape[1:], gd.shape[1:])
+    return pl.pallas_call(
+        kb_kernel,
+        name="backward",
+        out_shape=(
+            sds((T, D), BF), sds((T, D), BF), sds((T, 8), F32), sds((24, D), F32),
+            sds((4, 3, R, C), BF), sds((R, D), F32),
+        ) + tuple(sds(s, F32) for s in shapes),
+        in_specs=[vmem()] * 23 + [pl.BlockSpec(memory_space=pltpu.SMEM)] + [anyspace()] * 3,
+        out_specs=tuple([vmem()] * 9),
+        scratch_shapes=[VM((4,) + s, BF) for s in shapes] + [VM(s, BF) for s in shapes] + [VM((3,) + s, BF) for s in shapes] + [
+            VM((4, T, D), BF), VM((4, T, C), BF), VM((4, T, C), F32), VM((4, T, C), F32), VM((4, T, C), F32),
+            VM((T, C), F32), VM((2, T, D), BF), VM((T, D), BF), VM((T, D), F32),
+            VM((D, C), BF), VM((4, 8, T), F32), VM((4, 8, T), F32), VM((3, C, D), F32),
+            VM((8, 3, R, C), BF), VM((8, 3, R, C), BF), VM((3, R, C), BF), VM((2, R, D), BF), VM((8, R, D), BF), VM((R, D), BF),
+            VM((24, D), F32), VM((4, 24, D), F32), VM((8, 24, D), F32),
+            dma((3, 4)), dma((3, 4)), dma((3, 3)), dma((3, 3)), dma((3,)),
+            dma((3,)), dma((3,)), dma((2,)), dma((8,)), dma((3,)), dma((1,)), dma((3,)), dma((3,)),
+            dma((7,)), dma((8,)), dma((3,)), dma((3,)), dma((3,)), dma((3,)), dma((7,)), dma((8,)),
+        ],
+        compiler_params=pltpu.CompilerParams(collective_id=2, has_side_effects=True, vmem_limit_bytes=62 << 20),
+    )(ret, hidden, u, x, logits, pair, routes, place, gres, attn_all, q, k, v, o, lse, wo, wqkv,
+      gain_a, gain_f, router, proj, mix, cvec, starts, gg, gu, gd)
+
+
+def body_fast(
+    tokens, gate_res, routes, piece_starts, norm_attn, norm_ffn, w_query, w_key, w_value, w_out, router, mixing,
+    const_proj, const_vec, w_gate, w_up, w_down, cotangent,
+):
+    x, u, gres, route_ids = tokens[0], cotangent[0], gate_res[0], routes[0]
+    D = x.shape[1]
+    C = D // 4
+    first = lax.axis_index("exp") * C
+    wqkv = jnp.concatenate([lax.dynamic_slice_in_dim(w, first, C, 1) for w in (w_query, w_key, w_value)], axis=1)
+    gain_a, gain_f = norm_attn[None], norm_ffn[None]
+    (attn_all, q, k, v, o, lse, hidden, logits, pair, place, recv, wo, wq, gate, up, down) = call_ka(
+        x, u, wqkv, w_out, w_gate[0], w_up[0], w_down[0], gres, route_ids, route_ids.T, piece_starts,
+        gain_a, gain_f, router, const_proj, mixing,
+    )
+    ret, gg, gu, gd = call_kf(recv, gate, up, down)
+    layer_out, grad_tokens, d_res, small, ag, go, eg, eu, ed = call_kb(
+        ret, hidden, u, x, logits, pair, route_ids, place, gres, attn_all, q, k, v, o, lse, wo, wq,
+        gain_a, gain_f, router, const_proj, mixing, const_vec, piece_starts, gg, gu, gd,
+    )
+    qkv = ag.astype(F32).transpose(1, 2, 0, 3).reshape(3, D // 8, D)
+    return (
+        layer_out[None], grad_tokens[None], d_res[None], small[15], small[14], qkv[0], qkv[1], qkv[2], go,
+        small[0:8].T, small[16:24, 0:8], small[8:12].T, small[12:14], eg[None], eu[None], ed[None],
+    )
+
+
 def solution(mesh):
     placed = (
         P("fsdp", "exp", None),
@@ -451,7 +1364,7 @@
         P("fsdp", "exp", None),
     )
     return jax.shard_map(
-        body,
+        body_fast if (mesh.shape['exp'], mesh.shape['fsdp']) == (4, 8) else body,
         mesh=mesh,
         in_specs=placed,
         out_specs=(

time: 1320 us -> 405 us (0.31)
  waiting for transfers between devices: 815 us -> 0 us
  Pallas kernels: 0 us -> 370 us
  matrix products: 223 us -> 0 us
  local copies, waits for them, and re-layouts: 107 us -> 29.6 us
  other arithmetic: 52.3 us -> 1.91 us
  blocking collectives: 41.5 us -> 0 us
  starting transfers between devices: 34.8 us -> 0 us
  loops' own time: 20.3 us -> 0 us
  between operations: 16.7 us -> 0.77 us
    reduce_scatter x9 -> x0, waiting for transfers between devices: 515 us -> none  [the longest x1 75.1 us: body(): lax.psum_scatter(grad_up_full.astype(jnp.bfloat16), 'fsdp', scatter_dimen...]
    pallas_call x0 -> x3, Pallas kernels: none -> 370 us  [the longest x1 181 us: call_kb(): pl.pallas_call(kb_kernel, name='backward', out_shape=(sds((T, D), BF), sd...]
    all_gather x9 -> x0, waiting for transfers between devices: 248 us -> none  [the longest x1 54.4 us: body(): lax.all_gather(w_gate[0], 'fsdp', axis=0, tiled=True)]
    dot_general x57 -> x0, matrix products: 223 us -> none  [the longest x9 41.4 us: score_block(): jnp.einsum('qhd,khd->hqk', query_heads, key_block, preferred_element_type...]
    psum x1 -> x0, blocking collectives: 41.5 us -> none  [body(): lax.psum((d_norm_attn, d_norm_ffn, d_router, d_mixing, d_const_proj, d_co...]
    all_to_all x4 -> x0, starting transfers between devices: 34.1 us -> none  [the longest x1 18.6 us: body(): lax.all_to_all(d_dispatched.reshape(n_ffn, CAP, model_width), 'exp', spli...]
    psum x1 -> x0, waiting for transfers between devices: 33.6 us -> none  [body(): lax.psum(attn_shards[0].astype(jnp.bfloat16), 'exp').astype(jnp.float32)]
    convert_element_type x8 -> x0, local copies, waits for them, and re-layouts: 26.5 us -> none  [the longest x2 7.49 us: body(): d_expert_rows.reshape(2 * rows_dev, model_width).astype(jnp.bfloat16)]
  transfers between devices with their start and end apart: 23 -> 0, of which waited for: 20 -> 0; matrix products, arithmetic and copies ran while one was open for 14% -> 0% of each run, Pallas kernels for 0% -> 0%
where the time goes in v2:
time: 405 us; the launch traced here: 402 us
  Pallas kernels  370 us (91%)
  local copies, waits for them, and re-layouts  29.6 us (7%)
    pallas_call x1, Pallas kernels, call_kb(): pl.pallas_call(kb_kernel, name='backward', out_shape=(sds((T, D), BF), sd...  181 us
    pallas_call x1, Pallas kernels, call_ka(): pl.pallas_call(ka_kernel, name='forward', out_shape=(sds((4, T, D), BF),...  148 us
    pallas_call x1, Pallas kernels, call_kf(): pl.pallas_call(kf_kernel, name='experts', out_shape=(sds(recv.shape, BF),...  39.9 us
    unnamed x23, local copies, waits for them, and re-layouts  14.7 us

profile of v2, /device:TPU:30, one launch (start us, length us, event | category | flops | bytes accessed | tf_op | source)
XLA Modules:
  0.0 402.0 jit_solution(7928875768329951087)
XLA Ops:
  0.7 1.3 broadcast_in_dim.24.gain_a_ref
  2.0 1.3 broadcast_in_dim.25.gain_f_ref
  3.3 1.0 constant_dynamic-slice_fusion
  6.7 1.6 copy.42
  8.2 1.6 copy.45.router_ref
  9.9 1.6 copy.46.proj_ref
  11.5 148.5 %forward.1 = (bf16[4,512,768]{2,1,0:T(8,128)(2,1)}, bf16[4,512,192]{2,1,0:T(8,128)(2,1)}, bf16[4,512,192]{2,1,0:T(8,128)(2,1)}, bf16[4,512,192]{2,1,0:T(8,128)(2...) custom-call(bf16[512,768]{1,0:T(8,128)(2,1)} %bitcast.24, ...), custom_call_target="tpu_custom_call" | custom-call | tf_op jit(solution)/shard_map/forward/pallas_call | solution.py:772
  160.0 39.9 %experts.1 = (bf16[4,2,160,768]{3,2,1,0:T(8,128)(2,1)}, bf16[8,96,2048]{2,1,0:T(8,128)(2,1)}, bf16[8,96,2048]{2,1,0:T(8,128)(2,1)}, bf16[8,256,768]{2,1,0:T(8,128)(2,1)}) custom-call(bf16[4,2,160,768]{3,2,1,0:T(8,128)(2,1)} %get-tuple-element.45.recv, bf16[8,96,2048]{2,1,0:T(8,128)(2,1)} %get-tuple-element.46.gate_hbm, ...), custom_call_target="tpu_custom_call" | custom-call | tf_op jit(solution)/shard_map/experts/pallas_call | solution.py:896
  199.9 181.3 %backward.1 = (bf16[512,768]{1,0:T(8,128)(2,1)}, bf16[512,768]{1,0:T(8,128)(2,1)}, f32[512,8]{1,0:T(8,128)}, f32[24,768]{1,0:T(8,128)}, bf16[4,3,96,192]{3,2,1,0...) custom-call(bf16[4,2,160,768]{3,2,1,0:T(8,128)(2,1)} %get-tuple-element.49.ret, ...), custom_call_target="tpu_custom_call" | custom-call | tf_op jit(solution)/shard_map/backward/pallas_call | solution.py:1295
  381.2 1.3 slice.36
  382.5 1.3 slice.38
  383.8 1.4 slice_reduce_fusion
  385.2 1.3 slice_bitcast_fusion.1
  386.6 1.3 slice_bitcast_fusion
  387.9 1.7 copy.52
  389.6 1.2 convert_bitcast_fusion
  391.2 1.0 squeeze.47
  392.4 1.0 squeeze.46
  393.6 1.0 squeeze.45
  394.6 2.1 copy.59
  396.7 0.9 copy.60
  397.6 1.7 copy.61
  400.2 0.9 copy.63
  401.1 0.9 copy.64
  (21 shorter events, 4.2 us)
Async XLA Ops:
  0.6 2.6 copy-start
  5.9 5.6 %copy-start.1 = (s32[1,512,2]{2,1,0:T(8,128)}, s32[1,512,2]{2,1,0:T(8,128)S(1)}, u32[]{:S(2)}) copy-start(s32[1,512,2]{2,1,0:T(8,128)S(1)} %copy.43) | copy-start | bytes 12292
  390.9 5.8 %copy-start.5 = (bf16[512,768]{1,0:T(8,128)(2,1)S(1)}, bf16[512,768]{1,0:T(8,128)(2,1)}, u32[]{:S(2)}) copy-start(bf16[512,768]{1,0:T(8,128)(2,1)} %get-tuple-element.66) | copy-start | bytes 2359300
  392.1 7.2 %copy-start.4 = (f32[96,2048]{1,0:T(8,128)S(1)}, f32[96,2048]{1,0:T(8,128)}, u32[]{:S(2)}) copy-start(f32[96,2048]{1,0:T(8,128)} %get-tuple-element.71) | copy-start | bytes 2359300
  393.6 6.6 %copy-start.3 = (f32[96,2048]{1,0:T(8,128)S(1)}, f32[96,2048]{1,0:T(8,128)}, u32[]{:S(2)}) copy-start(f32[96,2048]{1,0:T(8,128)} %get-tuple-element.72) | copy-start | bytes 2359300
  394.6 6.5 %copy-start.2 = (f32[256,768]{1,0:T(8,128)S(1)}, f32[256,768]{1,0:T(8,128)}, u32[]{:S(2)}) copy-start(f32[256,768]{1,0:T(8,128)} %get-tuple-element.73) | copy-start | bytes 2359300

commit v3 on v0

--- a/solution.py
+++ b/solution.py
@@ -3,6 +3,8 @@
 import jax
 import jax.numpy as jnp
 from jax import lax
+from jax.experimental import pallas as pl
+from jax.experimental.pallas import tpu as pltpu
 from jax.sharding import PartitionSpec as P
 
 H = 12
@@ -429,6 +431,981 @@
     )
 
 
+MESH = pl.DeviceIdType.MESH
+BF = jnp.bfloat16
+F32 = jnp.float32
+LN2 = math.log(2.0)
+QSCALE = 1.0 / (LN2 * math.sqrt(HD))
+CHUNKS = 4
+
+
+class Place:
+    def __init__(self):
+        self.e = lax.axis_index("exp")
+        self.f = lax.axis_index("fsdp")
+        self.z = self.f // 2
+        self.x = self.f % 2
+        self.sib = self.e + 1 - 2 * (self.e % 2)
+        self.yp = (self.e + 2) % 4
+        self.diag = (self.sib + 2) % 4
+        self.xf = self.f + 1 - 2 * self.x
+        self.exp_peers = (self.sib, self.yp, self.diag)
+
+    def zf(self, d):
+        return ((self.z + d) % 4) * 2 + self.x
+
+    def fp(self, r):
+        return (self.f + r) % 8
+
+    def far_first(self, j):
+        return (self.e + (j % 2) * (1 - 2 * (self.e % 2)) + 2 * (1 - j // 2)) % 4
+
+    def near_first(self, j):
+        return (self.e + (j % 2) * (1 - 2 * (self.e % 2)) + 2 * (j // 2)) % 4
+
+    def barrier(self):
+        sem = pltpu.get_barrier_semaphore()
+        for p in self.exp_peers:
+            pl.semaphore_signal(sem, inc=1, device_id=(p, self.f), device_id_type=MESH)
+        for r in range(1, 8):
+            pl.semaphore_signal(sem, inc=1, device_id=(self.e, self.fp(r)), device_id_type=MESH)
+        pl.semaphore_wait(sem, 10)
+
+    def send(self, src, dst, ss, rs, e=None, f=None):
+        return pltpu.make_async_remote_copy(
+            src_ref=src,
+            dst_ref=dst,
+            send_sem=ss,
+            recv_sem=rs,
+            device_id=(self.e if e is None else e, self.f if f is None else f),
+            device_id_type=MESH,
+        )
+
+
+def lane_of(shape):
+    return lax.broadcasted_iota(jnp.int32, shape, len(shape) - 1)
+
+
+def row_of(shape):
+    return lax.broadcasted_iota(jnp.int32, shape, 0)
+
+
+def dot(a, b, ca=1, cb=0, precision=None):
+    return lax.dot_general(a, b, (((ca,), (cb,)), ((), ())), precision=precision, preferred_element_type=F32)
+
+
+def allowed_block(size, first):
+    key, query = row_of((size, size)), lane_of((size, size))
+    inside_k = (key >= first) & (key < first + PIECE)
+    inside_q = (query >= first) & (query < first + PIECE)
+    return (key <= query) | (inside_k & inside_q)
+
+
+def k1_kernel(
+    x_ref, u_ref, wq_ref, wk_ref, wv_ref, wo_ref, wg_ref, wu_ref, wd_ref, gres_ref, routes_ref, starts_ref,
+    gain_a_ref, gain_f_ref, router_ref, proj_ref, mix_ref,
+    attn_all, q_s, k_s, v_s, o_s, lse_s, hidden_ref, aux_ref, place_ref, ret_o, ret_d, wo_full, wq_full,
+    grad_gate, grad_up, grad_down, far_gate, far_up, far_down,
+    gate_full, up_full, down_full, wq_own, vt_s, attn_recv, nb, snd_r, snd_d, recv_r, recv_d, m_s, l_s, acc_s,
+    acc, d_acc, st_gate, st_up, st_down,
+    wq_ss, wq_rs, wo_ss, wo_rs, at_ss, at_rs, o_ss, o_rs, dr_ss, dr_rs, dd_ss, dd_rs, ro_ss, ro_rs, rd_ss, rd_rs,
+    us, ur, ds, dr, xs, xr, loc, st_sem, fs, fr,
+):
+    me = Place()
+    e, f, z, xf = me.e, me.f, me.z, me.xf
+    T, D = x_ref.shape
+    C = D // 4
+    R = wo_ref.shape[0]
+    FF = wg_ref.shape[1]
+    W = FF // CHUNKS
+    S = 4 * CAP
+    for k in range(4):
+
+        @pl.when(e == k)
+        def _():
+            for i, w in enumerate((wq_ref, wk_ref, wv_ref)):
+                wq_own[:, i * C : (i + 1) * C] = w[:, k * C : (k + 1) * C]
+
+    me.barrier()
+
+    def rows(ref, index):
+        return ref.at[pl.ds(pl.multiple_of(index * R, 32), R)]
+
+    early = ((wq_own, wq_full, wq_ss, wq_rs, 0), (wo_ref, wo_full, wo_ss, wo_rs, 1))
+    for src, dst, ss, rs, li in early:
+        for d in (1, 3, 2):
+            me.send(src, rows(dst, f), ss.at[d], rs.at[d], f=me.zf(d)).start()
+        me.send(src, rows(dst, f), ss.at[0], rs.at[0], f=xf).start()
+        pltpu.make_async_copy(src, rows(dst, f), loc.at[li]).start()
+
+    xv = x_ref[...].astype(F32)
+    inv = lax.rsqrt(jnp.mean(xv * xv, axis=-1, keepdims=True) + EPS)
+    attn_all[e] = (xv * inv * gain_a_ref[...].reshape(1, D)).astype(BF)
+
+    def at_copy(i, block, to=None):
+        ref = attn_all.at[block]
+        return me.send(ref, ref, at_ss.at[i], at_rs.at[i], e=to)
+
+    at_copy(1, e, me.yp).start()
+    at_copy(0, e, me.sib).start()
+
+    def early_slot(dst, d, other):
+        return rows(dst, ((z - d + 4) % 4) * 2 + (1 - me.x if other else me.x))
+
+    def early_forward(dst, ss, rs):
+        for d in (1, 3, 2):
+            slot = early_slot(dst, d, False)
+            me.send(slot, slot, ss.at[d], rs.at[d]).wait_recv()
+            me.send(slot, slot, ss.at[3 + d], rs.at[3 + d], f=xf).start()
+
+    def early_wait(src, dst, ss, rs, li):
+        pltpu.make_async_copy(src, rows(dst, f), loc.at[li]).wait()
+        me.send(rows(dst, xf), rows(dst, xf), ss.at[0], rs.at[0]).wait_recv()
+        for d in (1, 2, 3):
+            slot = early_slot(dst, d, True)
+            me.send(slot, slot, ss.at[3 + d], rs.at[3 + d]).wait_recv()
+
+    early_forward(*early[0][1:4])
+
+    units = [(wd_ref, down_full, None)]
+    for c in range(CHUNKS):
+        units += [(wg_ref, gate_full, c), (wu_ref, up_full, c)]
+
+    def cut(ref, c):
+        return ref if c is None else ref.at[:, pl.ds(pl.multiple_of(c * W, W), W)]
+
+    def up_copy(n, p, src, dst, to=None):
+        return me.send(src, dst, us.at[n, p], ur.at[n, p], f=to)
+
+    def down_copy(n, p, src, dst, to=None):
+        return me.send(src, dst, ds.at[n, p], dr.at[n, p], f=to)
+
+    def x_copy(n, i, src, dst, to=None):
+        return me.send(src, dst, xs.at[n, i], xr.at[n, i], f=to)
+
+    def experts(p):
+        for n, (src, full, c) in enumerate(units):
+
+            def at(slot):
+                return cut(full.at[slot], c)
+
+            own = cut(src, c)
+            if p == 0:
+                x_copy(n, 0, own, at(f), xf).start()
+
+                @pl.when(z <= 2)
+                def _():
+                    up_copy(n, 0, own, at(f), f + 2).start()
+
+                @pl.when(z >= 1)
+                def _():
+                    down_copy(n, 0, own, at(f), f - 2).start()
+
+            else:
+
+                @pl.when(z >= p)
+                def _():
+                    slot = at(f - 2 * p)
+                    up_copy(n, p - 1, slot, slot).wait_recv()
+                    if p <= 2:
+
+                        @pl.when(z <= 2)
+                        def _():
+                            up_copy(n, p, slot, slot, f + 2).start()
+
+                    x_copy(n, p, slot, slot, xf).start()
+
+                @pl.when(z + p <= 3)
+                def _():
+                    slot = at(f + 2 * p)
+                    down_copy(n, p - 1, slot, slot).wait_recv()
+                    if p <= 2:
+
+                        @pl.when(z >= 1)
+                        def _():
+                            down_copy(n, p, slot, slot, f - 2).start()
+
+                    x_copy(n, 3 + p, slot, slot, xf).start()
+
+    own_loads = ((wd_ref, down_full), (wg_ref, gate_full), (wu_ref, up_full))
+
+    def own_load(i):
+        src, full = own_loads[i]
+        return pltpu.make_async_copy(src, full.at[f], loc.at[2 + i])
+
+    experts(0)
+    for i in range(3):
+        own_load(i).start()
+
+    at_copy(1, me.yp).wait_recv()
+    at_copy(2, me.yp, me.sib).start()
+    at_copy(0, me.sib).wait_recv()
+    early_wait(*early[0])
+    early_forward(*early[1][1:4])
+    at_copy(2, me.diag).wait_recv()
+
+    def qkv_step(i, _):
+        b = i // 2
+        r = pl.ds(pl.multiple_of((i % 2) * 256, 256), 256)
+        out = dot(attn_all[b, r, :], wq_full[...])
+        q_s[b, r, :] = (out[:, 0:C] * QSCALE).astype(BF)
+        k_s[b, r, :] = out[:, C : 2 * C].astype(BF)
+        v = out[:, 2 * C : 3 * C]
+        v_s[b, r, :] = v.astype(BF)
+        vt_s[b, :, r] = v.T.astype(BF)
+        return 0
+
+    lax.fori_loop(0, 8, qkv_step, 0)
+
+    head_of = lane_of((T, C)) // HD
+    lse_s[...] = jnp.zeros_like(lse_s)
+
+    def query_step(j, _):
+        qb = me.far_first(j)
+        queries = [jnp.where(head_of == h, q_s[qb], jnp.zeros((T, C), BF)) for h in range(3)]
+        allowed = allowed_block(T, starts_ref[0, qb] - qb * T)
+        for h in range(3):
+            hr = pl.ds(h * HD, HD)
+            s = jnp.where(allowed, dot(k_s[qb], queries[h], 1, 1), NEG)
+            m = jnp.max(s, axis=0, keepdims=True)
+            p = jnp.exp2(s - m)
+            m_s[h : h + 1] = m
+            l_s[h : h + 1] = jnp.sum(p, axis=0, keepdims=True)
+            acc_s[hr] = dot(vt_s[qb, hr, :], p.astype(BF))
+
+        def key_step(kb, _):
+            for h in range(3):
+                hr = pl.ds(h * HD, HD)
+                query = jnp.where(head_of == h, q_s[qb], jnp.zeros((T, C), BF))
+                s = dot(k_s[kb], query, 1, 1)
+                m_old = m_s[h : h + 1]
+                m = jnp.maximum(m_old, jnp.max(s, axis=0, keepdims=True))
+                scale = jnp.exp2(m_old - m)
+                p = jnp.exp2(s - m)
+                m_s[h : h + 1] = m
+                l_s[h : h + 1] = l_s[h : h + 1] * scale + jnp.sum(p, axis=0, keepdims=True)
+                acc_s[hr] = acc_s[hr] * scale + dot(vt_s[kb, hr, :], p.astype(BF))
+            return 0
+
+        lax.fori_loop(0, qb, key_step, 0)
+        for h in range(3):
+            hr = pl.ds(h * HD, HD)
+            total = l_s[h : h + 1]
+            acc_s[hr] = acc_s[hr] / total
+            lse_s[qb, h : h + 1, :] = m_s[h : h + 1] + jnp.log2(total)
+        o_s[qb] = acc_s[...].T.astype(BF)
+        return 0
+
+    def o_copy(i, to=None):
+        p = me.exp_peers[i]
+        if to is None:
+            return me.send(o_s.at[p], attn_recv.at[p], o_ss.at[i], o_rs.at[i])
+        return me.send(o_s.at[p], attn_recv.at[e], o_ss.at[i], o_rs.at[i], e=p)
+
+    lax.fori_loop(0, 2, query_step, 0)
+    o_copy(1, True).start()
+    o_copy(2, True).start()
+    experts(1)
+    lax.fori_loop(2, 4, query_step, 0)
+    o_copy(0, True).start()
+    attn_recv[e] = o_s[e]
+
+    r0, r1 = routes_ref[0:1, :], routes_ref[1:2, :]
+    expert = row_of((8, T))
+    chosen = (expert == r0) | (expert == r1)
+    earlier = (row_of((T, T)) < lane_of((T, T))).astype(BF)
+    count = dot(chosen.astype(BF), earlier).astype(jnp.int32)
+    count = jnp.where(chosen, count, -1)
+    slot_id = row_of((CAP, T))
+    for k in range(4):
+        place_ref[k] = jnp.where(slot_id == count[k : k + 1, :], 1.0, 0.0).astype(BF)
+
+    early_wait(*early[1])
+    for i in (0, 1, 2):
+        o_copy(i).wait_recv()
+
+    def hidden_step(i, _):
+        r = pl.ds(pl.multiple_of(i * 256, 256), 256)
+        h = x_ref[r, :].astype(F32)
+        for b in range(4):
+            h = h + dot(attn_recv[b, r, :], wo_full[b * C : (b + 1) * C, :])
+        hidden_ref[r, :] = h
+        n = h * lax.rsqrt(jnp.mean(h * h, axis=-1, keepdims=True) + EPS) * gain_f_ref[...].reshape(1, D)
+        nb[r, :] = n.astype(BF)
+        aux_ref[0:8, r] = dot(router_ref[...], n, 1, 1, HIGH) + dot(mix_ref[...], gres_ref[:, r], 0, 0, HIGH)
+        aux_ref[8:12, r] = dot(proj_ref[...], n, 1, 1, HIGH)
+        return 0
+
+    lax.fori_loop(0, 2, hidden_step, 0)
+    experts(2)
+
+    logits = aux_ref[0:8, :]
+    top = jnp.max(jnp.where(chosen, logits, NEG), axis=0, keepdims=True)
+    weight = jnp.where(chosen, jnp.exp(logits - top), 0.0)
+    gates = weight / jnp.sum(weight, axis=0, keepdims=True)
+    pairs = aux_ref[8:12, :]
+    other = jnp.concatenate([pairs[1:2], pairs[0:1], pairs[3:4], pairs[2:3]], axis=0)
+    aux_ref[0:8, :] = gates
+    aux_ref[8:12, :] = 1.0 / (1.0 + jnp.exp(other - pairs))
+    aux_ref[12:16, :] = jnp.zeros((4, T), F32)
+
+    def d_copy(i, ref, out, ss, rs, k, to=None):
+        return me.send(ref.at[k], out.at[e if to is not None else k], ss.at[i], rs.at[i], e=to)
+
+    def dispatch_step(j, _):
+        k = me.far_first(j)
+        i = (j + 1) % 4
+        place = place_ref[k]
+        snd_r[k] = dot(place, nb[...]).astype(BF)
+        gate = aux_ref[pl.ds(k, 1), :]
+        gated = jnp.where(place > 0, gate.astype(BF), jnp.zeros((CAP, T), BF))
+        snd_d[k] = dot(gated, u_ref[...]).astype(BF)
+
+        @pl.when(j != 2)
+        def _():
+            d_copy(i, snd_r, recv_r, dr_ss, dr_rs, k, k).start()
+            d_copy(i, snd_d, recv_d, dd_ss, dd_rs, k, k).start()
+
+        @pl.when(j == 2)
+        def _():
+            recv_r[k] = snd_r[k]
+            recv_d[k] = snd_d[k]
+
+        return 0
+
+    lax.fori_loop(0, 4, dispatch_step, 0)
+    for i, p in enumerate(me.exp_peers):
+        d_copy(i, snd_r, recv_r, dr_ss, dr_rs, p).wait()
+        d_copy(i, snd_d, recv_d, dd_ss, dd_rs, p).wait()
+    experts(3)
+
+    acc[...] = jnp.zeros_like(acc)
+    d_acc[...] = jnp.zeros_like(d_acc)
+
+    def unit_wait(n, full, c):
+        def at(slot):
+            return cut(full.at[slot], c)
+
+        x_copy(n, 0, at(xf), at(xf)).wait_recv()
+        for p in (1, 2, 3):
+
+            @pl.when(z >= p)
+            def _():
+                x_copy(n, p, at(xf - 2 * p), at(xf - 2 * p)).wait_recv()
+
+            @pl.when(z + p <= 3)
+            def _():
+                x_copy(n, 3 + p, at(xf + 2 * p), at(xf + 2 * p)).wait_recv()
+
+    stages = ((st_gate, grad_gate, 0), (st_up, grad_up, 1), (st_down, grad_down, 2))
+
+    def stage_copy(c, i):
+        st, out, _ = stages[i]
+        if i == 2:
+            dst = out.at[pl.ds(2 * c, 2)]
+        else:
+            dst = out.at[:, :, pl.ds(pl.multiple_of(c * W, W), W)]
+        return pltpu.make_async_copy(st, dst, st_sem.at[i])
+
+    def ret_copy(i, snd, ret, ss, rs, to=None):
+        p = me.exp_peers[i]
+        return me.send(snd.at[p], ret.at[e if to else p], ss.at[i], rs.at[i], e=p if to else None)
+
+    def expert_step(c, _):
+        @pl.when(c == 0)
+        def _():
+            for i in range(3):
+                own_load(i).wait()
+            unit_wait(0, down_full, None)
+
+        unit_wait(1 + 2 * c, gate_full, c)
+        unit_wait(2 + 2 * c, up_full, c)
+        w = pl.ds(pl.multiple_of(c * W, W), W)
+        row_in = recv_r[...].reshape(S, D)
+        d_in = recv_d[...].reshape(S, D)
+        w_gate = gate_full[:, :, w].reshape(D, W)
+        w_up = up_full[:, :, w].reshape(D, W)
+        w_down = down_full[pl.ds(2 * c, 2)].reshape(W, D)
+        g = dot(row_in, w_gate)
+        up = dot(row_in, w_up)
+        sig = 1.0 / (1.0 + jnp.exp(-g))
+        silu = g * sig
+        inner = (silu * up).astype(BF)
+        acc[...] += dot(inner, w_down)
+
+        @pl.when(c == CHUNKS - 1)
+        def _():
+            snd_r[...] = acc[...].astype(BF).reshape(4, CAP, D)
+            for i in (1, 2, 0):
+                ret_copy(i, snd_r, ret_o, ro_ss, ro_rs, True).start()
+            ret_o[e] = snd_r[e]
+
+        d_inner = dot(d_in, w_down, 1, 1)
+        d_up = (d_inner * silu).astype(BF)
+        d_gate = (d_inner * up * (sig + silu * (1.0 - sig))).astype(BF)
+        d_acc[...] += dot(d_gate, w_gate, 1, 1) + dot(d_up, w_up, 1, 1)
+
+        @pl.when(c == CHUNKS - 1)
+        def _():
+            snd_d[...] = d_acc[...].astype(BF).reshape(4, CAP, D)
+            for i in (1, 2, 0):
+                ret_copy(i, snd_d, ret_d, rd_ss, rd_rs, True).start()
+            ret_d[e] = snd_d[e]
+
+        @pl.when(c > 0)
+        def _():
+            for i in range(3):
+                stage_copy(c - 1, i).wait()
+
+        st_down[...] = dot(inner, d_in, 0, 0).astype(BF).reshape(2, W // 2, D)
+        st_gate[...] = dot(row_in, d_gate, 0, 0).astype(BF).reshape(8, R, W)
+        st_up[...] = dot(row_in, d_up, 0, 0).astype(BF).reshape(8, R, W)
+        for i in range(3):
+            stage_copy(c, i).start()
+        return 0
+
+    lax.fori_loop(0, CHUNKS, expert_step, 0)
+    for i in range(3):
+        stage_copy(CHUNKS - 1, i).wait()
+
+    far_row = 2 * ((z + 3 - 2 * (z % 2)) % 4) + 1 - me.x
+    far = ((grad_gate, far_gate), (grad_up, far_up), (grad_down, far_down))
+    for i, (src, dst) in enumerate(far):
+        me.send(src.at[far_row], dst, fs.at[i], fr.at[i], f=xf).start()
+
+    for src, dst, ss, rs, li in early:
+        for j in range(7):
+            me.send(rows(dst, f), rows(dst, f), ss.at[j], rs.at[j]).wait_send()
+    for i in range(3):
+        at_copy(i, e).wait_send()
+        o_copy(i).wait_send()
+    for n, (src, full, c) in enumerate(units):
+        slot = cut(full.at[f], c)
+        x_copy(n, 0, slot, slot).wait_send()
+
+        @pl.when(z <= 2)
+        def _():
+            up_copy(n, 0, slot, slot).wait_send()
+
+        @pl.when(z >= 1)
+        def _():
+            down_copy(n, 0, slot, slot).wait_send()
+
+        for p in (1, 2, 3):
+
+            @pl.when(z >= p)
+            def _():
+                if p <= 2:
+
+                    @pl.when(z <= 2)
+                    def _():
+                        up_copy(n, p, slot, slot).wait_send()
+
+                x_copy(n, p, slot, slot).wait_send()
+
+            @pl.when(z + p <= 3)
+            def _():
+                if p <= 2:
+
+                    @pl.when(z >= 1)
+                    def _():
+                        down_copy(n, p, slot, slot).wait_send()
+
+                x_copy(n, 3 + p, slot, slot).wait_send()
+
+    for i in range(3):
+        ret_copy(i, snd_r, ret_o, ro_ss, ro_rs).wait()
+        ret_copy(i, snd_d, ret_d, rd_ss, rd_rs).wait()
+    for i, (src, dst) in enumerate(far):
+        me.send(src.at[far_row], dst, fs.at[i], fr.at[i]).wait()
+
+
+def sds(shape, dtype):
+    return jax.ShapeDtypeStruct(shape, dtype)
+
+
+def vmem():
+    return pl.BlockSpec(memory_space=pltpu.VMEM)
+
+
+def anyspace():
+    return pl.BlockSpec(memory_space=pl.ANY)
+
+
+def smem():
+    return pl.BlockSpec(memory_space=pltpu.SMEM)
+
+
+def call_k1(x, u, wq, wk, wv, wo, wg, wu, wd, gres, routes, starts, gain_a, gain_f, router, proj, mix):
+    T, D = x.shape
+    C, R, FF, S = D // 4, D // 8, wg.shape[1], 4 * CAP
+    n = 1 + 2 * CHUNKS
+    dma = pltpu.SemaphoreType.DMA
+    VM = pltpu.VMEM
+    block = VM((4, CAP, D), BF)
+    return pl.pallas_call(
+        k1_kernel,
+        name="forward",
+        out_shape=(
+            sds((4, T, D), BF), sds((4, T, C), BF), sds((4, T, C), BF), sds((4, T, C), BF), sds((4, T, C), BF),
+            sds((4, 8, T), F32), sds((T, D), F32), sds((16, T), F32), sds((4, CAP, T), BF),
+            sds((4, CAP, D), BF), sds((4, CAP, D), BF), sds((D, D), BF), sds((D, 3 * C), BF),
+            sds((8, R, FF), BF), sds((8, R, FF), BF), sds((8, FF // 8, D), BF),
+            sds((R, FF), BF), sds((R, FF), BF), sds((FF // 8, D), BF),
+        ),
+        in_specs=[vmem()] * 5 + [anyspace()] * 4 + [vmem()] * 2 + [smem()] + [vmem()] * 5,
+        out_specs=tuple([vmem()] * 13 + [anyspace()] * 6),
+        scratch_shapes=[
+            VM((8, R, FF), BF), VM((8, R, FF), BF), VM((8, FF // 8, D), BF), VM((R, 3 * C), BF), VM((4, C, T), BF),
+            VM((4, T, C), BF), VM((T, D), BF), block, block, block, block, VM((8, T), F32), VM((8, T), F32), VM((C, T), F32),
+            VM((S, D), F32), VM((S, D), F32), VM((8, R, FF // CHUNKS), BF), VM((8, R, FF // CHUNKS), BF), VM((2, FF // 8, D), BF),
+            dma((7,)), dma((7,)), dma((7,)), dma((7,)),
+        ] + [dma((3,))] * 12 + [
+            dma((n, 3)), dma((n, 3)), dma((n, 3)), dma((n, 3)), dma((n, 7)), dma((n, 7)),
+            dma((5,)), dma((3,)), dma((3,)), dma((3,)),
+        ],
+        compiler_params=pltpu.CompilerParams(collective_id=0, has_side_effects=True, vmem_limit_bytes=60 << 20),
+    )(x, u, wq, wk, wv, wo, wg, wu, wd, gres, routes, starts, gain_a, gain_f, router, proj, mix)
+
+
+def k2_kernel(
+    ret_o, ret_d, hidden, u_ref, x_ref, aux_ref, place_ref, gres_ref,
+    attn_all, q_s, k_s, v_s, o_s, lse_s, wo, wqkv, gain_a_ref, gain_f_ref, router_ref, proj_ref, mix_ref, cvec_ref, starts_ref,
+    g_gate, g_up, g_down, far_gate, far_up, far_down,
+    layer_out, grad_tokens, d_res, small_out, ag_out, go_b, eg_out, eu_out, ed_out,
+    xin_g, xin_u, xin_d, own_g, own_u, own_d, zin_g, zin_u, zin_d,
+    dh_all, da, kt_s, dq, dk, dv, dqt, pin, py_in, d_hidden, wk_s, del_r, gt, ag_s, ag_in, ag_fin, go_s, go_in,
+    small, sm1, sm2,
+    far_sem, xs, xr, zs, zr, own_sem, dh_ss, dh_rs, fw_ss, fw_rs, go_ss, go_rs, gb_ss, gb_rs, pd_ss, pd_rs, ag_ss, ag_rs,
+    ab_ss, ab_rs, s1_ss, s1_rs, s2_ss, s2_rs,
+):
+    me = Place()
+    e, f, z, x, xf = me.e, me.f, me.z, me.x, me.xf
+    T, D = x_ref.shape
+    C = D // 4
+    R = D // 8
+    M = 128
+
+    partner = z + 1 - 2 * (z % 2)
+    order = ((partner + 2) % 4, (z + 2) % 4, partner, z)
+    parts = (
+        (g_gate, xin_g, own_g, zin_g, far_gate, eg_out),
+        (g_up, xin_u, own_u, zin_u, far_up, eu_out),
+        (g_down, xin_d, own_d, zin_d, far_down, ed_out),
+    )
+
+    def far_copy(w):
+        return pltpu.make_async_copy(parts[w][4], parts[w][1].at[0], far_sem.at[w])
+
+    def own_copy(w, i):
+        return pltpu.make_async_copy(parts[w][0].at[2 * order[i] + x], parts[w][2], own_sem.at[w])
+
+    def x_copy(w, i):
+        return me.send(parts[w][0].at[2 * order[i] + 1 - x], parts[w][1].at[i], xs.at[w, i], xr.at[w, i], f=xf)
+
+    def z_copy(w, i):
+        to = order[1] if i == 1 else partner
+        return me.send(parts[w][1].at[i], parts[w][3].at[i], zs.at[w, i], zr.at[w, i], f=2 * to + x)
+
+    def x_send(i):
+        for w in range(3):
+            x_copy(w, i).start()
+
+    def rs_mid(i):
+        for w in range(3):
+            xin, own, zin = parts[w][1:4]
+            if i:
+                x_copy(w, i).wait_recv()
+            else:
+                far_copy(w).wait()
+            own_copy(w, i).wait()
+            total = xin[i].astype(F32) + own[...].astype(F32)
+            if i == 1:
+                z_copy(w, 0).wait_recv()
+                total = total + zin[0].astype(F32)
+            if i == 3:
+                z_copy(w, 1).wait_recv()
+                z_copy(w, 2).wait_recv()
+                total = total + zin[1].astype(F32) + zin[2].astype(F32)
+                parts[w][5][...] = total.astype(BF)
+            else:
+                xin[i] = total.astype(BF)
+                z_copy(w, i).start()
+                own_copy(w, i + 1).start()
+
+    for w in range(3):
+        far_copy(w).start()
+        own_copy(w, 0).start()
+    me.barrier()
+    x_send(1)
+    rs_mid(0)
+    x_send(2)
+
+    small[...] = jnp.zeros_like(small)
+    cv0, cv1 = cvec_ref[0:1, :], cvec_ref[1:2, :]
+    maps = jnp.concatenate([router_ref[...], proj_ref[...], jnp.zeros((4, D), F32)], axis=0).astype(BF)
+    lane8 = lane_of((M, 8))
+    lane4 = lane_of((M, 4))
+
+    def dh_copy(i, c, block, to=None):
+        ref = dh_all.at[block, pl.ds(pl.multiple_of(c * M, M), M)]
+        return me.send(ref, ref, dh_ss.at[i, c], dh_rs.at[i, c], e=to)
+
+    def mix_step(c, _):
+        r = pl.ds(pl.multiple_of(c * M, M), M)
+        h = hidden[r, :]
+        u = u_ref[r, :].astype(F32)
+        inv = lax.rsqrt(jnp.mean(h * h, axis=-1, keepdims=True) + EPS)
+        hn = h * inv
+        gain = gain_f_ref[...].reshape(1, D)
+        n = hn * gain
+        cols = aux_ref[:, r].T
+        gates = cols[:, 0:8]
+        a0, b0, a1, b1 = cols[:, 8:9], cols[:, 9:10], cols[:, 10:11], cols[:, 11:12]
+        g5, g6, g7 = cols[:, 5:6], cols[:, 6:7], cols[:, 7:8]
+        c_n = g5 + g6 * a0 + g7 * a1
+        c0 = g6 * b0
+        c1 = g7 * b1
+        mixed = h + c_n * n + c0 * cv0 + c1 * cv1
+        dg = jnp.zeros((M, 8), F32)
+        dn = c_n * u
+        for k in range(4):
+            place = place_ref[k, :, r]
+            rk = dot(place, ret_o[k], 0, 0)
+            mixed = mixed + cols[:, k : k + 1] * rk
+            dg = jnp.where(lane8 == k, jnp.sum(u * rk, axis=-1, keepdims=True), dg)
+            dn = dn + dot(place, ret_d[k], 0, 0)
+        layer_out[r, :] = mixed.astype(BF)
+        un = jnp.sum(u * n, axis=-1, keepdims=True)
+        uv0 = jnp.sum(u * cv0, axis=-1, keepdims=True)
+        uv1 = jnp.sum(u * cv1, axis=-1, keepdims=True)
+        dg = jnp.where(lane8 == 5, un, dg)
+        dg = jnp.where(lane8 == 6, a0 * un + b0 * uv0, dg)
+        dg = jnp.where(lane8 == 7, a1 * un + b1 * uv1, dg)
+        dlog = gates * (dg - jnp.sum(gates * dg, axis=-1, keepdims=True))
+        e0 = g6 * a0 * b0 * (un - uv0)
+        e1 = g7 * a1 * b1 * (un - uv1)
+        dpair = jnp.where(lane4 == 0, e0, jnp.where(lane4 == 1, -e0, jnp.where(lane4 == 2, e1, -e1)))
+        dl = jnp.concatenate([dlog, dpair, c0, c1, jnp.zeros((M, 2), F32)], axis=1)
+        low = dl.astype(BF)
+        d_res[:, r] = dot(mix_ref[...], dlog, 1, 1, HIGH)
+        dn = dn + dot(jnp.where(lane_of((M, 16)) < 12, low, jnp.zeros((M, 16), BF)), maps)
+        by_n = dot(low, n.astype(BF), 0, 0)
+        by_u = dot(low, u_ref[r, :], 0, 0)
+        small[0:12, :] += by_n[0:12]
+        small[12:14, :] += by_u[12:14]
+        small[14:15, :] += jnp.sum(dn * hn, axis=0, keepdims=True)
+        small[16:24, 0:8] += dot(gres_ref[:, r], dlog, 1, 0, HIGH)
+        gd = dn * gain
+        dh = u + inv * (gd - hn * jnp.mean(gd * hn, axis=-1, keepdims=True))
+        d_hidden[r, :] = dh
+        dh_all[e, r, :] = dh.astype(BF)
+        dh_copy(1, c, e, me.yp).start()
+        dh_copy(0, c, e, me.sib).start()
+        return 0
+
+    lax.fori_loop(0, T // M, mix_step, 0)
+    rs_mid(1)
+    x_send(3)
+
+    head_of = lane_of((T, C)) // HD
+    heads = (row_of((8, C)) == lane_of((8, C)) // HD).astype(F32)
+    wk_s[...] = wqkv[:, C : 2 * C]
+    dk[...] = jnp.zeros_like(dk)
+    dv[...] = jnp.zeros_like(dv)
+    gt[0] = jnp.zeros((C, D), F32)
+    for b in range(4):
+        kt_s[b] = k_s[b].T
+
+    def fw_copy(block, to=None):
+        return me.send(dh_all.at[block], dh_all.at[block], fw_ss.at[0], fw_rs.at[0], e=to)
+
+    def query_step(j, _):
+        qb = me.near_first(j)
+
+        @pl.when(j == 1)
+        def _():
+            for c in range(T // M):
+                dh_copy(0, c, me.sib).wait_recv()
+
+        @pl.when(j == 2)
+        def _():
+            for c in range(T // M):
+                dh_copy(1, c, me.yp).wait_recv()
+            fw_copy(me.yp, me.sib).start()
+
+        @pl.when(j == 3)
+        def _():
+            fw_copy(me.diag).wait_recv()
+
+        dhb = dh_all[qb]
+        low = dot(dhb, wo[pl.ds(pl.multiple_of(e * C, 64), C), :], 1, 1).astype(BF)
+        da[...] = low
+        ob = o_s[qb]
+        del_r[...] = dot(heads, low.astype(F32) * ob.astype(F32), 1, 1, HIGH)
+        gt[0] += dot(ob, dhb, 0, 0)
+
+        def pair(kb, h, masked):
+            zero = jnp.zeros((T, C), BF)
+            query = jnp.where(head_of == h, q_s[qb], zero)
+            d_out = jnp.where(head_of == h, da[...], zero)
+            p = jnp.exp2(dot(k_s[kb], query, 1, 1) - lse_s[qb, h : h + 1, :])
+            if masked:
+                p = jnp.where(allowed_block(T, starts_ref[0, qb] - qb * T), p, 0.0)
+            dp = dot(v_s[kb], d_out, 1, 1)
+            dsc = (p * (dp - del_r[h : h + 1, :])).astype(BF)
+            return dot(p.astype(BF), d_out), dot(dsc, query), dot(kt_s[kb, h * HD : (h + 1) * HD, :], dsc)
+
+        def block(kb, masked):
+            r = [pair(kb, h, masked) for h in range(3)]
+            dv[kb] += r[0][0] + r[1][0] + r[2][0]
+            dk[kb] += r[0][1] + r[1][1] + r[2][1]
+            for h in range(3):
+                if masked:
+                    dqt[h * HD : (h + 1) * HD, :] = r[h][2]
+                else:
+                    dqt[h * HD : (h + 1) * HD, :] += r[h][2]
+
+        block(qb, True)
+
+        def key_step(kb, _):
+            block(kb, False)
+            return 0
+
+        lax.fori_loop(0, qb, key_step, 0)
+        dq[qb] = (dqt[...].T * (1.0 / math.sqrt(HD))).astype(BF)
+        return 0
+
+    lax.fori_loop(0, 3, query_step, 0)
+    rs_mid(2)
+    lax.fori_loop(3, 4, query_step, 0)
+
+    go_s[0] = gt[0, 0:R, :].astype(BF)
+    go_s[1] = gt[0, R : 2 * R, :].astype(BF)
+    for j in range(2):
+
+        @pl.when(f != 2 * e + j)
+        def _():
+            me.send(go_s.at[j], go_in.at[f], go_ss.at[j], go_rs.at[f], f=2 * e + j).start()
+
+    def low(b):
+        return dq[b], (dk[b] * LN2).astype(BF), dv[b].astype(BF)
+
+    for i in range(3):
+        gt[i] = jnp.zeros((C, D), F32)
+
+    def grad_step(b, _):
+        a = attn_all[b]
+        for i, part in enumerate(low(b)):
+            gt[i] += dot(part, a, 0, 0)
+        return 0
+
+    lax.fori_loop(0, 4, grad_step, 0)
+    for i in range(3):
+        ag_s[:, i] = gt[i].T.astype(BF).reshape(8, R, C)
+    for r in range(1, 8):
+        me.send(ag_s.at[me.fp(r)], ag_in.at[f], ag_ss.at[r - 1], ag_rs.at[f], f=me.fp(r)).start()
+    ag_in[f] = ag_s[f]
+
+    for c in range(T // M):
+        dh_copy(0, c, e).wait_send()
+        dh_copy(1, c, e).wait_send()
+    fw_copy(e).wait_send()
+
+    def share_step(j, _):
+        b = (me.sib + 2 * j + (j // 2) * (e - me.sib)) % 4
+        low_q, low_k, low_v = low(b)
+        out = dot(low_q, wqkv[:, 0:C], 1, 1)
+        out = out + dot(low_k, wk_s[...], 1, 1)
+        out = out + dot(low_v, wqkv[:, 2 * C : 3 * C], 1, 1)
+        small[15:16, :] += jnp.sum(out * attn_all[b].astype(F32), axis=0, keepdims=True)
+        dh_all[b] = out.astype(BF)
+        return 0
+
+    def pd_copy(i, src, dst, to=None):
+        return me.send(src, dst, pd_ss.at[i], pd_rs.at[i], e=to)
+
+    lax.fori_loop(0, 2, share_step, 0)
+    pd_copy(1, dh_all.at[me.diag], pin.at[1], me.sib).start()
+    pd_copy(0, dh_all.at[me.sib], pin.at[0], me.sib).start()
+    lax.fori_loop(2, 4, share_step, 0)
+    pd_copy(1, pin.at[1], pin.at[1]).wait_recv()
+    dh_all[me.yp] = (dh_all[me.yp].astype(F32) + pin[1].astype(F32)).astype(BF)
+    pd_copy(2, dh_all.at[me.yp], py_in, me.yp).start()
+
+    small[15:16, :] = small[15:16, :] / gain_a_ref[...].reshape(1, D)
+    sm1[e] = small[...]
+    for i, p in enumerate(me.exp_peers):
+        me.send(small, sm1.at[e], s1_ss.at[i], s1_rs.at[i], e=p).start()
+
+    @pl.when(z == e)
+    def _():
+        total = go_s[x].astype(F32)
+        for r in range(1, 8):
+            s = go_in.at[me.fp(r)]
+            me.send(s, s, go_ss.at[0], go_rs.at[me.fp(r)]).wait_recv()
+            total = total + go_in[me.fp(r)].astype(F32)
+        go_b[...] = total.astype(BF)
+        for i, p in enumerate(me.exp_peers):
+            me.send(go_b, go_b, gb_ss.at[i], gb_rs.at[0], e=p).start()
+
+    for i, p in enumerate(me.exp_peers):
+        me.send(small, sm1.at[p], s1_ss.at[i], s1_rs.at[i]).wait()
+    sm2[f] = sm1[0] + sm1[1] + sm1[2] + sm1[3]
+    for r in range(1, 8):
+        me.send(sm2.at[f], sm2.at[f], s2_ss.at[r - 1], s2_rs.at[f], f=me.fp(r)).start()
+
+    rs_mid(3)
+
+    for r in range(1, 8):
+        s = ag_in.at[me.fp(r)]
+        me.send(s, s, ag_ss.at[r - 1], ag_rs.at[me.fp(r)]).wait_recv()
+    for i in range(3):
+        total = ag_in[0, i].astype(F32)
+        for r in range(1, 8):
+            total = total + ag_in[r, i].astype(F32)
+        ag_fin[i] = total.astype(BF)
+    for i, p in enumerate(me.exp_peers):
+        me.send(ag_fin, ag_out.at[e], ab_ss.at[i], ab_rs.at[i], e=p).start()
+    ag_out[e] = ag_fin[...]
+
+    for r in range(1, 8):
+        s = sm2.at[me.fp(r)]
+        me.send(s, s, s2_ss.at[r - 1], s2_rs.at[me.fp(r)]).wait_recv()
+    total = sm2[0]
+    for r in range(1, 8):
+        total = total + sm2[r]
+    small_out[...] = total
+
+    pd_copy(0, pin.at[0], pin.at[0]).wait_recv()
+    pd_copy(2, py_in, py_in).wait_recv()
+
+    def token_step(i, _):
+        r = pl.ds(pl.multiple_of(i * 256, 256), 256)
+        d = dh_all[e, r, :].astype(F32) + pin[0, r, :].astype(F32) + py_in[r, :].astype(F32)
+        xv = x_ref[r, :].astype(F32)
+        inv = lax.rsqrt(jnp.mean(xv * xv, axis=-1, keepdims=True) + EPS)
+        xn = xv * inv
+        gd = d * gain_a_ref[...].reshape(1, D)
+        grad_tokens[r, :] = (d_hidden[r, :] + inv * (gd - xn * jnp.mean(gd * xn, axis=-1, keepdims=True))).astype(BF)
+        return 0
+
+    lax.fori_loop(0, 2, token_step, 0)
+
+    @pl.when(z != e)
+    def _():
+        me.send(go_b, go_b, gb_ss.at[0], gb_rs.at[0]).wait_recv()
+
+    for w in range(3):
+        for i in range(3):
+            x_copy(w, i + 1).wait_send()
+            z_copy(w, i).wait_send()
+    for j in range(2):
+
+        @pl.when(f != 2 * e + j)
+        def _():
+            me.send(go_s.at[j], go_in.at[f], go_ss.at[j], go_rs.at[f]).wait_send()
+
+    @pl.when(z == e)
+    def _():
+        for i in range(3):
+            me.send(go_b, go_b, gb_ss.at[i], gb_rs.at[0]).wait_send()
+
+    for i in range(3):
+        pd_copy(i, py_in, py_in).wait_send()
+        me.send(ag_fin, ag_out.at[me.exp_peers[i]], ab_ss.at[i], ab_rs.at[i]).wait()
+    for r in range(1, 8):
+        me.send(ag_s.at[0], ag_in.at[f], ag_ss.at[r - 1], ag_rs.at[f]).wait_send()
+        me.send(sm2.at[f], sm2.at[f], s2_ss.at[r - 1], s2_rs.at[f]).wait_send()
+
+
+def call_k2(*args):
+    x, (gg, gu, gd) = args[4], args[23:26]
+    T, D = x.shape
+    C, R = D // 4, D // 8
+    dma = pltpu.SemaphoreType.DMA
+    VM = pltpu.VMEM
+    shapes = (gg.shape[1:], gu.shape[1:], gd.shape[1:])
+    return pl.pallas_call(
+        k2_kernel,
+        name="backward",
+        out_shape=(
+            sds((T, D), BF), sds((T, D), BF), sds((8, T), F32), sds((24, D), F32),
+            sds((4, 3, R, C), BF), sds((R, D), BF),
+        ) + tuple(sds(s, BF) for s in shapes),
+        in_specs=[vmem()] * 22 + [smem()] + [anyspace()] * 6,
+        out_specs=tuple([vmem()] * 9),
+        scratch_shapes=[VM((4,) + s, BF) for s in shapes] + [VM(s, BF) for s in shapes] + [VM((3,) + s, BF) for s in shapes] + [
+            VM((4, T, D), BF), VM((T, C), BF), VM((4, C, T), BF), VM((4, T, C), BF), VM((4, T, C), F32), VM((4, T, C), F32),
+            VM((C, T), F32), VM((2, T, D), BF), VM((T, D), BF), VM((T, D), F32), VM((D, C), BF), VM((8, T), F32), VM((3, C, D), F32),
+            VM((8, 3, R, C), BF), VM((8, 3, R, C), BF), VM((3, R, C), BF), VM((2, R, D), BF), VM((8, R, D), BF),
+            VM((24, D), F32), VM((4, 24, D), F32), VM((8, 24, D), F32),
+            dma((3,)), dma((3, 4)), dma((3, 4)), dma((3, 3)), dma((3, 3)), dma((3,)),
+            dma((2, 4)), dma((2, 4)), dma((1,)), dma((1,)), dma((2,)), dma((8,)), dma((3,)), dma((1,)), dma((3,)), dma((3,)),
+            dma((7,)), dma((8,)), dma((3,)), dma((3,)), dma((3,)), dma((3,)), dma((7,)), dma((8,)),
+        ],
+        compiler_params=pltpu.CompilerParams(collective_id=1, has_side_effects=True, vmem_limit_bytes=63 << 20),
+    )(*args)
+
+
+def k3_kernel(
+    layer_in, tokens_in, res_in, small, ag, go, eg, eu, ed,
+    layer_out, tokens_out, res_out, norm_a, norm_f, g_q, g_k, g_v, g_o, router, mixing, proj, cvec, o_gate, o_up, o_down,
+):
+    layer_out[...] = layer_in[...]
+    tokens_out[...] = tokens_in[...]
+    res_out[...] = res_in[...]
+    norm_a[...] = small[15, :]
+    norm_f[...] = small[14, :]
+    for i, out in enumerate((g_q, g_k, g_v)):
+        out[...] = jnp.concatenate([ag[b, i].astype(F32) for b in range(4)], axis=1)
+    g_o[...] = go[...].astype(F32)
+    router[...] = small[0:8, :]
+    mixing[...] = small[16:24, 0:8]
+    proj[...] = small[8:12, :]
+    cvec[...] = small[12:14, :]
+    o_gate[...] = eg[...].astype(F32)
+    o_up[...] = eu[...].astype(F32)
+    o_down[...] = ed[...].astype(F32)
+
+
+def call_k3(*args):
+    T, D = args[0].shape
+    R = D // 8
+    return pl.pallas_call(
+        k3_kernel,
+        name="finish",
+        out_shape=(
+            sds((T, D), BF), sds((T, D), BF), sds((8, T), F32), sds((D,), F32), sds((D,), F32),
+            sds((R, D), F32), sds((R, D), F32), sds((R, D), F32), sds((R, D), F32),
+            sds((8, D), F32), sds((8, 8), F32), sds((4, D), F32), sds((2, D), F32),
+        ) + tuple(sds(a.shape, F32) for a in args[6:9]),
+        in_specs=[vmem()] * 9,
+        out_specs=tuple([vmem()] * 16),
+    )(*args)
+
+
+def body_fast(
+    tokens, gate_res, routes, piece_starts, norm_attn, norm_ffn, w_query, w_key, w_value, w_out, router, mixing,
+    const_proj, const_vec, w_gate, w_up, w_down, cotangent,
+):
+    x, u = tokens[0], cotangent[0]
+    gres, route_ids = gate_res[0].T, routes[0].T
+    (attn_all, q, k, v, o, lse, hidden, aux, place, ret_o, ret_d, wo, wq, gg, gu, gd, fg, fu, fd) = call_k1(
+        x, u, w_query, w_key, w_value, w_out, w_gate[0], w_up[0], w_down[0], gres, route_ids, piece_starts,
+        norm_attn, norm_ffn, router.T, const_proj.T, mixing,
+    )
+    outs = call_k2(
+        ret_o, ret_d, hidden, u, x, aux, place, gres, attn_all, q, k, v, o, lse, wo, wq,
+        norm_attn, norm_ffn, router.T, const_proj.T, mixing, const_vec, piece_starts, gg, gu, gd, fg, fu, fd,
+    )
+    (layer_out, grad_tokens, d_res, norm_a, norm_f, g_q, g_k, g_v, g_o, g_router, g_mixing, g_proj, g_cvec, eg, eu, ed) = call_k3(*outs)
+    return (
+        layer_out[None], grad_tokens[None], d_res.T[None], norm_a, norm_f, g_q, g_k, g_v, g_o,
+        g_router.T, g_mixing, g_proj.T, g_cvec, eg[None], eu[None], ed[None],
+    )
+
+
 def solution(mesh):
     placed = (
         P("fsdp", "exp", None),
@@ -451,7 +1428,7 @@
         P("fsdp", "exp", None),
     )
     return jax.shard_map(
-        body,
+        body_fast if (mesh.shape['exp'], mesh.shape['fsdp']) == (4, 8) else body,
         mesh=mesh,
         in_specs=placed,
         out_specs=(

time: 1320 us -> 326 us (0.25)
  waiting for transfers between devices: 815 us -> 0 us
  Pallas kernels: 0 us -> 325 us
  matrix products: 223 us -> 0 us
  local copies, waits for them, and re-layouts: 107 us -> 0 us
  other arithmetic: 52.3 us -> 0 us
  blocking collectives: 41.5 us -> 0 us
  starting transfers between devices: 34.8 us -> 0 us
  loops' own time: 20.3 us -> 0 us
  between operations: 16.7 us -> 0.67 us
    reduce_scatter x9 -> x0, waiting for transfers between devices: 515 us -> none  [the longest x1 75.1 us: body(): lax.psum_scatter(grad_up_full.astype(jnp.bfloat16), 'fsdp', scatter_dimen...]
    pallas_call x0 -> x3, Pallas kernels: none -> 325 us  [the longest x1 176 us: call_k1(): pl.pallas_call(k1_kernel, name='forward', out_shape=(sds((4, T, D), BF),...]
    all_gather x9 -> x0, waiting for transfers between devices: 248 us -> none  [the longest x1 54.4 us: body(): lax.all_gather(w_gate[0], 'fsdp', axis=0, tiled=True)]
    dot_general x57 -> x0, matrix products: 223 us -> none  [the longest x9 41.4 us: score_block(): jnp.einsum('qhd,khd->hqk', query_heads, key_block, preferred_element_type...]
    psum x1 -> x0, blocking collectives: 41.5 us -> none  [body(): lax.psum((d_norm_attn, d_norm_ffn, d_router, d_mixing, d_const_proj, d_co...]
    all_to_all x4 -> x0, starting transfers between devices: 34.1 us -> none  [the longest x1 18.6 us: body(): lax.all_to_all(d_dispatched.reshape(n_ffn, CAP, model_width), 'exp', spli...]
    psum x1 -> x0, waiting for transfers between devices: 33.6 us -> none  [body(): lax.psum(attn_shards[0].astype(jnp.bfloat16), 'exp').astype(jnp.float32)]
    convert_element_type x8 -> x0, local copies, waits for them, and re-layouts: 26.5 us -> none  [the longest x2 7.49 us: body(): d_expert_rows.reshape(2 * rows_dev, model_width).astype(jnp.bfloat16)]
  transfers between devices with their start and end apart: 23 -> 0, of which waited for: 20 -> 0; matrix products, arithmetic and copies ran while one was open for 14% -> 0% of each run, Pallas kernels for 0% -> 0%
where the time goes in v3:
time: 326 us; the launch traced here: 325 us
  Pallas kernels  325 us (100%)
    pallas_call x1, Pallas kernels, call_k1(): pl.pallas_call(k1_kernel, name='forward', out_shape=(sds((4, T, D), BF),...  176 us
    pallas_call x1, Pallas kernels, call_k2(): pl.pallas_call(k2_kernel, name='backward', out_shape=(sds((T, D), BF), sd...  144 us

profile of v3, /device:TPU:30, one launch (start us, length us, event | category | flops | bytes accessed | tf_op | source)
XLA Modules:
  0.0 325.3 jit_solution(6942204226150646365)
XLA Ops:
  0.6 175.8 %forward.1 = (bf16[4,512,768]{2,1,0:T(8,128)(2,1)}, bf16[4,512,192]{2,1,0:T(8,128)(2,1)}, bf16[4,512,192]{2,1,0:T(8,128)(2,1)}, bf16[4,512,192]{2,1,0:T(8,128)(2...) custom-call(bf16[512,768]{1,0:T(8,128)(2,1)} %bitcast.23, ...), custom_call_target="tpu_custom_call" | custom-call | tf_op jit(solution)/shard_map/forward/pallas_call | solution.py:946
  176.4 144.4 %backward.1 = (bf16[512,768]{1,0:T(8,128)(2,1)}, bf16[512,768]{1,0:T(8,128)(2,1)}, f32[8,512]{1,0:T(8,128)}, f32[24,768]{1,0:T(8,128)}, bf16[4,3,96,192]{3,2,1,0...) custom-call(bf16[4,160,768]{2,1,0:T(8,128)(2,1)} %get-tuple-element., ...), custom_call_target="tpu_custom_call" | custom-call | tf_op jit(solution)/shard_map/backward/pallas_call | solution.py:1329
  320.8 4.4 %finish.1 = (bf16[512,768]{1,0:T(8,128)(2,1)}, bf16[512,768]{1,0:T(8,128)(2,1)}, f32[8,512]{1,0:T(8,128)}, f32[768]{0:T(1024)}, f32[768]{0:T(1024)}, /*index=5*/...) custom-call(bf16[512,768]{1,0:T(8,128)(2,1)} %get-tuple-element.79.l, ...), custom_call_target="tpu_custom_call" | custom-call | tf_op jit(solution)/shard_map/finish/pallas_call | solution.py:1375

commit v4 on v3

--- a/solution.py
+++ b/solution.py
@@ -463,6 +463,9 @@
     def near_first(self, j):
         return (self.e + (j % 2) * (1 - 2 * (self.e % 2)) + 2 * (j // 2)) % 4
 
+    def share_order(self, j):
+        return (self.e + (1 - j % 2) * (1 - 2 * (self.e % 2)) + 2 * (1 - j // 2)) % 4
+
     def barrier(self):
         sem = pltpu.get_barrier_semaphore()
         for p in self.exp_peers:
@@ -505,11 +508,11 @@
     x_ref, u_ref, wq_ref, wk_ref, wv_ref, wo_ref, wg_ref, wu_ref, wd_ref, gres_ref, routes_ref, starts_ref,
     gain_a_ref, gain_f_ref, router_ref, proj_ref, mix_ref,
     attn_all, q_s, k_s, v_s, o_s, lse_s, hidden_ref, aux_ref, place_ref, ret_o, ret_d, wo_full, wq_full,
-    grad_gate, grad_up, grad_down, far_gate, far_up, far_down,
+    grad_gate, grad_up, grad_down, far_gate, next_gate, side_gate, side_up,
     gate_full, up_full, down_full, wq_own, vt_s, attn_recv, nb, snd_r, snd_d, recv_r, recv_d, m_s, l_s, acc_s,
     acc, d_acc, st_gate, st_up, st_down,
     wq_ss, wq_rs, wo_ss, wo_rs, at_ss, at_rs, o_ss, o_rs, dr_ss, dr_rs, dd_ss, dd_rs, ro_ss, ro_rs, rd_ss, rd_rs,
-    us, ur, ds, dr, xs, xr, loc, st_sem, fs, fr,
+    us, ur, ds, dr, xs, xr, vs, vr, wc_ss, wc_rs, loc, st_sem, fs, fr,
 ):
     me = Place()
     e, f, z, xf = me.e, me.f, me.z, me.xf
@@ -528,15 +531,24 @@
 
     me.barrier()
 
-    def rows(ref, index):
-        return ref.at[pl.ds(pl.multiple_of(index * R, 32), R)]
-
-    early = ((wq_own, wq_full, wq_ss, wq_rs, 0), (wo_ref, wo_full, wo_ss, wo_rs, 1))
-    for src, dst, ss, rs, li in early:
+    def half(core):
+        return pl.ds(pl.multiple_of(core * (R // 2), 16), R // 2)
+
+    def wq_slot(index):
+        return wq_full.at[pl.ds(pl.multiple_of(index * R, 32), R)]
+
+    def wo_slot(index):
+        return wo_full.at[index, half(e % 2)]
+
+    early = (
+        (wq_own, wq_slot, wq_ss, wq_rs, 0),
+        (wo_ref.at[half(e % 2)], wo_slot, wo_ss, wo_rs, 1),
+    )
+    for src, slot_of, ss, rs, li in early:
         for d in (1, 3, 2):
-            me.send(src, rows(dst, f), ss.at[d], rs.at[d], f=me.zf(d)).start()
-        me.send(src, rows(dst, f), ss.at[0], rs.at[0], f=xf).start()
-        pltpu.make_async_copy(src, rows(dst, f), loc.at[li]).start()
+            me.send(src, slot_of(f), ss.at[d], rs.at[d], f=me.zf(d)).start()
+        me.send(src, slot_of(f), ss.at[0], rs.at[0], f=xf).start()
+        pltpu.make_async_copy(src, slot_of(f), loc.at[li]).start()
 
     xv = x_ref[...].astype(F32)
     inv = lax.rsqrt(jnp.mean(xv * xv, axis=-1, keepdims=True) + EPS)
@@ -549,27 +561,25 @@
     at_copy(1, e, me.yp).start()
     at_copy(0, e, me.sib).start()
 
-    def early_slot(dst, d, other):
-        return rows(dst, ((z - d + 4) % 4) * 2 + (1 - me.x if other else me.x))
-
-    def early_forward(dst, ss, rs):
+    def early_index(d, other):
+        return ((z - d + 4) % 4) * 2 + (1 - me.x if other else me.x)
+
+    def early_forward(src, slot_of, ss, rs, li):
         for d in (1, 3, 2):
-            slot = early_slot(dst, d, False)
+            slot = slot_of(early_index(d, False))
             me.send(slot, slot, ss.at[d], rs.at[d]).wait_recv()
             me.send(slot, slot, ss.at[3 + d], rs.at[3 + d], f=xf).start()
 
-    def early_wait(src, dst, ss, rs, li):
-        pltpu.make_async_copy(src, rows(dst, f), loc.at[li]).wait()
-        me.send(rows(dst, xf), rows(dst, xf), ss.at[0], rs.at[0]).wait_recv()
+    def early_wait(src, slot_of, ss, rs, li):
+        pltpu.make_async_copy(src, slot_of(f), loc.at[li]).wait()
+        me.send(slot_of(xf), slot_of(xf), ss.at[0], rs.at[0]).wait_recv()
         for d in (1, 2, 3):
-            slot = early_slot(dst, d, True)
+            slot = slot_of(early_index(d, True))
             me.send(slot, slot, ss.at[3 + d], rs.at[3 + d]).wait_recv()
 
-    early_forward(*early[0][1:4])
-
-    units = [(wd_ref, down_full, None)]
-    for c in range(CHUNKS):
-        units += [(wg_ref, gate_full, c), (wu_ref, up_full, c)]
+    def wo_copy(core, to=None):
+        ref = wo_full.at[:, half(core)]
+        return me.send(ref, ref, wc_ss.at[0], wc_rs.at[0], e=to)
 
     def cut(ref, c):
         return ref if c is None else ref.at[:, pl.ds(pl.multiple_of(c * W, W), W)]
@@ -583,49 +593,72 @@
     def x_copy(n, i, src, dst, to=None):
         return me.send(src, dst, xs.at[n, i], xr.at[n, i], f=to)
 
-    def experts(p):
-        for n, (src, full, c) in enumerate(units):
-
-            def at(slot):
-                return cut(full.at[slot], c)
-
+    def relay(n, p, src, full, c):
+        def at(slot):
+            return cut(full.at[slot], c)
+
+        if p == 0:
             own = cut(src, c)
-            if p == 0:
-                x_copy(n, 0, own, at(f), xf).start()
+            x_copy(n, 0, own, at(f), xf).start()
+
+            @pl.when(z <= 2)
+            def _():
+                up_copy(n, 0, own, at(f), f + 2).start()
+
+            @pl.when(z >= 1)
+            def _():
+                down_copy(n, 0, own, at(f), f - 2).start()
+
+            return
+
+        if p == 1 and c is None:
+            x_copy(n, 0, at(xf), at(xf)).wait_recv()
+
+            @pl.when(z <= 2)
+            def _():
+                side_copy(0, at(xf), at(xf), f + 2).start()
+
+            @pl.when(z >= 1)
+            def _():
+                side_copy(1, at(xf), at(xf), f - 2).start()
+
+        @pl.when(z >= p)
+        def _():
+            slot = at(f - 2 * p)
+            up_copy(n, p - 1, slot, slot).wait_recv()
+            if p <= 2:
 
                 @pl.when(z <= 2)
                 def _():
-                    up_copy(n, 0, own, at(f), f + 2).start()
+                    up_copy(n, p, slot, slot, f + 2).start()
+
+            if p > 1 or c is not None:
+                x_copy(n, p, slot, slot, xf).start()
+
+        @pl.when(z + p <= 3)
+        def _():
+            slot = at(f + 2 * p)
+            down_copy(n, p - 1, slot, slot).wait_recv()
+            if p <= 2:
 
                 @pl.when(z >= 1)
                 def _():
-                    down_copy(n, 0, own, at(f), f - 2).start()
-
-            else:
-
-                @pl.when(z >= p)
-                def _():
-                    slot = at(f - 2 * p)
-                    up_copy(n, p - 1, slot, slot).wait_recv()
-                    if p <= 2:
-
-                        @pl.when(z <= 2)
-                        def _():
-                            up_copy(n, p, slot, slot, f + 2).start()
-
-                    x_copy(n, p, slot, slot, xf).start()
-
-                @pl.when(z + p <= 3)
-                def _():
-                    slot = at(f + 2 * p)
-                    down_copy(n, p - 1, slot, slot).wait_recv()
-                    if p <= 2:
-
-                        @pl.when(z >= 1)
-                        def _():
-                            down_copy(n, p, slot, slot, f - 2).start()
-
-                    x_copy(n, 3 + p, slot, slot, xf).start()
+                    down_copy(n, p, slot, slot, f - 2).start()
+
+            if p > 1 or c is not None:
+                x_copy(n, 3 + p, slot, slot, xf).start()
+
+    def side_copy(i, src, dst, to=None):
+        return me.send(src, dst, vs.at[i], vr.at[i], f=to)
+
+    def relay_chunk(p, c):
+        relay(1 + 2 * c, p, wg_ref, gate_full, c)
+        relay(2 + 2 * c, p, wu_ref, up_full, c)
+
+    def experts(p):
+        relay(0, p, wd_ref, down_full, None)
+        for c in range(CHUNKS):
+            relay_chunk(p, c)
 
     own_loads = ((wd_ref, down_full), (wg_ref, gate_full), (wu_ref, up_full))
 
@@ -633,7 +666,10 @@
         src, full = own_loads[i]
         return pltpu.make_async_copy(src, full.at[f], loc.at[2 + i])
 
-    experts(0)
+    relay(0, 0, wd_ref, down_full, None)
+    early_forward(*early[0])
+    for c in range(CHUNKS):
+        relay_chunk(0, c)
     for i in range(3):
         own_load(i).start()
 
@@ -641,7 +677,7 @@
     at_copy(2, me.yp, me.sib).start()
     at_copy(0, me.sib).wait_recv()
     early_wait(*early[0])
-    early_forward(*early[1][1:4])
+    early_forward(*early[1])
     at_copy(2, me.diag).wait_recv()
 
     def qkv_step(i, _):
@@ -705,6 +741,8 @@
     lax.fori_loop(0, 2, query_step, 0)
     o_copy(1, True).start()
     o_copy(2, True).start()
+    early_wait(*early[1])
+    wo_copy(e % 2, me.sib).start()
     experts(1)
     lax.fori_loop(2, 4, query_step, 0)
     o_copy(0, True).start()
@@ -720,7 +758,7 @@
     for k in range(4):
         place_ref[k] = jnp.where(slot_id == count[k : k + 1, :], 1.0, 0.0).astype(BF)
 
-    early_wait(*early[1])
+    wo_copy(1 - e % 2).wait_recv()
     for i in (0, 1, 2):
         o_copy(i).wait_recv()
 
@@ -728,7 +766,7 @@
         r = pl.ds(pl.multiple_of(i * 256, 256), 256)
         h = x_ref[r, :].astype(F32)
         for b in range(4):
-            h = h + dot(attn_recv[b, r, :], wo_full[b * C : (b + 1) * C, :])
+            h = h + dot(attn_recv[b, r, :], wo_full[2 * b : 2 * b + 2].reshape(C, D))
         hidden_ref[r, :] = h
         n = h * lax.rsqrt(jnp.mean(h * h, axis=-1, keepdims=True) + EPS) * gain_f_ref[...].reshape(1, D)
         nb[r, :] = n.astype(BF)
@@ -736,8 +774,10 @@
         aux_ref[8:12, r] = dot(proj_ref[...], n, 1, 1, HIGH)
         return 0
 
+    relay(0, 2, wd_ref, down_full, None)
     lax.fori_loop(0, 2, hidden_step, 0)
-    experts(2)
+    relay_chunk(2, 0)
+    relay_chunk(2, 1)
 
     logits = aux_ref[0:8, :]
     top = jnp.max(jnp.where(chosen, logits, NEG), axis=0, keepdims=True)
@@ -774,10 +814,13 @@
         return 0
 
     lax.fori_loop(0, 4, dispatch_step, 0)
+    relay_chunk(2, 2)
+    relay_chunk(2, 3)
+    relay(0, 3, wd_ref, down_full, None)
+    relay_chunk(3, 0)
     for i, p in enumerate(me.exp_peers):
         d_copy(i, snd_r, recv_r, dr_ss, dr_rs, p).wait()
         d_copy(i, snd_d, recv_d, dd_ss, dd_rs, p).wait()
-    experts(3)
 
     acc[...] = jnp.zeros_like(acc)
     d_acc[...] = jnp.zeros_like(d_acc)
@@ -786,8 +829,19 @@
         def at(slot):
             return cut(full.at[slot], c)
 
-        x_copy(n, 0, at(xf), at(xf)).wait_recv()
-        for p in (1, 2, 3):
+        if c is None:
+
+            @pl.when(z >= 1)
+            def _():
+                side_copy(0, at(xf - 2), at(xf - 2)).wait_recv()
+
+            @pl.when(z <= 2)
+            def _():
+                side_copy(1, at(xf + 2), at(xf + 2)).wait_recv()
+
+        else:
+            x_copy(n, 0, at(xf), at(xf)).wait_recv()
+        for p in (2, 3) if c is None else (1, 2, 3):
 
             @pl.when(z >= p)
             def _():
@@ -812,6 +866,10 @@
         return me.send(snd.at[p], ret.at[e if to else p], ss.at[i], rs.at[i], e=p if to else None)
 
     def expert_step(c, _):
+        @pl.when(c < CHUNKS - 1)
+        def _():
+            relay_chunk(3, c + 1)
+
         @pl.when(c == 0)
         def _():
             for i in range(3):
@@ -868,28 +926,41 @@
     for i in range(3):
         stage_copy(CHUNKS - 1, i).wait()
 
-    far_row = 2 * ((z + 3 - 2 * (z % 2)) % 4) + 1 - me.x
-    far = ((grad_gate, far_gate), (grad_up, far_up), (grad_down, far_down))
-    for i, (src, dst) in enumerate(far):
-        me.send(src.at[far_row], dst, fs.at[i], fr.at[i], f=xf).start()
-
-    for src, dst, ss, rs, li in early:
+    partner = z + 1 - 2 * (z % 2)
+    far_row = 2 * ((partner + 2) % 4) + 1 - me.x
+    next_row = 2 * ((z + 2) % 4) + 1 - me.x
+    side_row = 2 * partner + 1 - me.x
+    far = (
+        (grad_gate.at[far_row], far_gate, xf),
+        (grad_gate.at[side_row], side_gate, 2 * partner + me.x),
+        (grad_gate.at[next_row], next_gate, xf),
+        (grad_up.at[side_row], side_up, 2 * partner + me.x),
+    )
+    for i, (src, dst, to) in enumerate(far):
+        me.send(src, dst, fs.at[i], fr.at[i], f=to).start()
+
+    for src, slot_of, ss, rs, li in early:
         for j in range(7):
-            me.send(rows(dst, f), rows(dst, f), ss.at[j], rs.at[j]).wait_send()
+            me.send(slot_of(f), slot_of(f), ss.at[j], rs.at[j]).wait_send()
+    wo_copy(e % 2).wait_send()
     for i in range(3):
         at_copy(i, e).wait_send()
         o_copy(i).wait_send()
-    for n, (src, full, c) in enumerate(units):
+    def relay_end(n, full, c):
         slot = cut(full.at[f], c)
         x_copy(n, 0, slot, slot).wait_send()
 
         @pl.when(z <= 2)
         def _():
             up_copy(n, 0, slot, slot).wait_send()
+            if c is None:
+                side_copy(0, slot, slot).wait_send()
 
         @pl.when(z >= 1)
         def _():
             down_copy(n, 0, slot, slot).wait_send()
+            if c is None:
+                side_copy(1, slot, slot).wait_send()
 
         for p in (1, 2, 3):
 
@@ -901,7 +972,8 @@
                     def _():
                         up_copy(n, p, slot, slot).wait_send()
 
-                x_copy(n, p, slot, slot).wait_send()
+                if p > 1 or c is not None:
+                    x_copy(n, p, slot, slot).wait_send()
 
             @pl.when(z + p <= 3)
             def _():
@@ -911,13 +983,22 @@
                     def _():
                         down_copy(n, p, slot, slot).wait_send()
 
-                x_copy(n, 3 + p, slot, slot).wait_send()
-
+                if p > 1 or c is not None:
+                    x_copy(n, 3 + p, slot, slot).wait_send()
+
+    relay_end(0, down_full, None)
+
+    def end_step(c, _):
+        relay_end(1 + 2 * c, gate_full, c)
+        relay_end(2 + 2 * c, up_full, c)
+        return 0
+
+    lax.fori_loop(0, CHUNKS, end_step, 0)
     for i in range(3):
         ret_copy(i, snd_r, ret_o, ro_ss, ro_rs).wait()
         ret_copy(i, snd_d, ret_d, rd_ss, rd_rs).wait()
-    for i, (src, dst) in enumerate(far):
-        me.send(src.at[far_row], dst, fs.at[i], fr.at[i]).wait()
+    for i, (src, dst, to) in enumerate(far):
+        me.send(src, dst, fs.at[i], fr.at[i]).wait()
 
 
 def sds(shape, dtype):
@@ -949,12 +1030,12 @@
         out_shape=(
             sds((4, T, D), BF), sds((4, T, C), BF), sds((4, T, C), BF), sds((4, T, C), BF), sds((4, T, C), BF),
             sds((4, 8, T), F32), sds((T, D), F32), sds((16, T), F32), sds((4, CAP, T), BF),
-            sds((4, CAP, D), BF), sds((4, CAP, D), BF), sds((D, D), BF), sds((D, 3 * C), BF),
+            sds((4, CAP, D), BF), sds((4, CAP, D), BF), sds((8, R, D), BF), sds((D, 3 * C), BF),
             sds((8, R, FF), BF), sds((8, R, FF), BF), sds((8, FF // 8, D), BF),
-            sds((R, FF), BF), sds((R, FF), BF), sds((FF // 8, D), BF),
+            sds((R, FF), BF), sds((R, FF), BF), sds((R, FF), BF), sds((R, FF), BF),
         ),
         in_specs=[vmem()] * 5 + [anyspace()] * 4 + [vmem()] * 2 + [smem()] + [vmem()] * 5,
-        out_specs=tuple([vmem()] * 13 + [anyspace()] * 6),
+        out_specs=tuple([vmem()] * 13 + [anyspace()] * 7),
         scratch_shapes=[
             VM((8, R, FF), BF), VM((8, R, FF), BF), VM((8, FF // 8, D), BF), VM((R, 3 * C), BF), VM((4, C, T), BF),
             VM((4, T, C), BF), VM((T, D), BF), block, block, block, block, VM((8, T), F32), VM((8, T), F32), VM((C, T), F32),
@@ -962,7 +1043,7 @@
             dma((7,)), dma((7,)), dma((7,)), dma((7,)),
         ] + [dma((3,))] * 12 + [
             dma((n, 3)), dma((n, 3)), dma((n, 3)), dma((n, 3)), dma((n, 7)), dma((n, 7)),
-            dma((5,)), dma((3,)), dma((3,)), dma((3,)),
+            dma((2,)), dma((2,)), dma((1,)), dma((1,)), dma((5,)), dma((3,)), dma((4,)), dma((4,)),
         ],
         compiler_params=pltpu.CompilerParams(collective_id=0, has_side_effects=True, vmem_limit_bytes=60 << 20),
     )(x, u, wq, wk, wv, wo, wg, wu, wd, gres, routes, starts, gain_a, gain_f, router, proj, mix)
@@ -970,13 +1051,14 @@
 
 def k2_kernel(
     ret_o, ret_d, hidden, u_ref, x_ref, aux_ref, place_ref, gres_ref,
-    attn_all, q_s, k_s, v_s, o_s, lse_s, wo, wqkv, gain_a_ref, gain_f_ref, router_ref, proj_ref, mix_ref, cvec_ref, starts_ref,
-    g_gate, g_up, g_down, far_gate, far_up, far_down,
+    attn_hbm, q_hbm, k_hbm, v_hbm, o_hbm, lse_s, wo_hbm, wqkv_hbm, gain_a_ref, gain_f_ref, router_ref, proj_ref, mix_ref, cvec_ref, starts_ref,
+    g_gate, g_up, g_down, far_gate, next_gate, side_gate, side_up,
     layer_out, grad_tokens, d_res, small_out, ag_out, go_b, eg_out, eu_out, ed_out,
-    xin_g, xin_u, xin_d, own_g, own_u, own_d, zin_g, zin_u, zin_d,
-    dh_all, da, kt_s, dq, dk, dv, dqt, pin, py_in, d_hidden, wk_s, del_r, gt, ag_s, ag_in, ag_fin, go_s, go_in,
+    xin_g, xin_u, xin_d, own_g, own_u, own_d, zin_g, zin_u, zin_d, cross_g, cross_u, cross_d,
+    attn_all, q_s, k_s, v_s, o_s, wo, wqkv,
+    dh_all, da, kt_s, dq, dk, dv, dqt, pin, py_in, d_hidden, wk_s, del_r, gt, go_acc, ag_s, ag_in, ag_fin, go_s, go_in,
     small, sm1, sm2,
-    far_sem, xs, xr, zs, zr, own_sem, dh_ss, dh_rs, fw_ss, fw_rs, go_ss, go_rs, gb_ss, gb_rs, pd_ss, pd_rs, ag_ss, ag_rs,
+    load_sem, late_sem, xs, xr, zs, zr, own_sem, dh_ss, dh_rs, fw_ss, fw_rs, go_ss, go_rs, gb_ss, gb_rs, pd_ss, pd_rs, ag_ss, ag_rs,
     ab_ss, ab_rs, s1_ss, s1_rs, s2_ss, s2_rs,
 ):
     me = Place()
@@ -987,59 +1069,102 @@
     M = 128
 
     partner = z + 1 - 2 * (z % 2)
-    order = ((partner + 2) % 4, (z + 2) % 4, partner, z)
+    targets = ((partner + 2) % 4, (z + 2) % 4, z, partner)
     parts = (
-        (g_gate, xin_g, own_g, zin_g, far_gate, eg_out),
-        (g_up, xin_u, own_u, zin_u, far_up, eu_out),
-        (g_down, xin_d, own_d, zin_d, far_down, ed_out),
-    )
-
-    def far_copy(w):
-        return pltpu.make_async_copy(parts[w][4], parts[w][1].at[0], far_sem.at[w])
-
-    def own_copy(w, i):
-        return pltpu.make_async_copy(parts[w][0].at[2 * order[i] + x], parts[w][2], own_sem.at[w])
+        (g_gate, xin_g, own_g, zin_g, cross_g, eg_out),
+        (g_up, xin_u, own_u, zin_u, cross_u, eu_out),
+        (g_down, xin_d, own_d, zin_d, cross_d, ed_out),
+    )
+
+    def load_copy(i):
+        src, dst = ((far_gate, xin_g.at[0]), (next_gate, xin_g.at[1]), (side_gate, cross_g), (side_up, cross_u))[i]
+        return pltpu.make_async_copy(src, dst, load_sem.at[i])
+
+    def own_copy(w, i, column):
+        return pltpu.make_async_copy(parts[w][0].at[2 * targets[i] + column], parts[w][2], own_sem.at[w])
 
     def x_copy(w, i):
-        return me.send(parts[w][0].at[2 * order[i] + 1 - x], parts[w][1].at[i], xs.at[w, i], xr.at[w, i], f=xf)
+        src = parts[w][4] if i == 2 and w < 2 else parts[w][0].at[2 * targets[i] + 1 - x]
+        dst = parts[w][4] if i == 3 else parts[w][1].at[i]
+        return me.send(src, dst, xs.at[w, i], xr.at[w, i], f=xf)
 
     def z_copy(w, i):
-        to = order[1] if i == 1 else partner
-        return me.send(parts[w][1].at[i], parts[w][3].at[i], zs.at[w, i], zr.at[w, i], f=2 * to + x)
-
-    def x_send(i):
-        for w in range(3):
-            x_copy(w, i).start()
-
-    def rs_mid(i):
-        for w in range(3):
-            xin, own, zin = parts[w][1:4]
-            if i:
-                x_copy(w, i).wait_recv()
-            else:
-                far_copy(w).wait()
-            own_copy(w, i).wait()
-            total = xin[i].astype(F32) + own[...].astype(F32)
-            if i == 1:
-                z_copy(w, 0).wait_recv()
-                total = total + zin[0].astype(F32)
-            if i == 3:
-                z_copy(w, 1).wait_recv()
-                z_copy(w, 2).wait_recv()
-                total = total + zin[1].astype(F32) + zin[2].astype(F32)
-                parts[w][5][...] = total.astype(BF)
-            else:
-                xin[i] = total.astype(BF)
-                z_copy(w, i).start()
-                own_copy(w, i + 1).start()
-
+        if i == 2:
+            src = parts[w][0].at[2 * partner + x] if w < 2 else parts[w][4]
+        else:
+            src = parts[w][1].at[i]
+        to = targets[1] if i == 1 else partner
+        return me.send(src, parts[w][3].at[i], zs.at[w, i], zr.at[w, i], f=2 * to + x)
+
+    def add(dst, *terms):
+        total = dst.astype(F32)
+        for term in terms:
+            total = total + term.astype(F32)
+        return total.astype(BF)
+
+    def rs_far(w):
+        xin, own = parts[w][1:3]
+        if w:
+            x_copy(w, 0).wait_recv()
+        else:
+            load_copy(0).wait()
+        own_copy(w, 0, x).wait()
+        xin[0] = add(xin[0], own[...])
+        z_copy(w, 0).start()
+        own_copy(w, 1, x).start()
+
+    def rs_cross(w):
+        xin, own, zin = parts[w][1:4]
+        if w:
+            x_copy(w, 1).wait_recv()
+        else:
+            load_copy(1).wait()
+        own_copy(w, 1, x).wait()
+        z_copy(w, 0).wait_recv()
+        xin[1] = add(xin[1], own[...], zin[0])
+        z_copy(w, 1).start()
+        if w < 2:
+            own_copy(w, 2, 1 - x).start()
+        else:
+            own_copy(w, 3, x).start()
+
+    def rs_side(w):
+        own, cross = parts[w][2], parts[w][4]
+        if w < 2:
+            load_copy(2 + w).wait()
+            own_copy(w, 2, 1 - x).wait()
+        else:
+            x_copy(w, 3).wait_recv()
+            own_copy(w, 3, x).wait()
+        cross[...] = add(cross[...], own[...])
+        if w < 2:
+            x_copy(w, 2).start()
+        z_copy(w, 2).start()
+        own_copy(w, 2, x).start()
+
+    def rs_end(w):
+        xin, own, zin = parts[w][1:4]
+        x_copy(w, 2).wait_recv()
+        own_copy(w, 2, x).wait()
+        z_copy(w, 1).wait_recv()
+        z_copy(w, 2).wait_recv()
+        parts[w][5][...] = add(xin[2], own[...], zin[1], zin[2])
+
+    for i in range(4):
+        load_copy(i).start()
     for w in range(3):
-        far_copy(w).start()
-        own_copy(w, 0).start()
+        own_copy(w, 0, x).start()
+    late = ((attn_hbm, attn_all), (q_hbm, q_s), (k_hbm, k_s), (v_hbm, v_s), (o_hbm, o_s), (wo_hbm, wo), (wqkv_hbm, wqkv))
+
+    def late_copy(i):
+        return pltpu.make_async_copy(late[i][0], late[i][1], late_sem.at[i])
+
+    for i in (5, 2, 4, 1, 3, 6, 0):
+        late_copy(i).start()
     me.barrier()
-    x_send(1)
-    rs_mid(0)
-    x_send(2)
+    for w, i in ((1, 0), (2, 0), (1, 1), (2, 1), (2, 3), (2, 2)):
+        x_copy(w, i).start()
+    rs_far(0)
 
     small[...] = jnp.zeros_like(small)
     cv0, cv1 = cvec_ref[0:1, :], cvec_ref[1:2, :]
@@ -1105,24 +1230,24 @@
         return 0
 
     lax.fori_loop(0, T // M, mix_step, 0)
-    rs_mid(1)
-    x_send(3)
+    rs_far(1)
+    rs_cross(0)
+    for i in range(7):
+        late_copy(i).wait()
 
     head_of = lane_of((T, C)) // HD
     heads = (row_of((8, C)) == lane_of((8, C)) // HD).astype(F32)
     wk_s[...] = wqkv[:, C : 2 * C]
     dk[...] = jnp.zeros_like(dk)
     dv[...] = jnp.zeros_like(dv)
-    gt[0] = jnp.zeros((C, D), F32)
+    go_acc[...] = jnp.zeros_like(go_acc)
     for b in range(4):
         kt_s[b] = k_s[b].T
 
     def fw_copy(block, to=None):
         return me.send(dh_all.at[block], dh_all.at[block], fw_ss.at[0], fw_rs.at[0], e=to)
 
-    def query_step(j, _):
-        qb = me.near_first(j)
-
+    def d_out_step(j, qb):
         @pl.when(j == 1)
         def _():
             for c in range(T // M):
@@ -1139,73 +1264,98 @@
             fw_copy(me.diag).wait_recv()
 
         dhb = dh_all[qb]
-        low = dot(dhb, wo[pl.ds(pl.multiple_of(e * C, 64), C), :], 1, 1).astype(BF)
-        da[...] = low
+        low = dot(dhb, wo[pl.ds(2 * e, 2)].reshape(C, D), 1, 1).astype(BF)
+        da[qb] = low
         ob = o_s[qb]
-        del_r[...] = dot(heads, low.astype(F32) * ob.astype(F32), 1, 1, HIGH)
-        gt[0] += dot(ob, dhb, 0, 0)
-
-        def pair(kb, h, masked):
+        del_r[qb] = dot(heads, low.astype(F32) * ob.astype(F32), 1, 1, HIGH)
+        go_acc[...] += dot(ob, dhb, 0, 0)
+
+    def head_block(qb, h):
+        hr = pl.ds(pl.multiple_of(h * HD, HD), HD)
+        mine = head_of == h
+
+        def block(kb, masked):
             zero = jnp.zeros((T, C), BF)
-            query = jnp.where(head_of == h, q_s[qb], zero)
-            d_out = jnp.where(head_of == h, da[...], zero)
-            p = jnp.exp2(dot(k_s[kb], query, 1, 1) - lse_s[qb, h : h + 1, :])
+            query = jnp.where(mine, q_s[qb], zero)
+            d_out = jnp.where(mine, da[qb], zero)
+            p = jnp.exp2(dot(k_s[kb], query, 1, 1) - lse_s[qb, pl.ds(h, 1), :])
             if masked:
                 p = jnp.where(allowed_block(T, starts_ref[0, qb] - qb * T), p, 0.0)
             dp = dot(v_s[kb], d_out, 1, 1)
-            dsc = (p * (dp - del_r[h : h + 1, :])).astype(BF)
-            return dot(p.astype(BF), d_out), dot(dsc, query), dot(kt_s[kb, h * HD : (h + 1) * HD, :], dsc)
-
-        def block(kb, masked):
-            r = [pair(kb, h, masked) for h in range(3)]
-            dv[kb] += r[0][0] + r[1][0] + r[2][0]
-            dk[kb] += r[0][1] + r[1][1] + r[2][1]
-            for h in range(3):
-                if masked:
-                    dqt[h * HD : (h + 1) * HD, :] = r[h][2]
-                else:
-                    dqt[h * HD : (h + 1) * HD, :] += r[h][2]
-
-        block(qb, True)
+            dsc = (p * (dp - del_r[qb, pl.ds(h, 1), :])).astype(BF)
+            dv[kb] += dot(p.astype(BF), d_out)
+            dk[kb] += dot(dsc, query)
+            return dot(kt_s[kb, hr, :], dsc)
+
+        dqt[...] = block(qb, True)
 
         def key_step(kb, _):
-            block(kb, False)
+            dqt[...] += block(kb, False)
             return 0
 
         lax.fori_loop(0, qb, key_step, 0)
-        dq[qb] = (dqt[...].T * (1.0 / math.sqrt(HD))).astype(BF)
+        dq[qb, hr, :] = (dqt[...] * (1.0 / math.sqrt(HD))).astype(BF)
+
+    def near_step(i, _):
+        j = i // 3
+        qb = me.near_first(j)
+
+        @pl.when(i % 3 == 0)
+        def _():
+            d_out_step(j, qb)
+
+        head_block(qb, i % 3)
         return 0
 
-    lax.fori_loop(0, 3, query_step, 0)
-    rs_mid(2)
-    lax.fori_loop(3, 4, query_step, 0)
-
-    go_s[0] = gt[0, 0:R, :].astype(BF)
-    go_s[1] = gt[0, R : 2 * R, :].astype(BF)
+    def far_pass(h):
+        def far_step(j, _):
+            qb = me.near_first(j)
+            if h == 0:
+                d_out_step(j, qb)
+            head_block(qb, h)
+            return 0
+
+        lax.fori_loop(2, 4, far_step, 0)
+
+    def ag_copy(h, r, src, dst, to=None):
+        return me.send(src, dst, ag_ss.at[h, r - 1], ag_rs.at[h, r - 1], f=to)
+
+    def weight_grads(h):
+        cols = slice(h * HD, (h + 1) * HD)
+        gt[...] = jnp.zeros_like(gt)
+
+        def grad_step(b, _):
+            low_k = (dk[b, :, cols] * LN2).T.astype(BF)
+            low_v = dv[b, :, cols].T.astype(BF)
+            gt[...] += dot(jnp.concatenate([dq[b, cols, :], low_k, low_v], axis=0), attn_all[b])
+            return 0
+
+        lax.fori_loop(0, 4, grad_step, 0)
+        ag_s[:, h] = gt[...].T.astype(BF).reshape(8, R, C)
+        for r in range(1, 8):
+            ag_copy(h, r, ag_s.at[me.fp(r), h], ag_in.at[r, h], me.fp(r)).start()
+        ag_in[0, h] = ag_s[f, h]
+
+    lax.fori_loop(0, 6, near_step, 0)
+    rs_far(2)
+    far_pass(0)
+    rs_cross(1)
+
+    go_s[0] = go_acc[0:R, :].astype(BF)
+    go_s[1] = go_acc[R : 2 * R, :].astype(BF)
     for j in range(2):
 
         @pl.when(f != 2 * e + j)
         def _():
             me.send(go_s.at[j], go_in.at[f], go_ss.at[j], go_rs.at[f], f=2 * e + j).start()
 
-    def low(b):
-        return dq[b], (dk[b] * LN2).astype(BF), dv[b].astype(BF)
-
-    for i in range(3):
-        gt[i] = jnp.zeros((C, D), F32)
-
-    def grad_step(b, _):
-        a = attn_all[b]
-        for i, part in enumerate(low(b)):
-            gt[i] += dot(part, a, 0, 0)
-        return 0
-
-    lax.fori_loop(0, 4, grad_step, 0)
-    for i in range(3):
-        ag_s[:, i] = gt[i].T.astype(BF).reshape(8, R, C)
-    for r in range(1, 8):
-        me.send(ag_s.at[me.fp(r)], ag_in.at[f], ag_ss.at[r - 1], ag_rs.at[f], f=me.fp(r)).start()
-    ag_in[f] = ag_s[f]
+    weight_grads(0)
+    far_pass(1)
+    weight_grads(1)
+    rs_cross(2)
+    rs_side(0)
+    rs_side(1)
+    far_pass(2)
 
     for c in range(T // M):
         dh_copy(0, c, e).wait_send()
@@ -1213,11 +1363,10 @@
     fw_copy(e).wait_send()
 
     def share_step(j, _):
-        b = (me.sib + 2 * j + (j // 2) * (e - me.sib)) % 4
-        low_q, low_k, low_v = low(b)
-        out = dot(low_q, wqkv[:, 0:C], 1, 1)
-        out = out + dot(low_k, wk_s[...], 1, 1)
-        out = out + dot(low_v, wqkv[:, 2 * C : 3 * C], 1, 1)
+        b = me.share_order(j)
+        out = dot(dq[b], wqkv[:, 0:C], 0, 1)
+        out = out + dot((dk[b] * LN2).astype(BF), wk_s[...], 1, 1)
+        out = out + dot(dv[b].astype(BF), wqkv[:, 2 * C : 3 * C], 1, 1)
         small[15:16, :] += jnp.sum(out * attn_all[b].astype(F32), axis=0, keepdims=True)
         dh_all[b] = out.astype(BF)
         return 0
@@ -1225,14 +1374,18 @@
     def pd_copy(i, src, dst, to=None):
         return me.send(src, dst, pd_ss.at[i], pd_rs.at[i], e=to)
 
-    lax.fori_loop(0, 2, share_step, 0)
+    lax.fori_loop(0, 1, share_step, 0)
     pd_copy(1, dh_all.at[me.diag], pin.at[1], me.sib).start()
+    lax.fori_loop(1, 2, share_step, 0)
+    pd_copy(1, pin.at[1], pin.at[1]).wait_recv()
+    dh_all[me.yp] = add(dh_all[me.yp], pin[1])
+    pd_copy(2, dh_all.at[me.yp], py_in, me.yp).start()
+    weight_grads(2)
+    lax.fori_loop(2, 3, share_step, 0)
     pd_copy(0, dh_all.at[me.sib], pin.at[0], me.sib).start()
-    lax.fori_loop(2, 4, share_step, 0)
-    pd_copy(1, pin.at[1], pin.at[1]).wait_recv()
-    dh_all[me.yp] = (dh_all[me.yp].astype(F32) + pin[1].astype(F32)).astype(BF)
-    pd_copy(2, dh_all.at[me.yp], py_in, me.yp).start()
-
+    lax.fori_loop(3, 4, share_step, 0)
+
+    rs_side(2)
     small[15:16, :] = small[15:16, :] / gain_a_ref[...].reshape(1, D)
     sm1[e] = small[...]
     for i, p in enumerate(me.exp_peers):
@@ -1255,19 +1408,15 @@
     for r in range(1, 8):
         me.send(sm2.at[f], sm2.at[f], s2_ss.at[r - 1], s2_rs.at[f], f=me.fp(r)).start()
 
-    rs_mid(3)
-
-    for r in range(1, 8):
-        s = ag_in.at[me.fp(r)]
-        me.send(s, s, ag_ss.at[r - 1], ag_rs.at[me.fp(r)]).wait_recv()
-    for i in range(3):
-        total = ag_in[0, i].astype(F32)
+    for h in range(3):
+        total = ag_in[0, h].astype(F32)
         for r in range(1, 8):
-            total = total + ag_in[r, i].astype(F32)
-        ag_fin[i] = total.astype(BF)
-    for i, p in enumerate(me.exp_peers):
-        me.send(ag_fin, ag_out.at[e], ab_ss.at[i], ab_rs.at[i], e=p).start()
-    ag_out[e] = ag_fin[...]
+            ag_copy(h, r, ag_in.at[r, h], ag_in.at[r, h]).wait_recv()
+            total = total + ag_in[r, h].astype(F32)
+        ag_fin[h] = total.astype(BF)
+        for i, p in enumerate(me.exp_peers):
+            me.send(ag_fin.at[h], ag_out.at[e, h], ab_ss.at[h, i], ab_rs.at[h, i], e=p).start()
+        ag_out[e, h] = ag_fin[h]
 
     for r in range(1, 8):
         s = sm2.at[me.fp(r)]
@@ -1291,6 +1440,8 @@
         return 0
 
     lax.fori_loop(0, 2, token_step, 0)
+    for w in range(3):
+        rs_end(w)
 
     @pl.when(z != e)
     def _():
@@ -1298,8 +1449,10 @@
 
     for w in range(3):
         for i in range(3):
-            x_copy(w, i + 1).wait_send()
+            if w or i == 2:
+                x_copy(w, i).wait_send()
             z_copy(w, i).wait_send()
+    x_copy(2, 3).wait_send()
     for j in range(2):
 
         @pl.when(f != 2 * e + j)
@@ -1313,14 +1466,17 @@
 
     for i in range(3):
         pd_copy(i, py_in, py_in).wait_send()
-        me.send(ag_fin, ag_out.at[me.exp_peers[i]], ab_ss.at[i], ab_rs.at[i]).wait()
+        for h in range(3):
+            me.send(ag_fin.at[h], ag_out.at[me.exp_peers[i], h], ab_ss.at[h, i], ab_rs.at[h, i]).wait()
     for r in range(1, 8):
-        me.send(ag_s.at[0], ag_in.at[f], ag_ss.at[r - 1], ag_rs.at[f]).wait_send()
+        for h in range(3):
+            ag_copy(h, r, ag_s.at[0, h], ag_in.at[r, h]).wait_send()
         me.send(sm2.at[f], sm2.at[f], s2_ss.at[r - 1], s2_rs.at[f]).wait_send()
 
 
 def call_k2(*args):
     x, (gg, gu, gd) = args[4], args[23:26]
+    late = args[8:13] + args[14:16]
     T, D = x.shape
     C, R = D // 4, D // 8
     dma = pltpu.SemaphoreType.DMA
@@ -1333,16 +1489,16 @@
             sds((T, D), BF), sds((T, D), BF), sds((8, T), F32), sds((24, D), F32),
             sds((4, 3, R, C), BF), sds((R, D), BF),
         ) + tuple(sds(s, BF) for s in shapes),
-        in_specs=[vmem()] * 22 + [smem()] + [anyspace()] * 6,
+        in_specs=[vmem()] * 8 + [anyspace()] * 5 + [vmem()] + [anyspace()] * 2 + [vmem()] * 6 + [smem()] + [anyspace()] * 7,
         out_specs=tuple([vmem()] * 9),
-        scratch_shapes=[VM((4,) + s, BF) for s in shapes] + [VM(s, BF) for s in shapes] + [VM((3,) + s, BF) for s in shapes] + [
-            VM((4, T, D), BF), VM((T, C), BF), VM((4, C, T), BF), VM((4, T, C), BF), VM((4, T, C), F32), VM((4, T, C), F32),
-            VM((C, T), F32), VM((2, T, D), BF), VM((T, D), BF), VM((T, D), F32), VM((D, C), BF), VM((8, T), F32), VM((3, C, D), F32),
+        scratch_shapes=[VM((3,) + s, BF) for s in shapes] + [VM(s, BF) for s in shapes] + [VM((3,) + s, BF) for s in shapes] + [VM(s, BF) for s in shapes] + [VM(a.shape, BF) for a in late] + [
+            VM((4, T, D), BF), VM((4, T, C), BF), VM((4, C, T), BF), VM((4, C, T), BF), VM((4, T, C), F32), VM((4, T, C), F32),
+            VM((HD, T), F32), VM((2, T, D), BF), VM((T, D), BF), VM((T, D), F32), VM((D, C), BF), VM((4, 8, T), F32), VM((C, D), F32), VM((C, D), F32),
             VM((8, 3, R, C), BF), VM((8, 3, R, C), BF), VM((3, R, C), BF), VM((2, R, D), BF), VM((8, R, D), BF),
             VM((24, D), F32), VM((4, 24, D), F32), VM((8, 24, D), F32),
-            dma((3,)), dma((3, 4)), dma((3, 4)), dma((3, 3)), dma((3, 3)), dma((3,)),
+            dma((4,)), dma((7,)), dma((3, 4)), dma((3, 4)), dma((3, 3)), dma((3, 3)), dma((3,)),
             dma((2, 4)), dma((2, 4)), dma((1,)), dma((1,)), dma((2,)), dma((8,)), dma((3,)), dma((1,)), dma((3,)), dma((3,)),
-            dma((7,)), dma((8,)), dma((3,)), dma((3,)), dma((3,)), dma((3,)), dma((7,)), dma((8,)),
+            dma((3, 7)), dma((3, 7)), dma((3, 3)), dma((3, 3)), dma((3,)), dma((3,)), dma((7,)), dma((8,)),
         ],
         compiler_params=pltpu.CompilerParams(collective_id=1, has_side_effects=True, vmem_limit_bytes=63 << 20),
     )(*args)
@@ -1358,7 +1514,9 @@
     norm_a[...] = small[15, :]
     norm_f[...] = small[14, :]
     for i, out in enumerate((g_q, g_k, g_v)):
-        out[...] = jnp.concatenate([ag[b, i].astype(F32) for b in range(4)], axis=1)
+        out[...] = jnp.concatenate(
+            [ag[b, h, :, i * HD : (i + 1) * HD].astype(F32) for b in range(4) for h in range(3)], axis=1
+        )
     g_o[...] = go[...].astype(F32)
     router[...] = small[0:8, :]
     mixing[...] = small[16:24, 0:8]
@@ -1391,13 +1549,13 @@
 ):
     x, u = tokens[0], cotangent[0]
     gres, route_ids = gate_res[0].T, routes[0].T
-    (attn_all, q, k, v, o, lse, hidden, aux, place, ret_o, ret_d, wo, wq, gg, gu, gd, fg, fu, fd) = call_k1(
+    (attn_all, q, k, v, o, lse, hidden, aux, place, ret_o, ret_d, wo, wq, gg, gu, gd, fg, ng, sg, su) = call_k1(
         x, u, w_query, w_key, w_value, w_out, w_gate[0], w_up[0], w_down[0], gres, route_ids, piece_starts,
         norm_attn, norm_ffn, router.T, const_proj.T, mixing,
     )
     outs = call_k2(
         ret_o, ret_d, hidden, u, x, aux, place, gres, attn_all, q, k, v, o, lse, wo, wq,
-        norm_attn, norm_ffn, router.T, const_proj.T, mixing, const_vec, piece_starts, gg, gu, gd, fg, fu, fd,
+        norm_attn, norm_ffn, router.T, const_proj.T, mixing, const_vec, piece_starts, gg, gu, gd, fg, ng, sg, su,
     )
     (layer_out, grad_tokens, d_res, norm_a, norm_f, g_q, g_k, g_v, g_o, g_router, g_mixing, g_proj, g_cvec, eg, eu, ed) = call_k3(*outs)
     return (

time: 326 us -> 293 us (0.90)
  Pallas kernels: 325 us -> 292 us
    pallas_call x1, Pallas kernels: 176 us -> 153 us  [call_k1(): pl.pallas_call(k1_kernel, name='forward', out_shape=(sds((4, T, D), BF),...]
    pallas_call x1, Pallas kernels: 144 us -> 135 us  [call_k2(): pl.pallas_call(k2_kernel, name='backward', out_shape=(sds((T, D), BF), sd...]
where the time goes in v4:
time: 293 us
  Pallas kernels  292 us (100%)
    pallas_call x1, Pallas kernels, call_k1(): pl.pallas_call(k1_kernel, name='forward', out_shape=(sds((4, T, D), BF),...  153 us
    pallas_call x1, Pallas kernels, call_k2(): pl.pallas_call(k2_kernel, name='backward', out_shape=(sds((T, D), BF), sd...  135 us

profile of v4, /device:TPU:30, one launch (start us, length us, event | category | flops | bytes accessed | tf_op | source)
XLA Modules:
  0.0 292.6 jit_solution(2235459062546313726)
XLA Ops:
  0.6 152.9 %forward.1 = (bf16[4,512,768]{2,1,0:T(8,128)(2,1)}, bf16[4,512,192]{2,1,0:T(8,128)(2,1)}, bf16[4,512,192]{2,1,0:T(8,128)(2,1)}, bf16[4,512,192]{2,1,0:T(8,128)(2...) custom-call(bf16[512,768]{1,0:T(8,128)(2,1)} %bitcast.23, ...), custom_call_target="tpu_custom_call" | custom-call | tf_op jit(solution)/shard_map/forward/pallas_call | solution.py:1027
  153.6 134.6 %backward.1 = (bf16[512,768]{1,0:T(8,128)(2,1)}, bf16[512,768]{1,0:T(8,128)(2,1)}, f32[8,512]{1,0:T(8,128)}, f32[24,768]{1,0:T(8,128)}, bf16[4,3,96,192]{3,2,1,0...) custom-call(bf16[4,160,768]{2,1,0:T(8,128)(2,1)} %get-tuple-element., ...), custom_call_target="tpu_custom_call" | custom-call | tf_op jit(solution)/shard_map/backward/pallas_call | solution.py:1485
  288.1 4.4 %finish.1 = (bf16[512,768]{1,0:T(8,128)(2,1)}, bf16[512,768]{1,0:T(8,128)(2,1)}, f32[8,512]{1,0:T(8,128)}, f32[768]{0:T(1024)}, f32[768]{0:T(1024)}, /*index=5*/...) custom-call(bf16[512,768]{1,0:T(8,128)(2,1)} %get-tuple-element.81.l, ...), custom_call_target="tpu_custom_call" | custom-call | tf_op jit(solution)/shard_map/finish/pallas_call | solution.py:1533

commit v5 on v4

--- a/solution.py
+++ b/solution.py
@@ -507,12 +507,13 @@
 def k1_kernel(
     x_ref, u_ref, wq_ref, wk_ref, wv_ref, wo_ref, wg_ref, wu_ref, wd_ref, gres_ref, routes_ref, starts_ref,
     gain_a_ref, gain_f_ref, router_ref, proj_ref, mix_ref,
-    attn_all, q_s, k_s, v_s, o_s, lse_s, hidden_ref, aux_ref, place_ref, ret_o, ret_d, wo_full, wq_full,
-    grad_gate, grad_up, grad_down, far_gate, next_gate, side_gate, side_up,
+    attn_hbm, q_hbm, k_hbm, v_hbm, o_hbm, lse_s, hidden_ref, aux_ref, place_ref, ret_o, ret_d, wo_hbm, wq_hbm,
+    grad_gate, grad_up, grad_down, far_gate, next_gate, near_gate, side_gate, far_up, side_up,
+    attn_all, q_s, k_s, v_s, o_s, wo_full, wq_full,
     gate_full, up_full, down_full, wq_own, vt_s, attn_recv, nb, snd_r, snd_d, recv_r, recv_d, m_s, l_s, acc_s,
     acc, d_acc, st_gate, st_up, st_down,
     wq_ss, wq_rs, wo_ss, wo_rs, at_ss, at_rs, o_ss, o_rs, dr_ss, dr_rs, dd_ss, dd_rs, ro_ss, ro_rs, rd_ss, rd_rs,
-    us, ur, ds, dr, xs, xr, vs, vr, wc_ss, wc_rs, loc, st_sem, fs, fr,
+    us, ur, ds, dr, xs, xr, vs, vr, wc_ss, wc_rs, loc, st_sem, fs, fr, keep_sem,
 ):
     me = Place()
     e, f, z, xf = me.e, me.f, me.z, me.xf
@@ -680,6 +681,16 @@
     early_forward(*early[1])
     at_copy(2, me.diag).wait_recv()
 
+    kept = (
+        (attn_all, attn_hbm), (wq_full, wq_hbm), (q_s, q_hbm), (k_s, k_hbm), (v_s, v_hbm), (wo_full, wo_hbm), (o_s, o_hbm),
+    )
+
+    def keep_copy(i):
+        return pltpu.make_async_copy(kept[i][0], kept[i][1], keep_sem.at[i])
+
+    keep_copy(0).start()
+    keep_copy(1).start()
+
     def qkv_step(i, _):
         b = i // 2
         r = pl.ds(pl.multiple_of((i % 2) * 256, 256), 256)
@@ -692,6 +703,8 @@
         return 0
 
     lax.fori_loop(0, 8, qkv_step, 0)
+    for i in (2, 3, 4):
+        keep_copy(i).start()
 
     head_of = lane_of((T, C)) // HD
     lse_s[...] = jnp.zeros_like(lse_s)
@@ -747,6 +760,7 @@
     lax.fori_loop(2, 4, query_step, 0)
     o_copy(0, True).start()
     attn_recv[e] = o_s[e]
+    keep_copy(6).start()
 
     r0, r1 = routes_ref[0:1, :], routes_ref[1:2, :]
     expert = row_of((8, T))
@@ -759,6 +773,7 @@
         place_ref[k] = jnp.where(slot_id == count[k : k + 1, :], 1.0, 0.0).astype(BF)
 
     wo_copy(1 - e % 2).wait_recv()
+    keep_copy(5).start()
     for i in (0, 1, 2):
         o_copy(i).wait_recv()
 
@@ -821,6 +836,28 @@
     for i, p in enumerate(me.exp_peers):
         d_copy(i, snd_r, recv_r, dr_ss, dr_rs, p).wait()
         d_copy(i, snd_d, recv_d, dd_ss, dd_rs, p).wait()
+
+    partner = z + 1 - 2 * (z % 2)
+    far_row = 2 * ((partner + 2) % 4) + 1 - me.x
+    next_row = 2 * ((z + 2) % 4) + 1 - me.x
+    side_row = 2 * partner + 1 - me.x
+    near_row = 2 * partner + me.x
+    first = (
+        (grad_gate, far_row, far_gate, xf),
+        (grad_gate, side_row, side_gate, near_row),
+        (grad_up, far_row, far_up, xf),
+        (grad_up, side_row, side_up, near_row),
+        (grad_gate, next_row, next_gate, xf),
+        (grad_gate, near_row, near_gate, near_row),
+    )
+
+    def first_copy(i, c, to=None):
+        src, row, dst, _ = first[i]
+        return me.send(cut(src.at[row], c), cut(dst, c), fs.at[i, c], fr.at[i, c], f=to)
+
+    def first_send(c):
+        for i in range(6):
+            first_copy(i, c, first[i][3]).start()
 
     acc[...] = jnp.zeros_like(acc)
     d_acc[...] = jnp.zeros_like(d_acc)
@@ -914,6 +951,7 @@
         def _():
             for i in range(3):
                 stage_copy(c - 1, i).wait()
+            first_send(c - 1)
 
         st_down[...] = dot(inner, d_in, 0, 0).astype(BF).reshape(2, W // 2, D)
         st_gate[...] = dot(row_in, d_gate, 0, 0).astype(BF).reshape(8, R, W)
@@ -925,19 +963,7 @@
     lax.fori_loop(0, CHUNKS, expert_step, 0)
     for i in range(3):
         stage_copy(CHUNKS - 1, i).wait()
-
-    partner = z + 1 - 2 * (z % 2)
-    far_row = 2 * ((partner + 2) % 4) + 1 - me.x
-    next_row = 2 * ((z + 2) % 4) + 1 - me.x
-    side_row = 2 * partner + 1 - me.x
-    far = (
-        (grad_gate.at[far_row], far_gate, xf),
-        (grad_gate.at[side_row], side_gate, 2 * partner + me.x),
-        (grad_gate.at[next_row], next_gate, xf),
-        (grad_up.at[side_row], side_up, 2 * partner + me.x),
-    )
-    for i, (src, dst, to) in enumerate(far):
-        me.send(src, dst, fs.at[i], fr.at[i], f=to).start()
+    first_send(CHUNKS - 1)
 
     for src, slot_of, ss, rs, li in early:
         for j in range(7):
@@ -997,8 +1023,15 @@
     for i in range(3):
         ret_copy(i, snd_r, ret_o, ro_ss, ro_rs).wait()
         ret_copy(i, snd_d, ret_d, rd_ss, rd_rs).wait()
-    for i, (src, dst, to) in enumerate(far):
-        me.send(src, dst, fs.at[i], fr.at[i]).wait()
+
+    def first_end(c, _):
+        for i in range(6):
+            first_copy(i, c).wait()
+        return 0
+
+    lax.fori_loop(0, CHUNKS, first_end, 0)
+    for i in range(7):
+        keep_copy(i).wait()
 
 
 def sds(shape, dtype):
@@ -1032,18 +1065,19 @@
             sds((4, 8, T), F32), sds((T, D), F32), sds((16, T), F32), sds((4, CAP, T), BF),
             sds((4, CAP, D), BF), sds((4, CAP, D), BF), sds((8, R, D), BF), sds((D, 3 * C), BF),
             sds((8, R, FF), BF), sds((8, R, FF), BF), sds((8, FF // 8, D), BF),
-            sds((R, FF), BF), sds((R, FF), BF), sds((R, FF), BF), sds((R, FF), BF),
+            sds((R, FF), BF), sds((R, FF), BF), sds((R, FF), BF), sds((R, FF), BF), sds((R, FF), BF), sds((R, FF), BF),
         ),
         in_specs=[vmem()] * 5 + [anyspace()] * 4 + [vmem()] * 2 + [smem()] + [vmem()] * 5,
-        out_specs=tuple([vmem()] * 13 + [anyspace()] * 7),
+        out_specs=tuple([anyspace()] * 5 + [vmem()] * 6 + [anyspace()] * 11),
         scratch_shapes=[
+            VM((4, T, D), BF), VM((4, T, C), BF), VM((4, T, C), BF), VM((4, T, C), BF), VM((4, T, C), BF), VM((8, R, D), BF), VM((D, 3 * C), BF),
             VM((8, R, FF), BF), VM((8, R, FF), BF), VM((8, FF // 8, D), BF), VM((R, 3 * C), BF), VM((4, C, T), BF),
             VM((4, T, C), BF), VM((T, D), BF), block, block, block, block, VM((8, T), F32), VM((8, T), F32), VM((C, T), F32),
             VM((S, D), F32), VM((S, D), F32), VM((8, R, FF // CHUNKS), BF), VM((8, R, FF // CHUNKS), BF), VM((2, FF // 8, D), BF),
             dma((7,)), dma((7,)), dma((7,)), dma((7,)),
         ] + [dma((3,))] * 12 + [
             dma((n, 3)), dma((n, 3)), dma((n, 3)), dma((n, 3)), dma((n, 7)), dma((n, 7)),
-            dma((2,)), dma((2,)), dma((1,)), dma((1,)), dma((5,)), dma((3,)), dma((4,)), dma((4,)),
+            dma((2,)), dma((2,)), dma((1,)), dma((1,)), dma((5,)), dma((3,)), dma((6, CHUNKS)), dma((6, CHUNKS)), dma((7,)),
         ],
         compiler_params=pltpu.CompilerParams(collective_id=0, has_side_effects=True, vmem_limit_bytes=60 << 20),
     )(x, u, wq, wk, wv, wo, wg, wu, wd, gres, routes, starts, gain_a, gain_f, router, proj, mix)
@@ -1052,13 +1086,13 @@
 def k2_kernel(
     ret_o, ret_d, hidden, u_ref, x_ref, aux_ref, place_ref, gres_ref,
     attn_hbm, q_hbm, k_hbm, v_hbm, o_hbm, lse_s, wo_hbm, wqkv_hbm, gain_a_ref, gain_f_ref, router_ref, proj_ref, mix_ref, cvec_ref, starts_ref,
-    g_gate, g_up, g_down, far_gate, next_gate, side_gate, side_up,
+    g_gate, g_up, g_down, far_gate, next_gate, near_gate, side_gate, far_up, side_up,
     layer_out, grad_tokens, d_res, small_out, ag_out, go_b, eg_out, eu_out, ed_out,
     xin_g, xin_u, xin_d, own_g, own_u, own_d, zin_g, zin_u, zin_d, cross_g, cross_u, cross_d,
     attn_all, q_s, k_s, v_s, o_s, wo, wqkv,
-    dh_all, da, kt_s, dq, dk, dv, dqt, pin, py_in, d_hidden, wk_s, del_r, gt, go_acc, ag_s, ag_in, ag_fin, go_s, go_in,
+    dh_all, da, kt_s, dq, dk, dv, dqt, pin, py_in, d_hidden, wk_s, del_r, gt, go_acc, ag_s, bx_in, bz_in, ag_fin, go_s, go_in,
     small, sm1, sm2,
-    load_sem, late_sem, xs, xr, zs, zr, own_sem, dh_ss, dh_rs, fw_ss, fw_rs, go_ss, go_rs, gb_ss, gb_rs, pd_ss, pd_rs, ag_ss, ag_rs,
+    load_sem, late_sem, xs, xr, zs, zr, own_sem, dh_ss, dh_rs, fw_ss, fw_rs, go_ss, go_rs, gb_ss, gb_rs, pd_ss, pd_rs, bx_ss, bx_rs, bz_ss, bz_rs,
     ab_ss, ab_rs, s1_ss, s1_rs, s2_ss, s2_rs,
 ):
     me = Place()
@@ -1077,7 +1111,10 @@
     )
 
     def load_copy(i):
-        src, dst = ((far_gate, xin_g.at[0]), (next_gate, xin_g.at[1]), (side_gate, cross_g), (side_up, cross_u))[i]
+        src, dst = (
+            (far_gate, xin_g.at[0]), (far_up, xin_u.at[0]), (next_gate, xin_g.at[1]),
+            (side_gate, cross_g), (side_up, cross_u), (near_gate, zin_g.at[2]),
+        )[i]
         return pltpu.make_async_copy(src, dst, load_sem.at[i])
 
     def own_copy(w, i, column):
@@ -1104,10 +1141,10 @@
 
     def rs_far(w):
         xin, own = parts[w][1:3]
-        if w:
+        if w == 2:
             x_copy(w, 0).wait_recv()
         else:
-            load_copy(0).wait()
+            load_copy(w).wait()
         own_copy(w, 0, x).wait()
         xin[0] = add(xin[0], own[...])
         z_copy(w, 0).start()
@@ -1118,7 +1155,7 @@
         if w:
             x_copy(w, 1).wait_recv()
         else:
-            load_copy(1).wait()
+            load_copy(2).wait()
         own_copy(w, 1, x).wait()
         z_copy(w, 0).wait_recv()
         xin[1] = add(xin[1], own[...], zin[0])
@@ -1131,15 +1168,14 @@
     def rs_side(w):
         own, cross = parts[w][2], parts[w][4]
         if w < 2:
-            load_copy(2 + w).wait()
+            load_copy(3 + w).wait()
             own_copy(w, 2, 1 - x).wait()
         else:
             x_copy(w, 3).wait_recv()
             own_copy(w, 3, x).wait()
         cross[...] = add(cross[...], own[...])
-        if w < 2:
-            x_copy(w, 2).start()
-        z_copy(w, 2).start()
+        if w:
+            z_copy(w, 2).start()
         own_copy(w, 2, x).start()
 
     def rs_end(w):
@@ -1147,10 +1183,13 @@
         x_copy(w, 2).wait_recv()
         own_copy(w, 2, x).wait()
         z_copy(w, 1).wait_recv()
-        z_copy(w, 2).wait_recv()
+        if w:
+            z_copy(w, 2).wait_recv()
+        else:
+            load_copy(5).wait()
         parts[w][5][...] = add(xin[2], own[...], zin[1], zin[2])
 
-    for i in range(4):
+    for i in range(6):
         load_copy(i).start()
     for w in range(3):
         own_copy(w, 0, x).start()
@@ -1162,9 +1201,10 @@
     for i in (5, 2, 4, 1, 3, 6, 0):
         late_copy(i).start()
     me.barrier()
-    for w, i in ((1, 0), (2, 0), (1, 1), (2, 1), (2, 3), (2, 2)):
+    for w, i in ((2, 0), (1, 1), (2, 1)):
         x_copy(w, i).start()
     rs_far(0)
+    rs_far(1)
 
     small[...] = jnp.zeros_like(small)
     cv0, cv1 = cvec_ref[0:1, :], cvec_ref[1:2, :]
@@ -1230,7 +1270,6 @@
         return 0
 
     lax.fori_loop(0, T // M, mix_step, 0)
-    rs_far(1)
     rs_cross(0)
     for i in range(7):
         late_copy(i).wait()
@@ -1317,8 +1356,14 @@
 
         lax.fori_loop(2, 4, far_step, 0)
 
-    def ag_copy(h, r, src, dst, to=None):
-        return me.send(src, dst, ag_ss.at[h, r - 1], ag_rs.at[h, r - 1], f=to)
+    def bx_copy(h, to=None):
+        return me.send(ag_s.at[1 - x, h], bx_in.at[h], bx_ss.at[h], bx_rs.at[h], f=to)
+
+    def bz_copy(h, d, to=None):
+        return me.send(bx_in.at[h, (z + d) % 4], bz_in.at[h, d - 1], bz_ss.at[h, d - 1], bz_rs.at[h, d - 1], f=to)
+
+    def ab_copy(h, i, to=None):
+        return me.send(ag_fin.at[h], ag_out.at[e if to is not None else me.exp_peers[i], h], ab_ss.at[h, i], ab_rs.at[h, i], e=to)
 
     def weight_grads(h):
         cols = slice(h * HD, (h + 1) * HD)
@@ -1331,10 +1376,26 @@
             return 0
 
         lax.fori_loop(0, 4, grad_step, 0)
-        ag_s[:, h] = gt[...].T.astype(BF).reshape(8, R, C)
-        for r in range(1, 8):
-            ag_copy(h, r, ag_s.at[me.fp(r), h], ag_in.at[r, h], me.fp(r)).start()
-        ag_in[0, h] = ag_s[f, h]
+        grads = gt[...].T.astype(BF).reshape(8, R, C)
+        for k in range(8):
+            ag_s[k % 2, h, k // 2] = grads[k]
+        bx_copy(h, xf).start()
+
+    def weight_rows(h):
+        bx_copy(h).wait_recv()
+        bx_in[h] = add(bx_in[h], ag_s[x, h])
+        for d in (2, 1, 3):
+            bz_copy(h, d, me.zf(d)).start()
+
+    def weight_sum(h):
+        total = bx_in[h, z].astype(F32)
+        for d in (1, 2, 3):
+            bz_copy(h, d).wait_recv()
+            total = total + bz_in[h, d - 1].astype(F32)
+        ag_fin[h] = total.astype(BF)
+        for i, p in enumerate(me.exp_peers):
+            ab_copy(h, i, p).start()
+        ag_out[e, h] = ag_fin[h]
 
     lax.fori_loop(0, 6, near_step, 0)
     rs_far(2)
@@ -1350,8 +1411,11 @@
             me.send(go_s.at[j], go_in.at[f], go_ss.at[j], go_rs.at[f], f=2 * e + j).start()
 
     weight_grads(0)
+    x_copy(2, 3).start()
     far_pass(1)
     weight_grads(1)
+    x_copy(2, 2).start()
+    weight_rows(0)
     rs_cross(2)
     rs_side(0)
     rs_side(1)
@@ -1381,15 +1445,25 @@
     dh_all[me.yp] = add(dh_all[me.yp], pin[1])
     pd_copy(2, dh_all.at[me.yp], py_in, me.yp).start()
     weight_grads(2)
+    x_copy(0, 2).start()
+    x_copy(1, 2).start()
     lax.fori_loop(2, 3, share_step, 0)
     pd_copy(0, dh_all.at[me.sib], pin.at[0], me.sib).start()
     lax.fori_loop(3, 4, share_step, 0)
 
+    small[15:16, :] = small[15:16, :] / gain_a_ref[...].reshape(1, D)
+    sm1[e] = small[...].astype(BF)
+    for i, p in enumerate(me.exp_peers):
+        me.send(sm1.at[e], sm1.at[e], s1_ss.at[i], s1_rs.at[i], e=p).start()
+    weight_rows(1)
     rs_side(2)
-    small[15:16, :] = small[15:16, :] / gain_a_ref[...].reshape(1, D)
-    sm1[e] = small[...]
+    weight_sum(0)
     for i, p in enumerate(me.exp_peers):
-        me.send(small, sm1.at[e], s1_ss.at[i], s1_rs.at[i], e=p).start()
+        me.send(sm1.at[p], sm1.at[p], s1_ss.at[i], s1_rs.at[i]).wait()
+    sm2[f] = add(sm1[0], sm1[1], sm1[2], sm1[3])
+    for r in range(1, 8):
+        me.send(sm2.at[f], sm2.at[f], s2_ss.at[r - 1], s2_rs.at[f], f=me.fp(r)).start()
+    weight_rows(2)
 
     @pl.when(z == e)
     def _():
@@ -1402,28 +1476,14 @@
         for i, p in enumerate(me.exp_peers):
             me.send(go_b, go_b, gb_ss.at[i], gb_rs.at[0], e=p).start()
 
-    for i, p in enumerate(me.exp_peers):
-        me.send(small, sm1.at[p], s1_ss.at[i], s1_rs.at[i]).wait()
-    sm2[f] = sm1[0] + sm1[1] + sm1[2] + sm1[3]
-    for r in range(1, 8):
-        me.send(sm2.at[f], sm2.at[f], s2_ss.at[r - 1], s2_rs.at[f], f=me.fp(r)).start()
-
-    for h in range(3):
-        total = ag_in[0, h].astype(F32)
-        for r in range(1, 8):
-            ag_copy(h, r, ag_in.at[r, h], ag_in.at[r, h]).wait_recv()
-            total = total + ag_in[r, h].astype(F32)
-        ag_fin[h] = total.astype(BF)
-        for i, p in enumerate(me.exp_peers):
-            me.send(ag_fin.at[h], ag_out.at[e, h], ab_ss.at[h, i], ab_rs.at[h, i], e=p).start()
-        ag_out[e, h] = ag_fin[h]
-
+    weight_sum(1)
+    weight_sum(2)
     for r in range(1, 8):
         s = sm2.at[me.fp(r)]
         me.send(s, s, s2_ss.at[r - 1], s2_rs.at[me.fp(r)]).wait_recv()
-    total = sm2[0]
+    total = sm2[0].astype(F32)
     for r in range(1, 8):
-        total = total + sm2[r]
+        total = total + sm2[r].astype(F32)
     small_out[...] = total
 
     pd_copy(0, pin.at[0], pin.at[0]).wait_recv()
@@ -1449,9 +1509,10 @@
 
     for w in range(3):
         for i in range(3):
-            if w or i == 2:
+            if (w, i) not in ((0, 0), (0, 1), (1, 0)):
                 x_copy(w, i).wait_send()
-            z_copy(w, i).wait_send()
+            if (w, i) != (0, 2):
+                z_copy(w, i).wait_send()
     x_copy(2, 3).wait_send()
     for j in range(2):
 
@@ -1467,10 +1528,12 @@
     for i in range(3):
         pd_copy(i, py_in, py_in).wait_send()
         for h in range(3):
-            me.send(ag_fin.at[h], ag_out.at[me.exp_peers[i], h], ab_ss.at[h, i], ab_rs.at[h, i]).wait()
+            ab_copy(h, i).wait()
+    for h in range(3):
+        bx_copy(h).wait_send()
+        for d in (1, 2, 3):
+            bz_copy(h, d).wait_send()
     for r in range(1, 8):
-        for h in range(3):
-            ag_copy(h, r, ag_s.at[0, h], ag_in.at[r, h]).wait_send()
         me.send(sm2.at[f], sm2.at[f], s2_ss.at[r - 1], s2_rs.at[f]).wait_send()
 
 
@@ -1489,16 +1552,16 @@
             sds((T, D), BF), sds((T, D), BF), sds((8, T), F32), sds((24, D), F32),
             sds((4, 3, R, C), BF), sds((R, D), BF),
         ) + tuple(sds(s, BF) for s in shapes),
-        in_specs=[vmem()] * 8 + [anyspace()] * 5 + [vmem()] + [anyspace()] * 2 + [vmem()] * 6 + [smem()] + [anyspace()] * 7,
+        in_specs=[vmem()] * 8 + [anyspace()] * 5 + [vmem()] + [anyspace()] * 2 + [vmem()] * 6 + [smem()] + [anyspace()] * 9,
         out_specs=tuple([vmem()] * 9),
         scratch_shapes=[VM((3,) + s, BF) for s in shapes] + [VM(s, BF) for s in shapes] + [VM((3,) + s, BF) for s in shapes] + [VM(s, BF) for s in shapes] + [VM(a.shape, BF) for a in late] + [
             VM((4, T, D), BF), VM((4, T, C), BF), VM((4, C, T), BF), VM((4, C, T), BF), VM((4, T, C), F32), VM((4, T, C), F32),
             VM((HD, T), F32), VM((2, T, D), BF), VM((T, D), BF), VM((T, D), F32), VM((D, C), BF), VM((4, 8, T), F32), VM((C, D), F32), VM((C, D), F32),
-            VM((8, 3, R, C), BF), VM((8, 3, R, C), BF), VM((3, R, C), BF), VM((2, R, D), BF), VM((8, R, D), BF),
-            VM((24, D), F32), VM((4, 24, D), F32), VM((8, 24, D), F32),
-            dma((4,)), dma((7,)), dma((3, 4)), dma((3, 4)), dma((3, 3)), dma((3, 3)), dma((3,)),
+            VM((2, 3, 4, R, C), BF), VM((3, 4, R, C), BF), VM((3, 3, R, C), BF), VM((3, R, C), BF), VM((2, R, D), BF), VM((8, R, D), BF),
+            VM((24, D), F32), VM((4, 24, D), BF), VM((8, 24, D), BF),
+            dma((6,)), dma((7,)), dma((3, 4)), dma((3, 4)), dma((3, 3)), dma((3, 3)), dma((3,)),
             dma((2, 4)), dma((2, 4)), dma((1,)), dma((1,)), dma((2,)), dma((8,)), dma((3,)), dma((1,)), dma((3,)), dma((3,)),
-            dma((3, 7)), dma((3, 7)), dma((3, 3)), dma((3, 3)), dma((3,)), dma((3,)), dma((7,)), dma((8,)),
+            dma((3,)), dma((3,)), dma((3, 3)), dma((3, 3)), dma((3, 3)), dma((3, 3)), dma((3,)), dma((3,)), dma((7,)), dma((8,)),
         ],
         compiler_params=pltpu.CompilerParams(collective_id=1, has_side_effects=True, vmem_limit_bytes=63 << 20),
     )(*args)
@@ -1549,13 +1612,13 @@
 ):
     x, u = tokens[0], cotangent[0]
     gres, route_ids = gate_res[0].T, routes[0].T
-    (attn_all, q, k, v, o, lse, hidden, aux, place, ret_o, ret_d, wo, wq, gg, gu, gd, fg, ng, sg, su) = call_k1(
+    (attn_all, q, k, v, o, lse, hidden, aux, place, ret_o, ret_d, wo, wq, gg, gu, gd, fg, ng, eg1, sg, fu, su) = call_k1(
         x, u, w_query, w_key, w_value, w_out, w_gate[0], w_up[0], w_down[0], gres, route_ids, piece_starts,
         norm_attn, norm_ffn, router.T, const_proj.T, mixing,
     )
     outs = call_k2(
         ret_o, ret_d, hidden, u, x, aux, place, gres, attn_all, q, k, v, o, lse, wo, wq,
-        norm_attn, norm_ffn, router.T, const_proj.T, mixing, const_vec, piece_starts, gg, gu, gd, fg, ng, sg, su,
+        norm_attn, norm_ffn, router.T, const_proj.T, mixing, const_vec, piece_starts, gg, gu, gd, fg, ng, eg1, sg, fu, su,
     )
     (layer_out, grad_tokens, d_res, norm_a, norm_f, g_q, g_k, g_v, g_o, g_router, g_mixing, g_proj, g_cvec, eg, eu, ed) = call_k3(*outs)
     return (

time: 293 us -> 275 us (0.939)
  Pallas kernels: 292 us -> 271 us
    pallas_call x1, Pallas kernels: 135 us -> 119 us  [call_k2(): pl.pallas_call(k2_kernel, name='backward', out_shape=(sds((T, D), BF), sd...]
    pallas_call x1, Pallas kernels: 153 us -> 148 us  [call_k1(): pl.pallas_call(k1_kernel, name='forward', out_shape=(sds((4, T, D), BF),...]
where the time goes in v5:
time: 275 us; the launch traced here: 272 us
  Pallas kernels  271 us (99%)
    pallas_call x1, Pallas kernels, call_k1(): pl.pallas_call(k1_kernel, name='forward', out_shape=(sds((4, T, D), BF),...  148 us
    pallas_call x1, Pallas kernels, call_k2(): pl.pallas_call(k2_kernel, name='backward', out_shape=(sds((T, D), BF), sd...  119 us

profile of v5, /device:TPU:30, one launch (start us, length us, event | category | flops | bytes accessed | tf_op | source)
XLA Modules:
  0.0 272.1 jit_solution(18383028209106144959)
XLA Ops:
  0.6 148.5 %forward.1 = (bf16[4,512,768]{2,1,0:T(8,128)(2,1)}, bf16[4,512,192]{2,1,0:T(8,128)(2,1)}, bf16[4,512,192]{2,1,0:T(8,128)(2,1)}, bf16[4,512,192]{2,1,0:T(8,128)(2...) custom-call(bf16[512,768]{1,0:T(8,128)(2,1)} %bitcast.23, ...), custom_call_target="tpu_custom_call" | custom-call | tf_op jit(solution)/shard_map/forward/pallas_call | solution.py:1060
  149.1 118.5 %backward.1 = (bf16[512,768]{1,0:T(8,128)(2,1)}, bf16[512,768]{1,0:T(8,128)(2,1)}, f32[8,512]{1,0:T(8,128)}, f32[24,768]{1,0:T(8,128)}, bf16[4,3,96,192]{3,2,1,0...) custom-call(bf16[4,160,768]{2,1,0:T(8,128)(2,1)} %get-tuple-element., ...), custom_call_target="tpu_custom_call" | custom-call | tf_op jit(solution)/shard_map/backward/pallas_call | solution.py:1548
  267.6 4.4 %finish.1 = (bf16[512,768]{1,0:T(8,128)(2,1)}, bf16[512,768]{1,0:T(8,128)(2,1)}, f32[8,512]{1,0:T(8,128)}, f32[768]{0:T(1024)}, f32[768]{0:T(1024)}, /*index=5*/...) custom-call(bf16[512,768]{1,0:T(8,128)(2,1)} %get-tuple-element.85.l, ...), custom_call_target="tpu_custom_call" | custom-call | tf_op jit(solution)/shard_map/finish/pallas_call | solution.py:1596

commit v6 on v5

--- a/solution.py
+++ b/solution.py
@@ -1399,8 +1399,8 @@
 
     lax.fori_loop(0, 6, near_step, 0)
     rs_far(2)
+    rs_cross(1)
     far_pass(0)
-    rs_cross(1)
 
     go_s[0] = go_acc[0:R, :].astype(BF)
     go_s[1] = go_acc[R : 2 * R, :].astype(BF)
@@ -1458,12 +1458,12 @@
     weight_rows(1)
     rs_side(2)
     weight_sum(0)
+    weight_rows(2)
     for i, p in enumerate(me.exp_peers):
         me.send(sm1.at[p], sm1.at[p], s1_ss.at[i], s1_rs.at[i]).wait()
     sm2[f] = add(sm1[0], sm1[1], sm1[2], sm1[3])
     for r in range(1, 8):
         me.send(sm2.at[f], sm2.at[f], s2_ss.at[r - 1], s2_rs.at[f], f=me.fp(r)).start()
-    weight_rows(2)
 
     @pl.when(z == e)
     def _():

time: 275 us -> 266 us (0.967)
  Pallas kernels: 271 us -> 263 us
    pallas_call x1, Pallas kernels: 119 us -> 111 us  [call_k2(): pl.pallas_call(k2_kernel, name='backward', out_shape=(sds((T, D), BF), sd...]
where the time goes in v6:
time: 266 us; the launch traced here: 264 us
  Pallas kernels  263 us (99%)
    pallas_call x1, Pallas kernels, call_k1(): pl.pallas_call(k1_kernel, name='forward', out_shape=(sds((4, T, D), BF),...  148 us
    pallas_call x1, Pallas kernels, call_k2(): pl.pallas_call(k2_kernel, name='backward', out_shape=(sds((T, D), BF), sd...  111 us

profile of v6, /device:TPU:30, one launch (start us, length us, event | category | flops | bytes accessed | tf_op | source)
XLA Modules:
  0.0 264.1 jit_solution(13046363652317490860)
XLA Ops:
  0.6 148.5 %forward.1 = (bf16[4,512,768]{2,1,0:T(8,128)(2,1)}, bf16[4,512,192]{2,1,0:T(8,128)(2,1)}, bf16[4,512,192]{2,1,0:T(8,128)(2,1)}, bf16[4,512,192]{2,1,0:T(8,128)(2...) custom-call(bf16[512,768]{1,0:T(8,128)(2,1)} %bitcast.23, ...), custom_call_target="tpu_custom_call" | custom-call | tf_op jit(solution)/shard_map/forward/pallas_call | solution.py:1060
  149.1 110.6 %backward.1 = (bf16[512,768]{1,0:T(8,128)(2,1)}, bf16[512,768]{1,0:T(8,128)(2,1)}, f32[8,512]{1,0:T(8,128)}, f32[24,768]{1,0:T(8,128)}, bf16[4,3,96,192]{3,2,1,0...) custom-call(bf16[4,160,768]{2,1,0:T(8,128)(2,1)} %get-tuple-element., ...), custom_call_target="tpu_custom_call" | custom-call | tf_op jit(solution)/shard_map/backward/pallas_call | solution.py:1548
  259.7 4.4 %finish.1 = (bf16[512,768]{1,0:T(8,128)(2,1)}, bf16[512,768]{1,0:T(8,128)(2,1)}, f32[8,512]{1,0:T(8,128)}, f32[768]{0:T(1024)}, f32[768]{0:T(1024)}, /*index=5*/...) custom-call(bf16[512,768]{1,0:T(8,128)(2,1)} %get-tuple-element.85.l, ...), custom_call_target="tpu_custom_call" | custom-call | tf_op jit(solution)/shard_map/finish/pallas_call | solution.py:1596

commit v7 on v6

--- a/solution.py
+++ b/solution.py
@@ -1568,11 +1568,27 @@
 
 
 def k3_kernel(
-    layer_in, tokens_in, res_in, small, ag, go, eg, eu, ed,
-    layer_out, tokens_out, res_out, norm_a, norm_f, g_q, g_k, g_v, g_o, router, mixing, proj, cvec, o_gate, o_up, o_down,
+    layer_in, tokens_in, eg, eu, ed, res_in, small, ag, go,
+    layer_out, tokens_out, o_gate, o_up, o_down, res_out, norm_a, norm_f, g_q, g_k, g_v, g_o, router, mixing, proj, cvec,
+    layer_s, tokens_s, eg_s, eu_s, ed_s, gate_s, up_s, down_s, in_sem, out_sem,
 ):
-    layer_out[...] = layer_in[...]
-    tokens_out[...] = tokens_in[...]
+    loads = ((layer_in, layer_s), (tokens_in, tokens_s), (eg, eg_s), (eu, eu_s), (ed, ed_s))
+    stores = ((layer_s, layer_out), (tokens_s, tokens_out), (gate_s, o_gate), (up_s, o_up), (down_s, o_down))
+
+    def load(i):
+        return pltpu.make_async_copy(loads[i][0], loads[i][1], in_sem.at[i])
+
+    def store(i):
+        return pltpu.make_async_copy(stores[i][0], stores[i][1], out_sem.at[i])
+
+    order = (2, 3, 4, 0, 1)
+    for i in order:
+        load(i).start()
+    for i in order:
+        load(i).wait()
+        if i >= 2:
+            stores[i][0][...] = loads[i][1][...].astype(F32)
+        store(i).start()
     res_out[...] = res_in[...]
     norm_a[...] = small[15, :]
     norm_f[...] = small[14, :]
@@ -1585,25 +1601,30 @@
     mixing[...] = small[16:24, 0:8]
     proj[...] = small[8:12, :]
     cvec[...] = small[12:14, :]
-    o_gate[...] = eg[...].astype(F32)
-    o_up[...] = eu[...].astype(F32)
-    o_down[...] = ed[...].astype(F32)
-
-
-def call_k3(*args):
-    T, D = args[0].shape
+    for i in order:
+        store(i).wait()
+
+
+def call_k3(layer, tokens, res, small, ag, go, eg, eu, ed):
+    T, D = layer.shape
     R = D // 8
-    return pl.pallas_call(
+    dma = pltpu.SemaphoreType.DMA
+    VM = pltpu.VMEM
+    experts = (eg, eu, ed)
+    outs = pl.pallas_call(
         k3_kernel,
         name="finish",
-        out_shape=(
-            sds((T, D), BF), sds((T, D), BF), sds((8, T), F32), sds((D,), F32), sds((D,), F32),
+        out_shape=(sds((T, D), BF), sds((T, D), BF)) + tuple(sds(a.shape, F32) for a in experts) + (
+            sds((8, T), F32), sds((D,), F32), sds((D,), F32),
             sds((R, D), F32), sds((R, D), F32), sds((R, D), F32), sds((R, D), F32),
             sds((8, D), F32), sds((8, 8), F32), sds((4, D), F32), sds((2, D), F32),
-        ) + tuple(sds(a.shape, F32) for a in args[6:9]),
-        in_specs=[vmem()] * 9,
-        out_specs=tuple([vmem()] * 16),
-    )(*args)
+        ),
+        in_specs=[anyspace()] * 5 + [vmem()] * 4,
+        out_specs=tuple([anyspace()] * 5 + [vmem()] * 11),
+        scratch_shapes=[VM((T, D), BF), VM((T, D), BF)] + [VM(a.shape, BF) for a in experts] + [VM(a.shape, F32) for a in experts]
+        + [dma((5,)), dma((5,))],
+    )(layer, tokens, eg, eu, ed, res, small, ag, go)
+    return outs[:2] + outs[5:] + outs[2:5]
 
 
 def body_fast(

time: 266 us -> 267 us (level)
  no operation moved by 1% of the time
where the time goes in v7:
time: 267 us; the launch traced here: 265 us
  Pallas kernels  264 us (99%)
    pallas_call x1, Pallas kernels, call_k1(): pl.pallas_call(k1_kernel, name='forward', out_shape=(sds((4, T, D), BF),...  148 us
    pallas_call x1, Pallas kernels, call_k2(): pl.pallas_call(k2_kernel, name='backward', out_shape=(sds((T, D), BF), sd...  111 us

profile of v7, /device:TPU:30, one launch (start us, length us, event | category | flops | bytes accessed | tf_op | source)
XLA Modules:
  0.0 265.1 jit_solution(1064134291297833850)
XLA Ops:
  0.6 148.5 %forward.1 = (bf16[4,512,768]{2,1,0:T(8,128)(2,1)}, bf16[4,512,192]{2,1,0:T(8,128)(2,1)}, bf16[4,512,192]{2,1,0:T(8,128)(2,1)}, bf16[4,512,192]{2,1,0:T(8,128)(2...) custom-call(bf16[512,768]{1,0:T(8,128)(2,1)} %bitcast.23, ...), custom_call_target="tpu_custom_call" | custom-call | tf_op jit(solution)/shard_map/forward/pallas_call | solution.py:1060
  149.1 110.6 %backward.1 = (bf16[512,768]{1,0:T(8,128)(2,1)}, bf16[512,768]{1,0:T(8,128)(2,1)}, f32[8,512]{1,0:T(8,128)}, f32[24,768]{1,0:T(8,128)}, bf16[4,3,96,192]{3,2,1,0...) custom-call(bf16[4,160,768]{2,1,0:T(8,128)(2,1)} %get-tuple-element., ...), custom_call_target="tpu_custom_call" | custom-call | tf_op jit(solution)/shard_map/backward/pallas_call | solution.py:1548
  259.7 5.2 %finish.1 = (bf16[512,768]{1,0:T(8,128)(2,1)}, bf16[512,768]{1,0:T(8,128)(2,1)}, f32[96,2048]{1,0:T(8,128)}, f32[96,2048]{1,0:T(8,128)}, f32[256,768]{1,0:T(8,12...) custom-call(bf16[512,768]{1,0:T(8,128)(2,1)} %get-tuple-element.85.l, ...), custom_call_target="tpu_custom_call" | custom-call | tf_op jit(solution)/shard_map/finish/pallas_call | solution.py:1614
